TPU v7x, 32 devices: a whole 2x2x4 slice. The times are simulated.
32 devices in a mesh: dp: 8 (over z, x), tensor: 4 (over y, core).
Axes of the slice: x: 2, y: 2, z: 4, core: 2. Of those that a mesh axis runs over, the one named last changes fastest.
Arguments:
- block_input: bfloat16 [20480, 1536], P(('dp', 'tensor')), may hold values from -6 to 6
- seq_lengths: int32 [8, 5], P('dp'), may hold values from 1 to 1024, 2560 in all within a row
- w_qkv: float32 [768, 3, 768], P('dp', None, 'tensor'), may hold values from -0.21875 to 0.21875
- w_out: float32 [768, 768], P('dp', 'tensor'), may hold values from -0.875 to 0.875
- w_gate_up: float32 [768, 2, 3072], P('dp', None, 'tensor'), may hold values from -0.21875 to 0.21875
- w_down: float32 [768, 3072], P('dp', 'tensor'), may hold values from -0.109375 to 0.109375
- gain_attn: float32 [768], replicated, may hold values from 0.5 to 1.5
- gain_ffn: float32 [768], replicated, may hold values from 0.5 to 1.5
- mix_matrix: float32 [2, 2], replicated, may hold values from 0.3 to 1
- correct_gain: float32 [2], replicated, may hold values from 0.5 to 1.5
- cotangent: bfloat16 [20480, 1536], P(('dp', 'tensor')), may hold values from -6 to 6
Outputs:
- block_output: bfloat16 [20480, 1536], P(('dp', 'tensor'))
- grad_input: float32 [20480, 1536], P(('dp', 'tensor'))
- grad_w_qkv: float32 [768, 3, 768], P('dp', None, 'tensor')
- grad_w_out: float32 [768, 768], P('dp', 'tensor')
- grad_w_gate_up: float32 [768, 2, 3072], P('dp', None, 'tensor')
- grad_w_down: float32 [768, 3072], P('dp', 'tensor')
- grad_gain_attn: float32 [768], replicated
- grad_gain_ffn: float32 [768], replicated
- grad_mix_matrix: float32 [2, 2], replicated
- grad_correct_gain: float32 [2], replicated
Inputs may be any that keep to these rules, and one draw needn't show every extreme that they name: Each row of seq_lengths sums to 2560, and its largest entry is 1024.
All inputs are finite; a program needn't handle non-finite values.
Results may differ from a plain program's by a relative error of at most 0.014.
Values may be sent and summed in bfloat16 or wider, within the bound.
A program may use at most 192 MiB of HBM per device.

v0:
```python
import functools
import math

import jax
import jax.numpy as jnp
from jax import lax
from jax.experimental import pallas as pl
from jax.experimental.pallas import tpu as pltpu
from jax.sharding import PartitionSpec as P

HEAD_DIM = 64
EPS = 1e-06
BIG = 1e30
BLK = 256
SUB = 128
MESH = pl.DeviceIdType.MESH


def dot(a, b):
    return jnp.dot(a, b, preferred_element_type=jnp.float32)


def dot_nt(a, b):
    return lax.dot_general(a, b, (((1,), (1,)), ((), ())), preferred_element_type=jnp.float32)


def dot_tn(a, b):
    return lax.dot_general(a, b, (((0,), (0,)), ((), ())), preferred_element_type=jnp.float32)


def turned(a):
    return a.astype(jnp.float32).T


def seg_vector(len_ref, pos):
    begin = jnp.zeros_like(pos)
    edge = jnp.int32(0)
    for k in range(len_ref.shape[1] - 1):
        edge = edge + len_ref[0, k]
        begin = jnp.where(pos >= edge, edge, begin)
    return begin


def seg_scalar(len_ref, row):
    begin = jnp.int32(0)
    end = jnp.int32(0)
    edge = jnp.int32(0)
    for k in range(len_ref.shape[1]):
        after = edge + len_ref[0, k]
        inside = (row >= edge) & (row < after)
        begin = jnp.where(inside, edge, begin)
        end = jnp.where(inside, after, end)
        edge = after
    return begin, end


def place(me, chunk, per):
    return (chunk // per) ^ me, pl.multiple_of((chunk % per) * SUB, SUB)


def fwd_kernel(heads, parts, len_ref, me_ref, *refs):
    proj = refs[:parts]
    o_ref, ot_ref, lse_ref, qt, kh, vt, acc, mx, tot = refs[parts:]
    i = pl.program_id(0)
    part_rows = proj[0].shape[0]
    per = part_rows // SUB
    blk, hd = BLK, HEAD_DIM
    feats = heads * hd
    me = me_ref[0]

    @pl.when(i == 0)
    def _():
        for c in range(parts):
            base = (me ^ c) * part_rows
            def turn(s, carry, c=c, base=base):
                src = pl.ds(pl.multiple_of(s * SUB, SUB), SUB)
                at = pl.ds(pl.multiple_of(base + s * SUB, SUB), SUB)
                rows = proj[c][src, :]
                qt[:, at] = (turned(rows[:, :feats]) * 0.125).astype(jnp.bfloat16)
                vt[:, at] = turned(rows[:, 2 * feats :]).astype(jnp.bfloat16)
                for h in range(heads):
                    kh[h, at, :] = rows[:, feats + h * hd : feats + (h + 1) * hd]
                return carry
            lax.fori_loop(0, per, turn, 0)

    first = pl.multiple_of(i * blk, blk)
    cols = pl.ds(first, blk)
    pos = first + lax.broadcasted_iota(jnp.int32, (1, blk), 1)
    begin = seg_vector(len_ref, pos)
    b_first, _ = seg_scalar(len_ref, first)
    b_last, _ = seg_scalar(len_ref, first + blk - 1)
    j_lo = b_first // blk
    j_full = jnp.minimum((b_last + blk - 1) // blk, i)
    mx[...] = jnp.full_like(mx, -BIG)
    tot[...] = jnp.zeros_like(tot)
    acc[...] = jnp.zeros_like(acc)

    def step(j, masked, first_pass):
        at = pl.ds(pl.multiple_of(j * blk, blk), blk)
        if masked:
            key = j * blk + lax.broadcasted_iota(jnp.int32, (blk, blk), 0)
            ok = (key >= begin) & (key <= pos)
        scores = []
        for h in range(heads):
            s = dot(kh[h, at, :], qt[h * hd : (h + 1) * hd, cols])
            scores.append(jnp.where(ok, s, -BIG) if masked else s)
        if first_pass:
            for h in range(heads):
                old = mx[h : h + 1]
                new = jnp.maximum(old, jnp.max(scores[h], axis=0, keepdims=True))
                total = jnp.sum(jnp.exp(scores[h] - new), axis=0, keepdims=True)
                mx[h : h + 1] = new
                tot[h : h + 1] = jnp.exp(old - new) * tot[h : h + 1] + total
        else:
            for h in range(heads):
                hs = slice(h * hd, (h + 1) * hd)
                p = jnp.exp(scores[h] - mx[h : h + 1])
                acc[hs] += dot(vt[hs, at], p.astype(jnp.bfloat16))

    def loop(lo, hi, masked, first_pass):
        def body(j, carry):
            step(j, masked, first_pass)
            return carry
        lax.fori_loop(lo, hi, body, 0)

    for first_pass in (True, False):
        loop(j_lo, j_full, True, first_pass)
        loop(jnp.maximum(j_full, j_lo), i, False, first_pass)
        step(i, True, first_pass)
        if first_pass:
            mx[...] = mx[...] + jnp.log(tot[...])
            lse_ref[...] = mx[...]
    ot_ref[...] = acc[...]
    out = acc[...].T.astype(jnp.bfloat16)
    for s in range(blk // SUB):
        c, row = place(me, i * (blk // SUB) + s, per)
        o_ref[c, pl.ds(row, SUB), :] = out[s * SUB : (s + 1) * SUB]


def attn_fwd(lengths, me, proj):
    parts = len(proj)
    part_rows, width = proj[0].shape
    feats = width // 3
    rows = parts * part_rows
    heads = feats // HEAD_DIM
    return pl.pallas_call(
        functools.partial(fwd_kernel, heads, parts),
        out_shape=(
            jax.ShapeDtypeStruct((parts, part_rows, feats), jnp.bfloat16),
            jax.ShapeDtypeStruct((feats, rows), jnp.float32),
            jax.ShapeDtypeStruct((8, rows), jnp.float32),
        ),
        grid_spec=pltpu.PrefetchScalarGridSpec(
            num_scalar_prefetch=2,
            grid=(rows // BLK,),
            in_specs=[pl.BlockSpec((part_rows, width), lambda i, s, m: (0, 0))] * parts,
            out_specs=(
                pl.BlockSpec((parts, part_rows, feats), lambda i, s, m: (0, 0, 0)),
                pl.BlockSpec((feats, BLK), lambda i, s, m: (0, i)),
                pl.BlockSpec((8, BLK), lambda i, s, m: (0, i)),
            ),
            scratch_shapes=[
                pltpu.VMEM((feats, rows), jnp.bfloat16),
                pltpu.VMEM((heads, rows, HEAD_DIM), jnp.bfloat16),
                pltpu.VMEM((feats, rows), jnp.bfloat16),
                pltpu.VMEM((feats, BLK), jnp.float32),
                pltpu.VMEM((8, BLK), jnp.float32),
                pltpu.VMEM((8, BLK), jnp.float32),
            ],
        ),
        cost_estimate=pl.CostEstimate(
            flops=rows * feats * 4096, bytes_accessed=12 * rows * feats, transcendentals=rows * 512 * heads
        ),
        name="attn_fwd",
    )(lengths, me, *proj)


def bwd_kernel(heads, parts, len_ref, me_ref, *refs):
    proj = refs[:parts]
    grads = refs[parts : 2 * parts]
    ot_ref, lse_ref, d_ref, qt, qp, gt, gp, kh, vh, kt, dqt, delta, dkv = refs[2 * parts :]
    j = pl.program_id(0)
    n = pl.num_programs(0)
    part_rows = proj[0].shape[0]
    per = part_rows // SUB
    blk, hd = BLK, HEAD_DIM
    feats = heads * hd
    me = me_ref[0]

    @pl.when(j == 0)
    def _():
        zero = jnp.zeros((SUB, hd), jnp.bfloat16)
        for c in range(parts):
            base = (me ^ c) * part_rows
            def turn(s, carry, c=c, base=base):
                src = pl.ds(pl.multiple_of(s * SUB, SUB), SUB)
                at = pl.ds(pl.multiple_of(base + s * SUB, SUB), SUB)
                rows = proj[c][src, :]
                g = grads[c][src, :]
                g_turned = turned(g)
                qt[:, at] = (turned(rows[:, :feats]) * 0.125).astype(jnp.bfloat16)
                kt[:, at] = turned(rows[:, feats : 2 * feats]).astype(jnp.bfloat16)
                gt[:, at] = g_turned.astype(jnp.bfloat16)
                prod = g_turned * ot_ref[:, at]
                dqt[:, at] = jnp.zeros((feats, SUB), jnp.float32)
                for h in range(heads):
                    hs = slice(h * hd, (h + 1) * hd)
                    delta[h : h + 1, at] = jnp.sum(prod[hs], axis=0, keepdims=True)
                    qp[h, at, :] = jnp.concatenate([rows[:, hs], zero], axis=1)
                    gp[h, at, :] = jnp.concatenate([zero, g[:, hs]], axis=1)
                    kh[h, at, :] = rows[:, feats + h * hd : feats + (h + 1) * hd]
                    vh[h, at, :] = rows[:, 2 * feats + h * hd : 2 * feats + (h + 1) * hd]
                return carry
            lax.fori_loop(0, per, turn, 0)

    first = pl.multiple_of(j * blk, blk)
    keys = pl.ds(first, blk)
    _, e_first = seg_scalar(len_ref, first)
    _, e_last = seg_scalar(len_ref, first + blk - 1)
    i_hi = (e_last - 1) // blk + 1
    i_full = jnp.clip(e_first // blk, j + 1, i_hi)
    key = first + lax.broadcasted_iota(jnp.int32, (blk, blk), 0)

    def step(i, masked, start):
        at = pl.ds(pl.multiple_of(i * blk, blk), blk)
        if masked:
            pos = i * blk + lax.broadcasted_iota(jnp.int32, (1, blk), 1)
            begin = seg_vector(len_ref, pos)
            ok = (key >= begin) & (key <= pos)
        scores, dprobs = [], []
        for h in range(heads):
            hs = slice(h * hd, (h + 1) * hd)
            scores.append(dot(kh[h, keys, :], qt[hs, at]))
            dprobs.append(dot(vh[h, keys, :], gt[hs, at]))
        both = []
        for h in range(heads):
            e = scores[h] - lse_ref[h : h + 1, at]
            if masked:
                e = jnp.where(ok, e, -BIG)
            p = jnp.exp(e)
            ds = p * (dprobs[h] - delta[h : h + 1, at])
            both.append((p.astype(jnp.bfloat16), ds.astype(jnp.bfloat16)))
        for h in range(heads):
            hs = slice(h * hd, (h + 1) * hd)
            p, ds = both[h]
            add = dot(
                jnp.concatenate([ds, p], axis=1),
                jnp.concatenate([qp[h, at, :], gp[h, at, :]], axis=0),
            )
            if start:
                dkv[h] = add
            else:
                dkv[h] += add
            dqt[hs, at] += dot(kt[hs, keys], ds)

    def loop(lo, hi, masked):
        def body(i, carry):
            step(i, masked, False)
            return carry
        lax.fori_loop(lo, hi, body, 0)

    step(j, True, True)
    loop(j + 1, i_full, False)
    loop(i_full, i_hi, True)
    pair = jnp.concatenate(
        [dkv[h][:, :hd] * 0.125 for h in range(heads)] + [dkv[h][:, hd:] for h in range(heads)], axis=1
    ).astype(jnp.bfloat16)
    for s in range(blk // SUB):
        c, row = place(me, j * (blk // SUB) + s, per)
        d_ref[c, pl.ds(row, SUB), feats:] = pair[s * SUB : (s + 1) * SUB]

    @pl.when(j == n - 1)
    def _():
        for c in range(parts):
            base = (me ^ c) * part_rows
            def turn(s, carry, c=c, base=base):
                at = pl.ds(pl.multiple_of(base + s * SUB, SUB), SUB)
                dst = pl.ds(pl.multiple_of(s * SUB, SUB), SUB)
                d_ref[c, dst, :feats] = (dqt[:, at] * 0.125).T.astype(jnp.bfloat16)
                return carry
            lax.fori_loop(0, per, turn, 0)


def attn_bwd(lengths, me, proj, grads, heads_turned, log_total):
    parts = len(proj)
    part_rows, width = proj[0].shape
    feats = width // 3
    rows = parts * part_rows
    heads = feats // HEAD_DIM
    return pl.pallas_call(
        functools.partial(bwd_kernel, heads, parts),
        out_shape=jax.ShapeDtypeStruct((parts, part_rows, width), jnp.bfloat16),
        grid_spec=pltpu.PrefetchScalarGridSpec(
            num_scalar_prefetch=2,
            grid=(rows // BLK,),
            in_specs=[pl.BlockSpec((part_rows, width), lambda i, s, m: (0, 0))] * parts
            + [pl.BlockSpec((part_rows, feats), lambda i, s, m: (0, 0))] * parts
            + [
                pl.BlockSpec((feats, rows), lambda i, s, m: (0, 0)),
                pl.BlockSpec((8, rows), lambda i, s, m: (0, 0)),
            ],
            out_specs=pl.BlockSpec((parts, part_rows, width), lambda i, s, m: (0, 0, 0)),
            scratch_shapes=[
                pltpu.VMEM((feats, rows), jnp.bfloat16),
                pltpu.VMEM((heads, rows, 2 * HEAD_DIM), jnp.bfloat16),
                pltpu.VMEM((feats, rows), jnp.bfloat16),
                pltpu.VMEM((heads, rows, 2 * HEAD_DIM), jnp.bfloat16),
                pltpu.VMEM((heads, rows, HEAD_DIM), jnp.bfloat16),
                pltpu.VMEM((heads, rows, HEAD_DIM), jnp.bfloat16),
                pltpu.VMEM((feats, rows), jnp.bfloat16),
                pltpu.VMEM((feats, rows), jnp.float32),
                pltpu.VMEM((8, rows), jnp.float32),
                pltpu.VMEM((heads, BLK, 2 * HEAD_DIM), jnp.float32),
            ],
        ),
        cost_estimate=pl.CostEstimate(
            flops=rows * feats * 10240, bytes_accessed=20 * rows * feats, transcendentals=rows * 512 * heads
        ),
        name="attn_bwd",
    )(lengths, me, *proj, *grads, heads_turned, log_total)


def gelu_parts(v):
    c = math.sqrt(2 / math.pi)
    square = v * v
    t = jnp.tanh(c * v * (1.0 + 0.044715 * square))
    half = 0.5 * (1.0 + t)
    slope = half + (0.5 * v) * (1.0 - t * t) * (c * (1.0 + 3 * 0.044715 * square))
    return v * half, slope


def ffn_kernel(tile, x_ref, g_ref, wg_ref, wu_ref, wd_ref, h_ref, dg_ref, du_ref, branch_ref, dx_ref, branch, dx):
    u = pl.program_id(0)
    x = x_ref[...]
    gate = dot(x, wg_ref[...])
    up = dot(x, wu_ref[...])
    grad_hidden = dot(g_ref[...], wd_ref[...])
    act, slope = gelu_parts(gate)
    hidden = (act * up).astype(jnp.bfloat16)
    dgate = (slope * (grad_hidden * up)).astype(jnp.bfloat16)
    dup = (grad_hidden * act).astype(jnp.bfloat16)
    h_ref[...] = hidden
    dg_ref[...] = dgate
    du_ref[...] = dup
    b_add = dot_nt(hidden, wd_ref[...])
    d_add = dot_nt(dgate, wg_ref[...]) + dot_nt(dup, wu_ref[...])

    @pl.when(u == 0)
    def _():
        branch[...] = b_add
        dx[...] = d_add

    @pl.when(u > 0)
    def _():
        branch[...] += b_add
        dx[...] += d_add

    @pl.when(u == pl.num_programs(0) - 1)
    def _():
        branch_ref[...] = branch[...]
        dx_ref[...] = dx[...].astype(jnp.bfloat16)


def ffn_rows(x, g, weights, tile=256):
    rows, d = x.shape
    units = weights.shape[1] // 3
    n = units // tile
    full = pl.BlockSpec((rows, d), lambda u: (0, 0))
    cols = pl.BlockSpec((rows, tile), lambda u: (0, u))
    wide = jax.ShapeDtypeStruct((rows, units), jnp.bfloat16)
    narrow = jax.ShapeDtypeStruct((rows, d), jnp.bfloat16)
    return pl.pallas_call(
        functools.partial(ffn_kernel, tile),
        out_shape=(wide, wide, wide, jax.ShapeDtypeStruct((rows, d), jnp.float32), narrow),
        grid=(n,),
        in_specs=[
            full,
            full,
            pl.BlockSpec((d, tile), lambda u: (0, u)),
            pl.BlockSpec((d, tile), lambda u: (0, u + n)),
            pl.BlockSpec((d, tile), lambda u: (0, u + 2 * n)),
        ],
        out_specs=(cols, cols, cols, full, full),
        scratch_shapes=[pltpu.VMEM((rows, d), jnp.float32), pltpu.VMEM((rows, d), jnp.float32)],
        cost_estimate=pl.CostEstimate(
            flops=12 * rows * d * units,
            bytes_accessed=2 * (4 * rows * d + 3 * rows * units + 3 * d * units),
            transcendentals=rows * units,
        ),
        name="ffn_rows",
    )(x, g, weights, weights, weights)


def wgrad_kernel(parts, n, *refs):
    xs, gs, gates, ups, hiddens = [refs[parts * m : parts * (m + 1)] for m in range(5)]
    out, left_t = refs[-2:]
    i = pl.program_id(0)
    rows = xs[0].shape[0]

    def turn_all(lefts):
        for c in range(parts):
            def turn(s, carry, c=c):
                src = pl.ds(pl.multiple_of(s * SUB, SUB), SUB)
                at = pl.ds(pl.multiple_of(c * rows + s * SUB, SUB), SUB)
                left_t[:, at] = turned(lefts[c][src, :]).astype(jnp.bfloat16)
                return carry
            lax.fori_loop(0, rows // SUB, turn, 0)

    def product(rights):
        total = dot(left_t[:, :rows], rights[0][...])
        for c in range(1, parts):
            total += dot(left_t[:, c * rows : (c + 1) * rows], rights[c][...])
        out[...] = total.astype(jnp.bfloat16)

    @pl.when(i == 0)
    def _():
        turn_all(xs)

    @pl.when(i == 2 * n)
    def _():
        turn_all(gs)

    @pl.when(i < n)
    def _():
        product(gates)

    @pl.when((i >= n) & (i < 2 * n))
    def _():
        product(ups)

    @pl.when(i >= 2 * n)
    def _():
        product(hiddens)


def wgrad(xs, gs, gates, ups, hiddens, tile=256):
    parts = len(xs)
    rows, d = xs[0].shape
    units = gates[0].shape[1]
    n = units // tile

    def tiles(m):
        return [pl.BlockSpec((rows, tile), lambda i: (0, jnp.clip(i - m * n, 0, n - 1)))] * parts

    return pl.pallas_call(
        functools.partial(wgrad_kernel, parts, n),
        out_shape=jax.ShapeDtypeStruct((d, 3 * units), jnp.bfloat16),
        grid=(3 * n,),
        in_specs=[pl.BlockSpec((rows, d), lambda i: (0, 0))] * (2 * parts) + tiles(0) + tiles(1) + tiles(2),
        out_specs=pl.BlockSpec((d, tile), lambda i: (0, i)),
        scratch_shapes=[pltpu.VMEM((d, parts * rows), jnp.bfloat16)],
        cost_estimate=pl.CostEstimate(
            flops=6 * parts * rows * d * units,
            bytes_accessed=2 * parts * rows * (2 * d + 3 * units) + 6 * d * units,
            transcendentals=0,
        ),
        name="wgrad",
    )(*xs, *gs, *gates, *ups, *hiddens)


def rms_norm(features, norm_gain):
    return features * lax.rsqrt(jnp.mean(features * features, axis=-1, keepdims=True) + EPS) * norm_gain


def norm_back(v, gain, e):
    rate = lax.rsqrt(jnp.mean(v * v, axis=-1, keepdims=True) + EPS)
    scaled = gain * e
    dot_mean = jnp.mean(scaled * v, axis=-1, keepdims=True)
    return rate * scaled - v * (rate * rate * rate * dot_mean), jnp.sum(e * v * rate, axis=0, keepdims=True)


def middle_kernel(parts, share, came, got, middle, top, gain, *refs):
    weights = refs[:parts]
    grad_ref, low_ref = refs[parts : parts + 2]
    heads = refs[parts + 2 : 2 * parts + 2]
    gain_ref = refs[-1]
    f32 = jnp.float32
    e = share[...].astype(f32) + came[...].astype(f32) + got[...].astype(f32)
    grad, part = norm_back(middle[...], gain[...], e)
    grad = top[...] + grad
    grad_ref[...] = grad
    low = grad.astype(jnp.bfloat16)
    low_ref[...] = low
    for c in range(parts):
        heads[c][...] = dot(low, weights[c][...]).astype(jnp.bfloat16)

    @pl.when(pl.program_id(0) == 0)
    def _():
        gain_ref[...] = part

    @pl.when(pl.program_id(0) > 0)
    def _():
        gain_ref[...] += part


def middle_back(share, came, got, middle, top, gain, weights, block=160):
    rows, d = middle.shape
    feats = weights[0].shape[1]
    parts = len(weights)
    row = pl.BlockSpec((block, d), lambda i: (i, 0))
    one = pl.BlockSpec((1, d), lambda i: (0, 0))
    outs = pl.pallas_call(
        functools.partial(middle_kernel, parts),
        out_shape=(
            jax.ShapeDtypeStruct((rows, d), jnp.float32),
            jax.ShapeDtypeStruct((rows, d), jnp.bfloat16),
            *[jax.ShapeDtypeStruct((rows, feats), jnp.bfloat16)] * parts,
            jax.ShapeDtypeStruct((1, d), jnp.float32),
        ),
        grid=(rows // block,),
        in_specs=[row] * 5 + [one] + [pl.BlockSpec((d, feats), lambda i: (0, 0))] * parts,
        out_specs=(row, row, *[pl.BlockSpec((block, feats), lambda i: (i, 0))] * parts, one),
        cost_estimate=pl.CostEstimate(
            flops=2 * rows * d * feats * parts, bytes_accessed=22 * rows * d, transcendentals=rows
        ),
        name="middle_back",
    )(share, came, got, middle, top, gain[None], *weights)
    return outs[0], outs[1], list(outs[2 : 2 + parts]), outs[-1]


def input_kernel(share, came, got_a, got_b, inputs, cot, grad_middle, early, gain, mix, correct, out, sums):
    i = pl.program_id(0)
    f32 = jnp.float32
    d = gain.shape[1]
    got = jnp.where(i < pl.num_programs(0) // 2, got_a[...].astype(f32), got_b[...].astype(f32))
    e = share[...].astype(f32) + came[...].astype(f32) + got
    one, two = inputs[:, :d].astype(f32), inputs[:, d:].astype(f32)
    cot_one, cot_two = cot[:, :d].astype(f32), cot[:, d:].astype(f32)
    grad, part = norm_back(mix[0, 0] * one + mix[0, 1] * two, gain[...], e)
    main = cot_one + grad_middle[...] + grad - (correct[0] * cot_one + correct[1] * cot_two)
    out[:, :d] = mix[0, 0] * main + mix[1, 0] * cot_two
    out[:, d:] = mix[0, 1] * main + mix[1, 1] * cot_two

    @pl.when(i == 0)
    def _():
        sums[...] = early[...]

    sums[0:1] += part
    for r, value in enumerate((main * one, main * two, cot_two * one, cot_two * two)):
        sums[r + 1 : r + 2] += jnp.sum(value, axis=0, keepdims=True)


def input_back(share, came, got, inputs, cot, grad_middle, early, gain, mix, correct, block=160):
    rows, d = grad_middle.shape
    half = rows // block // 2
    row = pl.BlockSpec((block, d), lambda i: (i, 0))
    wide = pl.BlockSpec((block, 2 * d), lambda i: (i, 0))
    sums = pl.BlockSpec((8, d), lambda i: (0, 0))
    small = pl.BlockSpec(memory_space=pltpu.SMEM)
    return pl.pallas_call(
        input_kernel,
        out_shape=(jax.ShapeDtypeStruct((rows, 2 * d), jnp.float32), jax.ShapeDtypeStruct((8, d), jnp.float32)),
        grid=(2 * half,),
        in_specs=[
            row,
            row,
            pl.BlockSpec((block, d), lambda i: (jnp.minimum(i, half - 1), 0)),
            pl.BlockSpec((block, d), lambda i: (jnp.maximum(i - half, 0), 0)),
            wide,
            wide,
            row,
            sums,
            pl.BlockSpec((1, d), lambda i: (0, 0)),
            small,
            small,
        ],
        out_specs=(wide, sums),
        cost_estimate=pl.CostEstimate(flops=60 * rows * d, bytes_accessed=30 * rows * d, transcendentals=rows),
        name="input_back",
    )(share, came, *got, inputs, cot, grad_middle, early, gain[None], mix, correct)


def swap(array, bit):
    count = lax.axis_size("tensor")
    return lax.ppermute(array, "tensor", [(i, i ^ bit) for i in range(count)])


def after(value, *others):
    return lax.optimization_barrier((value, *others))[0]


def flipped(index, bits):
    bit = 1
    while bit <= bits:
        if bits & bit:
            index = index + bit - 2 * bit * lax.rem(lax.div(index, bit), 2)
        bit *= 2
    return index


def start_kernel(
    count, chunks, x, qkv, wo, sib, far, diag, qkv_all, wo_all,
    local_sem, sib_sem, far_send, far_recv, diag_send, diag_recv, qkv_dp, wo_dp,
):
    t = lax.axis_index("tensor")
    g = lax.axis_index("dp")
    order = []
    bit = 2
    while bit < count:
        order.append(bit)
        bit *= 2
    order.append(1)

    def last(e):
        return max(k for k, b in enumerate(order) if e & b)

    barrier = pltpu.get_barrier_semaphore()
    for c in (1, 2):
        pl.semaphore_signal(barrier, inc=1, device_id={"tensor": flipped(t, c)}, device_id_type=MESH)
    for b in order:
        pl.semaphore_signal(barrier, inc=1, device_id={"dp": flipped(g, b)}, device_id_type=MESH)
    pl.semaphore_wait(barrier, 2 + len(order))

    size = x.shape[0] // chunks

    def far_copy(k):
        rows = pl.ds(k * size, size)
        return pltpu.make_async_remote_copy(
            x.at[rows], far.at[rows], far_send.at[k], far_recv.at[k], {"tensor": flipped(t, 2)}, MESH
        )

    def diag_copy(k):
        rows = pl.ds(k * size, size)
        return pltpu.make_async_remote_copy(
            far.at[rows], diag.at[rows], diag_send.at[k], diag_recv.at[k], {"tensor": flipped(t, 1)}, MESH
        )

    def dp_copy(which, e):
        own, whole, sems = ((qkv, qkv_all, qkv_dp), (wo, wo_all, wo_dp))[which]
        b = order[last(e)]
        block = flipped(g, e ^ b)
        return pltpu.make_async_remote_copy(
            own if e == b else whole.at[block],
            whole.at[block],
            sems.at[0, e - 1],
            sems.at[1, e - 1],
            {"dp": flipped(g, b)},
            MESH,
        )

    def dp_arrival(which, e):
        whole, sems = ((qkv_all, qkv_dp), (wo_all, wo_dp))[which]
        dst = whole.at[flipped(g, e)]
        return pltpu.make_async_remote_copy(
            dst, dst, sems.at[0, e - 1], sems.at[1, e - 1], {"dp": flipped(g, order[last(e)])}, MESH
        )

    sends = []

    def go(copy):
        copy.start()
        sends.append(copy)

    for b in order:
        go(dp_copy(0, b))
    fars = [far_copy(k) for k in range(chunks)]
    for copy in fars:
        go(copy)
    near = pltpu.make_async_remote_copy(
        x, sib, sib_sem.at[0], sib_sem.at[1], {"tensor": flipped(t, 1)}, MESH
    )
    go(near)
    kept = [
        pltpu.make_async_copy(qkv, qkv_all.at[g], local_sem.at[0]),
        pltpu.make_async_copy(wo, wo_all.at[g], local_sem.at[1]),
    ]
    for copy in kept:
        copy.start()
    for b in order:
        go(dp_copy(1, b))
    diags = []

    def pass_on(k):
        fars[k].wait_recv()
        diags.append(diag_copy(k))
        go(diags[-1])

    done = 0
    for e in sorted(range(1, count), key=lambda e: (last(e), e)):
        for which in (0, 1):
            dp_arrival(which, e).wait_recv()
            for b in order[last(e) + 1 :]:
                go(dp_copy(which, e ^ b))
        if done < chunks and e & 1 == 0:
            pass_on(done)
            done += 1
    while done < chunks:
        pass_on(done)
        done += 1
    for copy in diags:
        copy.wait_recv()
    near.wait_recv()
    for copy in sends:
        copy.wait_send()
    for copy in kept:
        copy.wait()


def start(x, qkv, wo, chunks=4):
    count = lax.axis_size("dp")
    rows = jax.ShapeDtypeStruct(x.shape, x.dtype)
    dma = pltpu.SemaphoreType.DMA
    sib, far, diag, qkv_all, wo_all = pl.pallas_call(
        functools.partial(start_kernel, count, chunks),
        out_shape=(
            rows,
            rows,
            rows,
            jax.ShapeDtypeStruct((count, *qkv.shape), qkv.dtype),
            jax.ShapeDtypeStruct((count, *wo.shape), wo.dtype),
        ),
        in_specs=[pl.BlockSpec(memory_space=pl.ANY)] * 3,
        out_specs=(pl.BlockSpec(memory_space=pl.ANY),) * 5,
        scratch_shapes=[
            dma((2,)),
            dma((2,)),
            dma((chunks,)),
            dma((chunks,)),
            dma((chunks,)),
            dma((chunks,)),
            dma((2, count - 1)),
            dma((2, count - 1)),
        ],
        compiler_params=pltpu.CompilerParams(collective_id=0, has_side_effects=True),
        cost_estimate=pl.CostEstimate(flops=0, bytes_accessed=100_000_000, transcendentals=0),
        name="start",
    )(x, qkv, wo)
    whole = count * qkv.shape[0]
    return [x, sib, far, diag], qkv_all.reshape(whole, -1), wo_all.reshape(whole, -1)


def spread(rows):
    far = swap(rows, 2)
    return [rows, swap(rows, 1), far, swap(far, 1)]


def exchange(blocks):
    return [blocks[0]] + [swap(blocks[c], c) for c in range(1, len(blocks))]


def summed(shares, before=None, beside=None):
    f32 = jnp.float32
    far = (shares[2].astype(f32) + swap(shares[3], 1).astype(f32)).astype(jnp.bfloat16)
    if before is not None:
        far = after(far, before)
    got = swap(far, 2)
    near = shares[0].astype(f32) + swap(shares[1], 1).astype(f32)
    if beside is not None:
        got, beside = lax.optimization_barrier((got, beside(far)))
    return near + got.astype(f32), beside


def end_kernel(count, blocks, mine, out, total, own, inbox, near, mid, far, own_sem, in_sem, near_sem, far_sem):
    t = lax.axis_index("tensor")
    g = lax.axis_index("dp")
    f32 = jnp.float32
    barrier = pltpu.get_barrier_semaphore()
    for c in (1, 2, 3):
        pl.semaphore_signal(barrier, inc=1, device_id={"tensor": flipped(t, c)}, device_id_type=MESH)
    for e in range(1, count):
        pl.semaphore_signal(barrier, inc=1, device_id={"dp": flipped(g, e)}, device_id_type=MESH)
    pl.semaphore_wait(barrier, 2 + count)

    nears = [
        pltpu.make_async_remote_copy(
            mine, near.at[c - 1], near_sem.at[0, c - 1], near_sem.at[1, c - 1], {"tensor": flipped(t, c)}, MESH
        )
        for c in (1, 2, 3)
    ]
    ins = [
        pltpu.make_async_remote_copy(
            blocks.at[flipped(g, e)],
            inbox.at[e - 1],
            in_sem.at[0, e - 1],
            in_sem.at[1, e - 1],
            {"dp": flipped(g, e)},
            MESH,
        )
        for e in range(1, count)
    ]
    fars = [
        pltpu.make_async_remote_copy(
            mid, far.at[e - 1], far_sem.at[0, e - 1], far_sem.at[1, e - 1], {"dp": flipped(g, e)}, MESH
        )
        for e in range(1, count)
    ]
    kept = pltpu.make_async_copy(blocks.at[g], own, own_sem.at[0])
    for copy in nears:
        copy.start()
    for copy in nears:
        copy.wait_recv()
    mid[...] = (mine[...] + near[0]) + (near[1] + near[2])
    for copy in fars:
        copy.start()
    for copy in ins:
        copy.start()
    kept.start()
    for copy in fars:
        copy.wait_recv()
    level = [mid[...]] + [far[e] for e in range(count - 1)]
    while len(level) > 1:
        level = [level[k] + level[k + 1] for k in range(0, len(level), 2)]
    total[...] = level[0]
    kept.wait()
    out[...] = own[...].astype(f32)
    for e, copy in enumerate(ins):
        copy.wait_recv()
        out[...] += inbox[e].astype(f32)
    for copy in nears + fars + ins:
        copy.wait_send()


def end(blocks, mine):
    count, rows, cols = blocks.shape
    dma = pltpu.SemaphoreType.DMA
    vmem = pl.BlockSpec(memory_space=pltpu.VMEM)
    return pl.pallas_call(
        functools.partial(end_kernel, count),
        out_shape=(
            jax.ShapeDtypeStruct((rows, cols), jnp.float32),
            jax.ShapeDtypeStruct(mine.shape, jnp.float32),
        ),
        in_specs=[pl.BlockSpec(memory_space=pl.ANY), vmem],
        out_specs=(vmem, vmem),
        scratch_shapes=[
            pltpu.VMEM((rows, cols), blocks.dtype),
            pltpu.VMEM((count - 1, rows, cols), blocks.dtype),
            pltpu.VMEM((3, *mine.shape), jnp.float32),
            pltpu.VMEM(mine.shape, jnp.float32),
            pltpu.VMEM((count - 1, *mine.shape), jnp.float32),
            dma((1,)),
            dma((2, count - 1)),
            dma((2, 3)),
            dma((2, count - 1)),
        ],
        compiler_params=pltpu.CompilerParams(collective_id=1, has_side_effects=True),
        cost_estimate=pl.CostEstimate(flops=0, bytes_accessed=50_000_000, transcendentals=0),
        name="end",
    )(blocks, mine)


def local(
    block_input, seq_lengths, w_qkv, w_out, w_gate_up, w_down, gain_attn, gain_ffn, mix_matrix, correct_gain, cotangent
):
    f32, bf16 = jnp.float32, jnp.bfloat16
    width = gain_attn.shape[0]
    me = lax.axis_index("tensor").astype(jnp.int32)[None]
    shard = w_qkv.shape[0]
    feats = w_out.shape[1]
    inputs = block_input.astype(f32)
    stream_one = inputs[:, :width]
    stream_two = inputs[:, width:]
    predicted_main = mix_matrix[0, 0] * stream_one + mix_matrix[0, 1] * stream_two
    predicted_side = mix_matrix[1, 0] * stream_one + mix_matrix[1, 1] * stream_two
    units = w_down.shape[1]

    normed_attn, qkv_all, out_mine = start(
        rms_norm(predicted_main, gain_attn).astype(bf16),
        w_qkv.reshape(shard, 3 * feats).astype(bf16),
        w_out.astype(bf16),
    )
    ffn_mine = jnp.concatenate([w_gate_up.reshape(shard, -1), w_down], axis=1).astype(bf16)
    ffn_all = lax.all_gather(after(ffn_mine, normed_attn[1]), "dp", axis=0, tiled=True)
    proj = [dot(x, qkv_all).astype(bf16) for x in normed_attn]
    attended, heads_turned, log_total = attn_fwd(seq_lengths, me, proj)

    incoming = cotangent.astype(f32)
    cot_one = incoming[:, :width]
    cot_two = incoming[:, width:]
    grad_top = correct_gain[0] * cot_one + correct_gain[1] * cot_two
    grad_ffn = spread(after(grad_top.astype(bf16), normed_attn[1]))

    out_parts = [out_mine] + [swap(out_mine, c) for c in (1, 2, 3)]
    attended = after(attended, grad_ffn[2], out_parts[2], out_parts[3])
    head_parts = exchange([attended[c] for c in range(len(proj))])
    attn_branch = sum(dot_nt(a, w) for a, w in zip(head_parts, out_parts))
    middle = predicted_main + attn_branch

    normed_mine = rms_norm(middle, gain_ffn).astype(bf16)
    normed_ffn = [normed_mine, swap(normed_mine, 1), swap(normed_mine, 2)]
    pieces = [ffn_rows(x, g, ffn_all) for x, g in zip(normed_ffn, grad_ffn[:2])]
    normed_ffn[2] = after(normed_ffn[2], pieces[0][0], pieces[1][0])
    normed_ffn.append(swap(normed_ffn[2], 1))
    pieces += [ffn_rows(x, g, ffn_all) for x, g in zip(normed_ffn[2:], grad_ffn[2:])]
    hidden, dgate, dup, branch, dnormed = zip(*pieces)
    far = (dnormed[2].astype(f32) + swap(dnormed[3], 1).astype(f32)).astype(bf16)
    got = swap(far, 2)
    came = swap(dnormed[1], 1)
    weight_ffn = wgrad([after(normed_ffn[0], far)] + normed_ffn[1:], grad_ffn, dgate, dup, hidden)
    got, came, weight_ffn = lax.optimization_barrier((got, came, weight_ffn))
    weight_ffn = lax.psum_scatter(weight_ffn, "dp", scatter_dimension=0, tiled=True)
    grad_middle, grad_attn, grad_heads, grad_gain_ffn = middle_back(
        dnormed[0], came, got, middle, grad_top, gain_ffn, out_parts
    )
    grad_heads = exchange(grad_heads)
    grad_proj = attn_bwd(seq_lengths, me, proj, grad_heads, heads_turned, log_total)
    *late, later_attn = lax.optimization_barrier((*head_parts, grad_heads[2], grad_heads[3], grad_attn))
    out_shares = exchange([dot_tn(later_attn, a).astype(bf16) for a in late[:4]])
    weight_out = sum(s.astype(f32) for s in out_shares)
    ffn_branch, (grad_proj, weight_out) = summed(branch, before=late[4], beside=lambda far: (grad_proj, weight_out))
    grad_proj = [grad_proj[c] for c in range(len(proj))]

    correction = (middle + ffn_branch) - predicted_main
    block_output = jnp.concatenate(
        [predicted_main + correct_gain[0] * correction, predicted_side + correct_gain[1] * correction], axis=1
    ).astype(bf16)
    early = jnp.concatenate(
        [
            jnp.zeros((5, width), f32),
            grad_gain_ffn,
            jnp.sum(cot_one * correction, axis=0, keepdims=True),
            jnp.sum(cot_two * correction, axis=0, keepdims=True),
        ],
        axis=0,
    )

    far = [dot_nt(g, qkv_all).astype(bf16) for g in grad_proj[2:]]
    far = (far[0].astype(f32) + swap(far[1], 1).astype(f32)).astype(bf16)
    half = far.shape[0] // 2
    got = [swap(far[:half], 2), swap(far[half:], 2)]
    *late, far = lax.optimization_barrier((*grad_proj, *normed_attn, weight_out, far))
    near = [dot_nt(g, qkv_all).astype(bf16) for g in late[:2]]
    weight_qkv = sum(dot_tn(x, g) for x, g in zip(late[4:8], late[:4]))
    last = jnp.concatenate([weight_qkv, late[8]], axis=1).astype(bf16)
    last = last.reshape(lax.axis_size("dp"), shard, -1)
    last, weight_ffn, got[0] = lax.optimization_barrier((last, weight_ffn, got[0]))
    came = swap(near[1], 1)
    got[1], last, came, early, block_output = lax.optimization_barrier((got[1], last, came, early, block_output))
    grad_input, small = input_back(
        near[0], came, got, block_input, cotangent, grad_middle, early, gain_attn, mix_matrix, correct_gain
    )
    weight_ffn = weight_ffn.astype(f32)
    sum_gate_up = weight_ffn[:, : 2 * units].reshape(shard, 2, units)
    sum_down = weight_ffn[:, 2 * units :]
    last, small = end(last, small)
    sum_qkv = last[:, : 3 * feats].reshape(shard, 3, feats)
    sum_out = last[:, 3 * feats :]
    return (
        block_output,
        grad_input,
        sum_qkv,
        sum_out,
        sum_gate_up,
        sum_down,
        small[0],
        small[5],
        small[1:5].sum(axis=1).reshape(2, 2),
        small[6:].sum(axis=1),
    )


def solution(mesh):
    placed = (
        P(("dp", "tensor"), None),
        P("dp", None),
        P("dp", None, "tensor"),
        P("dp", "tensor"),
        P("dp", None, "tensor"),
        P("dp", "tensor"),
        P(),
        P(),
        P(),
        P(),
        P(("dp", "tensor"), None),
    )
    return jax.shard_map(
        local,
        mesh=mesh,
        in_specs=placed,
        out_specs=(
            P(("dp", "tensor"), None),
            P(("dp", "tensor"), None),
            P("dp", None, "tensor"),
            P("dp", "tensor"),
            P("dp", None, "tensor"),
            P("dp", "tensor"),
            P(),
            P(),
            P(),
            P(),
        ),
        check_vma=False,
    )
```

profile of v0, /device:TPU:8, one launch (start us, length us, event | category | flops | bytes accessed | tf_op | source)
XLA Modules:
  0.0 369.1 jit_solution(8351135176719765688)
XLA Ops:
  7.2 1.5 fusion.7
  8.7 2.1 convert_element_type.102
  10.8 2.2 multiply_reduce_fusion.3
  16.9 27.8 %start.1 = (bf16[640,768]{1,0:T(8,128)(2,1)}, bf16[640,768]{1,0:T(8,128)(2,1)}, bf16[640,768]{1,0:T(8,128)(2,1)}, bf16[8,96,576]{2,1,0:T(8,128)(2,1)}, bf16[8,96,192]{2,1,0:T(8,128)(2,1)}) custom-call(bf16[640,768]{1,0:T(8,128)(2,1)} %multiply_convert_fusion.1.x, bf16[96,576]{1,0:T(8,128)(2,1)} %copy.30.qkv, bf16[96,192]{1,0:T(8,128)(2,1)} %convert_element_type.106.wo), custom_call_target="tpu_custom_call" | custom-call | bytes 100000000 | tf_op jit(solution)/shard_map/start/pallas_call | solution.py:703
  47.0 2.1 convert_element_type.111
  49.8 4.0 %fusion.5 = (bf16[640,768]{1,0:T(8,128)(2,1)}, f32[640,768]{1,0:T(8,128)}) fusion(f32[640,1536]{1,0:T(8,128)S(1)} %convert_element_type.111, f32[]{:T(128)} %bitcast.6, f32[]{:T(128)} %bitcast.5), kind=kLoop, calls=%fused_computation.51 | loop fusion | flops 1966080 | bytes 6881288 | tf_op jit(solution)/shard_map/convert_element_type | solution.py:871
  54.3 1.9 convolution_convert_fusion.6.refs_1_
  56.1 1.8 convolution_convert_fusion.7.refs_0_
  58.0 1.8 convolution_convert_fusion.4.refs_3_
  59.8 1.9 convolution_convert_fusion.5.refs_2_
  61.6 30.0 %attn_fwd.1 = (bf16[4,640,192]{2,1,0:T(8,128)(2,1)}, f32[192,2560]{1,0:T(8,128)}, f32[8,2560]{1,0:T(8,128)}) custom-call(s32[1,5]{1,0:T(1,128)} %len_ref.3, s32[1]{0:T(128)} %bitcast.2.me_ref, bf16[640,576]{1,0:T(8,128)(2,1)} %convolution_convert_fusion.7.refs_0_, bf16[640,576]{1,0:T(8,128)(2,1)} %convolution_convert_fusion.6.refs_1_, ...), custom_call_target="tpu_custom_call" | custom-call | flops 2013265920 | bytes 5898240 | tf_op jit(solution)/shard_map/attn_fwd/pallas_call | solution.py:146
  91.7 2.4 slice_bitcast_fusion.7
  94.1 1.6 collective-permute-start.5
  95.7 1.4 fusion.4
  97.7 6.9 %collective-permute-done.5 = bf16[640,192]{1,0:T(8,128)(2,1)S(1)} collective-permute-done((bf16[640,192]{1,0:T(8,128)(2,1)S(1)}, bf16[640,192]{1,0:T(8,128)(2,1)S(1)}, u32[]{:S(2)}, u32[]{:S(2)}) %collective-permute-start.5) | collective-permute-done | bytes 245792 | tf_op jit(solution)/shard_map/ppermute | solution.py:575
  106.0 4.8 %collective-permute-done.6 = bf16[640,192]{1,0:T(8,128)(2,1)S(1)} collective-permute-done((bf16[640,192]{1,0:T(8,128)(2,1)S(1)}, bf16[640,192]{1,0:T(8,128)(2,1)S(1)}, u32[]{:S(2)}, u32[]{:S(2)}) %collective-permute-start.6) | collective-permute-done | bytes 245792 | tf_op jit(solution)/shard_map/ppermute | solution.py:575
  111.7 1.4 copy-done.4
  113.7 1.6 collective-permute-start.7
  115.3 10.6 %ffn_rows.4 = (bf16[640,768]{1,0:T(8,128)(2,1)}, bf16[640,768]{1,0:T(8,128)(2,1)}, bf16[640,768]{1,0:T(8,128)(2,1)}, f32[640,768]{1,0:T(8,128)}, bf16[640,768]{1,0:T(8,128)(2,1)}) custom-call(bf16[640,768]{1,0:T(8,128)(2,1)} %copy-done.30, bf16[640,768]{1,0:T(8,128)(2,1)} %get-tuple-element.87.g_ref.refs_4_, ...), custom_call_target="tpu_custom_call" | custom-call | flops 4529848320 | bytes 10420224 | tf_op jit(solution)/shard_map/ffn_rows/pallas_call | solution.py:372
  125.9 10.6 %ffn_rows.5 = (bf16[640,768]{1,0:T(8,128)(2,1)}, bf16[640,768]{1,0:T(8,128)(2,1)}, bf16[640,768]{1,0:T(8,128)(2,1)}, f32[640,768]{1,0:T(8,128)}, bf16[640,768]{1,0:T(8,128)(2,1)}) custom-call(bf16[640,768]{1,0:T(8,128)(2,1)} %collective-permute-done.8.x_ref.refs_1_, bf16[640,768]{1,0:T(8,128)(2,1)} %collective-permute-done.9.g_ref.refs_5_, ...), custom_call_target="tpu_custom_call" | custom-call | flops 4529848320 | bytes 10420224 | tf_op jit(solution)/shard_map/ffn_rows/pallas_call | solution.py:372
  137.7 2.8 collective-permute-done.10.x_ref.refs_3_
  141.4 11.1 %ffn_rows.7 = (bf16[640,768]{1,0:T(8,128)(2,1)}, bf16[640,768]{1,0:T(8,128)(2,1)}, bf16[640,768]{1,0:T(8,128)(2,1)}, f32[640,768]{1,0:T(8,128)}, bf16[640,768]{1,0:T(8,128)(2,1)}) custom-call(bf16[640,768]{1,0:T(8,128)(2,1)} %copy-done.44, bf16[640,768]{1,0:T(8,128)(2,1)} %collective-permute-done.11.g_ref.refs_7_, ...), custom_call_target="tpu_custom_call" | custom-call | flops 4529848320 | bytes 10420224 | tf_op jit(solution)/shard_map/ffn_rows/pallas_call | solution.py:372
  153.3 10.7 %ffn_rows.6 = (bf16[640,768]{1,0:T(8,128)(2,1)}, bf16[640,768]{1,0:T(8,128)(2,1)}, bf16[640,768]{1,0:T(8,128)(2,1)}, f32[640,768]{1,0:T(8,128)}, bf16[640,768]{1,0:T(8,128)(2,1)}) custom-call(bf16[640,768]{1,0:T(8,128)(2,1)} %collective-permute-done.7.x_ref.refs_2_, bf16[640,768]{1,0:T(8,128)(2,1)} %collective-permute-done.g_ref.refs_6_, ...), custom_call_target="tpu_custom_call" | custom-call | flops 4529848320 | bytes 10420224 | tf_op jit(solution)/shard_map/ffn_rows/pallas_call | solution.py:372
  163.9 2.7 add_convert_fusion.3
  166.6 1.6 collective-permute-start.15
  168.2 24.5 %wgrad.1 = bf16[768,2304]{1,0:T(8,128)(2,1)} custom-call(bf16[640,768]{1,0:T(8,128)(2,1)} %copy-done.30, bf16[640,768]{1,0:T(8,128)(2,1)} %collective-permute-done.8.x_ref.refs_1_, bf16[640,768]{1,0:T(8,128)(2,1)} %collective-permute-done.7.x_ref.refs_2_, bf16[640,768]{1,0:T(8,128)(2,1)} %copy-done.44, bf16[640,768]{1,0:T(8,128)(2,1)} %get-tuple-element.87.g_ref.refs_4_, ...), custom_call_target="tpu_custom_call" | custom-call | flops 9059696640 | bytes 23199744 | tf_op jit(solution)/shard_map/wgrad/pallas_call | solution.py:445
  194.1 7.4 %middle_back.1 = (f32[640,768]{1,0:T(8,128)}, bf16[640,768]{1,0:T(8,128)(2,1)}, bf16[640,192]{1,0:T(8,128)(2,1)}, bf16[640,192]{1,0:T(8,128)(2,1)}, bf16[640,192...) custom-call(bf16[640,768]{1,0:T(8,128)(2,1)} %get-tuple-element.96.share, bf16[640,768]{1,0:T(8,128)(2,1)} %copy-done.31, ...), custom_call_target="tpu_custom_call" | custom-call | flops 754974720 | bytes 10813440 | tf_op jit(solution)/shard_map/middle_back/pallas_call | solution.py:502
  201.9 1.3 collective-permute-start.19
  203.7 3.4 add_convert_fusion.4
  207.5 4.8 %collective-permute-done.18.refs_6_ = bf16[640,192]{1,0:T(8,128)(2,1)S(1)} collective-permute-done((bf16[640,192]{1,0:T(8,128)(2,1)}, bf16[640,192]{1,0:T(8,128)(2,1)S(1)}, u32[]{:S(2)}, u32[]{:S(2)}) %collective-permute-start.18) | collective-permute-done | bytes 245792 | tf_op jit(solution)/shard_map/ppermute | solution.py:575
  212.3 5.9 %collective-permute-done.19.refs_7_ = bf16[640,192]{1,0:T(8,128)(2,1)S(1)} collective-permute-done((bf16[640,192]{1,0:T(8,128)(2,1)}, bf16[640,192]{1,0:T(8,128)(2,1)S(1)}, u32[]{:S(2)}, u32[]{:S(2)}) %collective-permute-start.19) | collective-permute-done | bytes 245792 | tf_op jit(solution)/shard_map/ppermute | solution.py:575
  219.4 1.3 collective-permute-start.20
  224.5 31.4 %attn_bwd.1 = bf16[4,640,576]{2,1,0:T(8,128)(2,1)} custom-call(s32[1,5]{1,0:T(1,128)} %len_ref.3, s32[1]{0:T(128)} %bitcast.2.me_ref, bf16[640,576]{1,0:T(8,128)(2,1)} %convolution_convert_fusion.7.refs_0_, bf16[640,576]{1,0:T(8,128)(2,1)} %convolution_convert_fusion.6.refs_1_, bf16[640,576]{1,0:T(8,128)(2,1)} %convolution_convert_fusion.5.refs_2_, ...), custom_call_target="tpu_custom_call" | custom-call | flops 5033164800 | bytes 9830400 | tf_op jit(solution)/shard_map/attn_bwd/pallas_call | solution.py:290
  256.0 2.5 fusion.3
  258.5 2.2 convolution_convert_fusion.2
  261.6 4.0 %add_convert_fusion.1 = (bf16[640,768]{1,0:T(8,128)(2,1)S(1)}, f32[640,768]{1,0:T(8,128)S(1)}) fusion(f32[640,768]{1,0:T(8,128)S(1)} %get-tuple-element.185, f32[]{:T(128)} %bitcast.5, f32[640,768]{1,0:T(8,128)S(1)} %copy-done.5, bf16[640,768]{1,0:T(8,128)(2,1)} %collective-permute-done.13, f32[640,768]{1,0:T(8,128)S(1)} %copy-done.10, ...), kind=kLoop, calls=%fused_computation.2 | loop fusion | flops 3932160 | bytes 11796484 | tf_op jit(solution)/shard_map/convert
  265.9 2.6 multiply_reduce_fusion.1
  269.2 1.4 pad_maximum_fusion
  273.2 1.9 convolution_convert_fusion.1
  283.8 1.3 pad_maximum_fusion.1.blocks
  285.1 2.0 convolution_convert_fusion.share
  287.1 3.4 collective-permute-done.25.got_a
  290.5 10.1 %collective-permute-done.24.got_b = bf16[320,768]{1,0:T(8,128)(2,1)} collective-permute-done((bf16[320,768]{1,0:T(8,128)(2,1)}, bf16[320,768]{1,0:T(8,128)(2,1)}, u32[]{:S(2)}, u32[]{:S(2)}) %collective-permute-start.24) | collective-permute-done | bytes 491552 | tf_op jit(solution)/shard_map/ppermute | solution.py:575
  300.6 7.9 %input_back.1 = (f32[640,1536]{1,0:T(8,128)}, f32[8,768]{1,0:T(8,128)}) custom-call(bf16[640,768]{1,0:T(8,128)(2,1)} %convolution_convert_fusion.share, bf16[640,768]{1,0:T(8,128)(2,1)} %collective-permute-done.26.came, bf16[320,768]{1,0:T(8,128)(2,1)} %copy-done.33, bf16[320,768]{1,0:T(8,128)(2,1)} %collective-permute-done.24.got_b, ...), custom_call_target="tpu_custom_call" | custom-call | flops 29491200 | bytes 14745600 | tf_op jit(solution)/shard_map/input_back/pallas_call | solution.py:550
  308.5 43.6 %end.1 = (f32[96,768]{1,0:T(8,128)}, f32[8,768]{1,0:T(8,128)}) custom-call(bf16[8,96,768]{2,1,0:T(8,128)(2,1)} %pad_maximum_fusion.1.blocks, f32[8,768]{1,0:T(8,128)} %get-tuple-element.150.mine), custom_call_target="tpu_custom_call" | custom-call | bytes 50000000 | tf_op jit(solution)/shard_map/end/pallas_call | solution.py:817
  353.1 1.6 slice.107
  354.7 1.4 slice_reduce_fusion.2
  357.0 1.4 slice_reduce_fusion.1
  (188 shorter events, 39.6 us)
Async XLA Ops:
  7.2 108.1 %all-gather.2.cloned.1.call-start = ((), (), s32[]{:S(2)}) async-start(), calls=%async_computation.1 | async-start | bytes 3981312 | tf_op jit(solution)/shard_map/all_gather | solution.py:863
  44.8 245.7 %reduce-scatter.2.cloned.1.call-start = ((), (), s32[]{:S(2)}) async-start(), calls=%async_computation.2 | async-start | bytes 3981312 | tf_op jit(solution)/shard_map/reduce_scatter | solution.py:891
  44.8 46.8 %collective-permute-start.1 = (bf16[768,192]{1,0:T(8,128)(2,1)}, bf16[768,192]{1,0:T(8,128)(2,1)S(1)}, u32[]{:S(2)}, u32[]{:S(2)}) collective-permute-start(bf16[768,192]{1,0:T(8,128)(2,1)} %bitcast.72), channel_id=1, source_target_pairs={{0,2},{1,3},{2,0},{3,1},{4,6},{5,7},{6,4},{7,5},{8,10},{9,11},{10,... | collective-permute-start | bytes 884744 | tf_op jit(solution)/shard_map/ppermute | solution.py:575
  45.4 46.2 %collective-permute-start.2 = (bf16[768,192]{1,0:T(8,128)(2,1)}, bf16[768,192]{1,0:T(8,128)(2,1)S(1)}, u32[]{:S(2)}, u32[]{:S(2)}) collective-permute-start(bf16[768,192]{1,0:T(8,128)(2,1)} %bitcast.73), channel_id=1, source_target_pairs={{0,3},{1,2},{2,1},{3,0},{4,7},{5,6},{6,5},{7,4},{8,11},{9,10},{10,... | collective-permute-start | bytes 884744 | tf_op jit(solution)/shard_map/ppermute | solution.py:575
  46.6 58.5 %collective-permute-start.4 = (bf16[768,192]{1,0:T(8,128)(2,1)}, bf16[768,192]{1,0:T(8,128)(2,1)S(1)}, u32[]{:S(2)}, u32[]{:S(2)}) collective-permute-start(bf16[768,192]{1,0:T(8,128)(2,1)} %bitcast.74), channel_id=1, source_target_pairs={{0,1},{1,0},{2,3},{3,2},{4,5},{5,4},{6,7},{7,6},{8,9},{9,8},{10,11... | collective-permute-start | bytes 884744 | tf_op jit(solution)/shard_map/ppermute | solution.py:575
  49.1 4.7 %copy-start.2 = (f32[640,1536]{1,0:T(8,128)}, f32[640,1536]{1,0:T(8,128)S(1)}, u32[]{:S(2)}) copy-start(f32[640,1536]{1,0:T(8,128)S(1)} %convert_element_type.111) | copy-start | bytes 11796484
  49.8 4.5 %copy-start.28 = (bf16[640,768]{1,0:T(8,128)(2,1)S(1)}, bf16[640,768]{1,0:T(8,128)(2,1)}, u32[]{:S(2)}) copy-start(bf16[640,768]{1,0:T(8,128)(2,1)} %get-tuple-element.129) | copy-start | bytes 2949124
  49.8 4.5 %copy-start.41 = (bf16[8,96,576]{2,1,0:T(8,128)(2,1)S(1)}, bf16[8,96,576]{2,1,0:T(8,128)(2,1)}, u32[]{:S(2)}) copy-start(bf16[8,96,576]{2,1,0:T(8,128)(2,1)} %get-tuple-element.82) | copy-start | bytes 2654212
  53.8 37.8 %collective-permute-start = (bf16[640,768]{1,0:T(8,128)(2,1)}, bf16[640,768]{1,0:T(8,128)(2,1)}, u32[]{:S(2)}, u32[]{:S(2)}) collective-permute-start(bf16[640,768]{1,0:T(8,128)(2,1)} %get-tuple-element.87.g_ref.refs_4_), channel_id=1, source_target_pairs={{0,2},{1,3},{2,0},{3,1},{4,6},{5,7},{6,4},{7,5},{8,10},{9,11},{10,... | collective-permute-start | bytes 2949128 | tf_op jit(solution)/shard_map/ppermute | solution.py:575
  54.3 71.7 %collective-permute-start.9 = (bf16[640,768]{1,0:T(8,128)(2,1)}, bf16[640,768]{1,0:T(8,128)(2,1)}, u32[]{:S(2)}, u32[]{:S(2)}) collective-permute-start(bf16[640,768]{1,0:T(8,128)(2,1)} %get-tuple-element.87.g_ref.refs_4_), channel_id=1, source_target_pairs={{0,1},{1,0},{2,3},{3,2},{4,5},{5,4},{6,7},{7,6},{8,9},{9,8},{10,11... | collective-permute-start | bytes 2949128 | tf_op jit(solution)/shard_map/ppermute | solution.py:575
  91.6 13.0 %copy-start.14 = (bf16[768,192]{1,0:T(8,128)(2,1)}, bf16[768,192]{1,0:T(8,128)(2,1)S(1)}, u32[]{:S(2)}) copy-start(bf16[768,192]{1,0:T(8,128)(2,1)S(1)} %collective-permute-done.1.refs_2_) | copy-start | bytes 884740
  91.6 19.1 %copy-start.12 = (bf16[768,192]{1,0:T(8,128)(2,1)}, bf16[768,192]{1,0:T(8,128)(2,1)S(1)}, u32[]{:S(2)}) copy-start(bf16[768,192]{1,0:T(8,128)(2,1)S(1)} %collective-permute-done.2.refs_3_) | copy-start | bytes 884740
  94.1 10.6 %collective-permute-start.5 = (bf16[640,192]{1,0:T(8,128)(2,1)S(1)}, bf16[640,192]{1,0:T(8,128)(2,1)S(1)}, u32[]{:S(2)}, u32[]{:S(2)}) collective-permute-start(bf16[640,192]{1,0:T(8,128)(2,1)S(1)} %get-tuple-element.193), channel_id=1, source_target_pairs={{0,2},{1,3},{2,0},{3,1},{4,6},{5,7},{6,4},{7,5},{8,10},{9,11},{10,... | collective-permute-start | bytes 737288 | tf_op jit(solution)/shard_map/ppermute | solution.py:575
  97.1 8.0 %collective-permute-start.3 = (bf16[640,192]{1,0:T(8,128)(2,1)S(1)}, bf16[640,192]{1,0:T(8,128)(2,1)S(1)}, u32[]{:S(2)}, u32[]{:S(2)}) collective-permute-start(bf16[640,192]{1,0:T(8,128)(2,1)S(1)} %get-tuple-element.194), channel_id=1, source_target_pairs={{0,1},{1,0},{2,3},{3,2},{4,5},{5,4},{6,7},{7,6},{8,9},{9,8},{10,11... | collective-permute-start | bytes 737288 | tf_op jit(solution)/shard_map/ppermute | solution.py:575
  97.4 13.3 %collective-permute-start.6 = (bf16[640,192]{1,0:T(8,128)(2,1)S(1)}, bf16[640,192]{1,0:T(8,128)(2,1)S(1)}, u32[]{:S(2)}, u32[]{:S(2)}) collective-permute-start(bf16[640,192]{1,0:T(8,128)(2,1)S(1)} %get-tuple-element.192), channel_id=1, source_target_pairs={{0,3},{1,2},{2,1},{3,0},{4,7},{5,6},{6,5},{7,4},{8,11},{9,10},{10,... | collective-permute-start | bytes 737288 | tf_op jit(solution)/shard_map/ppermute | solution.py:575
  105.1 6.5 %copy-start.15 = (bf16[768,192]{1,0:T(8,128)(2,1)}, bf16[768,192]{1,0:T(8,128)(2,1)S(1)}, u32[]{:S(2)}) copy-start(bf16[768,192]{1,0:T(8,128)(2,1)S(1)} %collective-permute-done.4.refs_1_) | copy-start | bytes 884740
  106.0 7.1 %copy-start.37 = (f32[768]{0:T(1024)S(1)}, f32[768]{0:T(1024)}, u32[]{:S(2)}) copy-start(f32[768]{0:T(1024)} %param.18) | copy-start | bytes 9220
  113.3 12.6 %collective-permute-start.8 = (bf16[640,768]{1,0:T(8,128)(2,1)S(1)}, bf16[640,768]{1,0:T(8,128)(2,1)}, u32[]{:S(2)}, u32[]{:S(2)}) collective-permute-start(bf16[640,768]{1,0:T(8,128)(2,1)S(1)} %multiply_convert_fusion.x_ref.refs_0_), channel_id=1, source_target_pairs={{0,1},{1,0},{2,3},{3,2},{4,5},{5,4},{6,7},{7,6},{8,9},{9,8},{10,11... | collective-permute-start | bytes 2949128 | tf_op jit(solution)/shard_map/ppermute | solution.py:575
  113.7 24.0 %collective-permute-start.7 = (bf16[640,768]{1,0:T(8,128)(2,1)S(1)}, bf16[640,768]{1,0:T(8,128)(2,1)}, u32[]{:S(2)}, u32[]{:S(2)}) collective-permute-start(bf16[640,768]{1,0:T(8,128)(2,1)S(1)} %multiply_convert_fusion.x_ref.refs_0_), channel_id=1, source_target_pairs={{0,2},{1,3},{2,0},{3,1},{4,6},{5,7},{6,4},{7,5},{8,10},{9,11},{10,... | collective-permute-start | bytes 2949128 | tf_op jit(solution)/shard_map/ppermute | solution.py:575
  115.3 22.4 %collective-permute-start.11 = (bf16[640,768]{1,0:T(8,128)(2,1)}, bf16[640,768]{1,0:T(8,128)(2,1)}, u32[]{:S(2)}, u32[]{:S(2)}) collective-permute-start(bf16[640,768]{1,0:T(8,128)(2,1)} %collective-permute-done.g_ref.refs_6_), channel_id=1, source_target_pairs={{0,1},{1,0},{2,3},{3,2},{4,5},{5,4},{6,7},{7,6},{8,9},{9,8},{10,11... | collective-permute-start | bytes 2949128 | tf_op jit(solution)/shard_map/ppermute | solution.py:575
  137.7 2.8 collective-permute-start.10
  152.5 11.4 %collective-permute-start.14 = (bf16[640,768]{1,0:T(8,128)(2,1)}, bf16[640,768]{1,0:T(8,128)(2,1)}, u32[]{:S(2)}, u32[]{:S(2)}) collective-permute-start(bf16[640,768]{1,0:T(8,128)(2,1)} %get-tuple-element.98), channel_id=1, source_target_pairs={{0,1},{1,0},{2,3},{3,2},{4,5},{5,4},{6,7},{7,6},{8,9},{9,8},{10,11... | collective-permute-start | bytes 2949128 | tf_op jit(solution)/shard_map/ppermute | solution.py:575
  152.7 39.9 %collective-permute-start.16 = (bf16[640,768]{1,0:T(8,128)(2,1)}, bf16[640,768]{1,0:T(8,128)(2,1)S(1)}, u32[]{:S(2)}, u32[]{:S(2)}) collective-permute-start(bf16[640,768]{1,0:T(8,128)(2,1)} %get-tuple-element.99), channel_id=1, source_target_pairs={{0,1},{1,0},{2,3},{3,2},{4,5},{5,4},{6,7},{7,6},{8,9},{9,8},{10,11... | collective-permute-start | bytes 2949128 | tf_op jit(solution)/shard_map/ppermute | solution.py:575
  153.1 50.5 %collective-permute-start.12 = (f32[640,768]{1,0:T(8,128)}, f32[640,768]{1,0:T(8,128)}, u32[]{:S(2)}, u32[]{:S(2)}) collective-permute-start(f32[640,768]{1,0:T(8,128)} %get-tuple-element.95), channel_id=1, source_target_pairs={{0,1},{1,0},{2,3},{3,2},{4,5},{5,4},{6,7},{7,6},{8,9},{9,8},{10,11... | collective-permute-start | bytes 5898248 | tf_op jit(solution)/shard_map/ppermute | solution.py:575
  166.6 26.1 %collective-permute-start.15 = (bf16[640,768]{1,0:T(8,128)(2,1)}, bf16[640,768]{1,0:T(8,128)(2,1)}, u32[]{:S(2)}, u32[]{:S(2)}) collective-permute-start(bf16[640,768]{1,0:T(8,128)(2,1)} %add_convert_fusion.3), channel_id=1, source_target_pairs={{0,2},{1,3},{2,0},{3,1},{4,6},{5,7},{6,4},{7,5},{8,10},{9,11},{10,... | collective-permute-start | bytes 2949128 | tf_op jit(solution)/shard_map/ppermute | solution.py:575
  194.0 67.6 %collective-permute-start.27 = (f32[640,768]{1,0:T(8,128)}, f32[640,768]{1,0:T(8,128)}, u32[]{:S(2)}, u32[]{:S(2)}) collective-permute-start(f32[640,768]{1,0:T(8,128)} %get-tuple-element.140), channel_id=1, source_target_pairs={{0,1},{1,0},{2,3},{3,2},{4,5},{5,4},{6,7},{7,6},{8,9},{9,8},{10,11... | collective-permute-start | bytes 5898248 | tf_op jit(solution)/shard_map/ppermute | solution.py:575
  201.4 10.9 %collective-permute-start.18 = (bf16[640,192]{1,0:T(8,128)(2,1)}, bf16[640,192]{1,0:T(8,128)(2,1)S(1)}, u32[]{:S(2)}, u32[]{:S(2)}) collective-permute-start(bf16[640,192]{1,0:T(8,128)(2,1)} %get-tuple-element.115), channel_id=1, source_target_pairs={{0,2},{1,3},{2,0},{3,1},{4,6},{5,7},{6,4},{7,5},{8,10},{9,11},{10,... | collective-permute-start | bytes 737288 | tf_op jit(solution)/shard_map/ppermute | solution.py:575
  201.9 16.3 %collective-permute-start.19 = (bf16[640,192]{1,0:T(8,128)(2,1)}, bf16[640,192]{1,0:T(8,128)(2,1)S(1)}, u32[]{:S(2)}, u32[]{:S(2)}) collective-permute-start(bf16[640,192]{1,0:T(8,128)(2,1)} %get-tuple-element.116), channel_id=1, source_target_pairs={{0,3},{1,2},{2,1},{3,0},{4,7},{5,6},{6,5},{7,4},{8,11},{9,10},{10,... | collective-permute-start | bytes 737288 | tf_op jit(solution)/shard_map/ppermute | solution.py:575
  203.3 20.2 %collective-permute-start.17 = (bf16[640,192]{1,0:T(8,128)(2,1)}, bf16[640,192]{1,0:T(8,128)(2,1)S(1)}, u32[]{:S(2)}, u32[]{:S(2)}) collective-permute-start(bf16[640,192]{1,0:T(8,128)(2,1)} %get-tuple-element.114), channel_id=1, source_target_pairs={{0,1},{1,0},{2,3},{3,2},{4,5},{5,4},{6,7},{7,6},{8,9},{9,8},{10,11... | collective-permute-start | bytes 737288 | tf_op jit(solution)/shard_map/ppermute | solution.py:575
  203.6 14.6 %copy-start.6 = (bf16[640,768]{1,0:T(8,128)(2,1)S(1)}, bf16[640,768]{1,0:T(8,128)(2,1)}, u32[]{:S(2)}) copy-start(bf16[640,768]{1,0:T(8,128)(2,1)} %get-tuple-element.120) | copy-start | bytes 2949124
  203.6 14.6 %copy-start.22 = (bf16[640,192]{1,0:T(8,128)(2,1)S(1)}, bf16[640,192]{1,0:T(8,128)(2,1)}, u32[]{:S(2)}) copy-start(bf16[640,192]{1,0:T(8,128)(2,1)} %copy-done.21) | copy-start | bytes 737284
  203.7 17.1 %copy-start.20 = (bf16[640,192]{1,0:T(8,128)(2,1)S(1)}, bf16[640,192]{1,0:T(8,128)(2,1)}, u32[]{:S(2)}) copy-start(bf16[640,192]{1,0:T(8,128)(2,1)} %copy-done.19) | copy-start | bytes 737284
  207.1 15.3 %copy-start.17 = (bf16[640,192]{1,0:T(8,128)(2,1)S(1)}, bf16[640,192]{1,0:T(8,128)(2,1)}, u32[]{:S(2)}) copy-start(bf16[640,192]{1,0:T(8,128)(2,1)} %copy-done.16) | copy-start | bytes 737284
  207.1 51.4 %collective-permute-start.13 = (bf16[640,768]{1,0:T(8,128)(2,1)}, bf16[640,768]{1,0:T(8,128)(2,1)}, u32[]{:S(2)}, u32[]{:S(2)}) collective-permute-start(bf16[640,768]{1,0:T(8,128)(2,1)} %add_convert_fusion.4), channel_id=1, source_target_pairs={{0,2},{1,3},{2,0},{3,1},{4,6},{5,7},{6,4},{7,5},{8,10},{9,11},{10,... | collective-permute-start | bytes 2949128 | tf_op jit(solution)/shard_map/ppermute | solution.py:575
  212.3 11.2 %copy-start.45 = (bf16[640,192]{1,0:T(8,128)(2,1)}, bf16[640,192]{1,0:T(8,128)(2,1)S(1)}, u32[]{:S(2)}) copy-start(bf16[640,192]{1,0:T(8,128)(2,1)S(1)} %collective-permute-done.18.refs_6_) | copy-start | bytes 737284
  218.2 5.3 %copy-start.46 = (bf16[640,192]{1,0:T(8,128)(2,1)}, bf16[640,192]{1,0:T(8,128)(2,1)S(1)}, u32[]{:S(2)}) copy-start(bf16[640,192]{1,0:T(8,128)(2,1)S(1)} %collective-permute-done.19.refs_7_) | copy-start | bytes 737284
  219.4 36.6 %collective-permute-start.20 = (bf16[768,192]{0,1:T(8,128)(2,1)}, bf16[768,192]{0,1:T(8,128)(2,1)}, u32[]{:S(2)}, u32[]{:S(2)}) collective-permute-start(bf16[768,192]{0,1:T(8,128)(2,1)} %convolution_convert_fusion.10), channel_id=1, source_target_pairs={{0,1},{1,0},{2,3},{3,2},{4,5},{5,4},{6,7},{7,6},{8,9},{9,8},{10,11... | collective-permute-start | bytes 884744 | tf_op jit(solution)/shard_map/ppermute | solution.py:575
  221.9 34.1 %collective-permute-start.21 = (bf16[768,192]{0,1:T(8,128)(2,1)}, bf16[768,192]{0,1:T(8,128)(2,1)}, u32[]{:S(2)}, u32[]{:S(2)}) collective-permute-start(bf16[768,192]{0,1:T(8,128)(2,1)} %convolution_convert_fusion.9), channel_id=1, source_target_pairs={{0,2},{1,3},{2,0},{3,1},{4,6},{5,7},{6,4},{7,5},{8,10},{9,11},{10,... | collective-permute-start | bytes 884744 | tf_op jit(solution)/shard_map/ppermute | solution.py:575
  223.5 32.5 %collective-permute-start.22 = (bf16[768,192]{0,1:T(8,128)(2,1)}, bf16[768,192]{0,1:T(8,128)(2,1)}, u32[]{:S(2)}, u32[]{:S(2)}) collective-permute-start(bf16[768,192]{0,1:T(8,128)(2,1)} %convolution_convert_fusion.8), channel_id=1, source_target_pairs={{0,3},{1,2},{2,1},{3,0},{4,7},{5,6},{6,5},{7,4},{8,11},{9,10},{10,... | collective-permute-start | bytes 884744 | tf_op jit(solution)/shard_map/ppermute | solution.py:575
  224.5 31.5 %copy-start.18 = (bf16[640,192]{1,0:T(8,128)(2,1)S(1)}, bf16[640,192]{1,0:T(8,128)(2,1)}, u32[]{:S(2)}) copy-start(bf16[640,192]{1,0:T(8,128)(2,1)} %get-tuple-element.121) | copy-start | bytes 737284
  256.0 5.6 %copy-start.10 = (f32[640,768]{1,0:T(8,128)S(1)}, f32[640,768]{1,0:T(8,128)}, u32[]{:S(2)}) copy-start(f32[640,768]{1,0:T(8,128)} %get-tuple-element.139) | copy-start | bytes 5898244
  260.8 11.4 %collective-permute-start.23 = (bf16[640,768]{1,0:T(8,128)(2,1)S(1)}, bf16[640,768]{1,0:T(8,128)(2,1)S(1)}, u32[]{:S(2)}, u32[]{:S(2)}) collective-permute-start(bf16[640,768]{1,0:T(8,128)(2,1)S(1)} %convolution_convert_fusion.2), channel_id=1, source_target_pairs={{0,1},{1,0},{2,3},{3,2},{4,5},{5,4},{6,7},{7,6},{8,9},{9,8},{10,11... | collective-permute-start | bytes 2949128 | tf_op jit(solution)/shard_map/ppermute | solution.py:575
  273.2 5.0 %copy-start.29 = (bf16[640,768]{1,0:T(8,128)(2,1)S(1)}, bf16[640,768]{1,0:T(8,128)(2,1)}, u32[]{:S(2)}) copy-start(bf16[640,768]{1,0:T(8,128)(2,1)} %get-tuple-element.129) | copy-start | bytes 2949124
  275.1 25.5 %collective-permute-start.26 = (bf16[640,768]{1,0:T(8,128)(2,1)}, bf16[640,768]{1,0:T(8,128)(2,1)}, u32[]{:S(2)}, u32[]{:S(2)}) collective-permute-start(bf16[640,768]{1,0:T(8,128)(2,1)} %convolution_convert_fusion.1), channel_id=1, source_target_pairs={{0,1},{1,0},{2,3},{3,2},{4,5},{5,4},{6,7},{7,6},{8,9},{9,8},{10,11... | collective-permute-start | bytes 2949128 | tf_op jit(solution)/shard_map/ppermute | solution.py:575
  276.2 14.3 %collective-permute-start.25 = (bf16[320,768]{1,0:T(8,128)(2,1)}, bf16[320,768]{1,0:T(8,128)(2,1)S(1)}, u32[]{:S(2)}, u32[]{:S(2)}) collective-permute-start(bf16[320,768]{1,0:T(8,128)(2,1)} %get-tuple-element.195), channel_id=1, source_target_pairs={{0,2},{1,3},{2,0},{3,1},{4,6},{5,7},{6,4},{7,5},{8,10},{9,11},{10,... | collective-permute-start | bytes 1474568 | tf_op jit(solution)/shard_map/ppermute | solution.py:575
  277.2 23.4 %collective-permute-start.24 = (bf16[320,768]{1,0:T(8,128)(2,1)}, bf16[320,768]{1,0:T(8,128)(2,1)}, u32[]{:S(2)}, u32[]{:S(2)}) collective-permute-start(bf16[320,768]{1,0:T(8,128)(2,1)} %get-tuple-element.196), channel_id=1, source_target_pairs={{0,2},{1,3},{2,0},{3,1},{4,6},{5,7},{6,4},{7,5},{8,10},{9,11},{10,... | collective-permute-start | bytes 1474568 | tf_op jit(solution)/shard_map/ppermute | solution.py:575
  290.5 10.1 %copy-start.33 = (bf16[320,768]{1,0:T(8,128)(2,1)}, bf16[320,768]{1,0:T(8,128)(2,1)S(1)}, u32[]{:S(2)}) copy-start(bf16[320,768]{1,0:T(8,128)(2,1)S(1)} %collective-permute-done.25.got_a) | copy-start | bytes 1474564
  308.5 49.9 %copy-start.11 = (bf16[96,2304]{1,0:T(8,128)(2,1)S(1)}, bf16[96,2304]{1,0:T(8,128)(2,1)}, u32[]{:S(2)}) copy-start(bf16[96,2304]{1,0:T(8,128)(2,1)} %reduce-scatter.2.cloned.1.call-done) | copy-start | bytes 1327108
  (30 other events, 66.8 us)
Sparse Core Ops, SparseCore 0:
  44.9 63.7 all-gather.1
  192.9 80.0 reduce-scatter.1
where the time goes:
time: 373 us; the launch traced here: 369 us
  Pallas kernels  216 us (58%)
  waiting for transfers between devices  39.9 us (11%)
  other arithmetic  31.6 us (8%)
  matrix products  27.6 us (7%)
  local copies, waits for them, and re-layouts  21.8 us (6%)
  starting transfers between devices  17.6 us (5%)
  between operations  14.9 us (4%)
    pallas_call x1, Pallas kernels, end(): pl.pallas_call(functools.partial(end_kernel, count), out_shape=(jax.Shape...  43.6 us
    pallas_call x4, Pallas kernels, ffn_rows(): pl.pallas_call(functools.partial(ffn_kernel, tile), out_shape=(wide, wide...  43 us
    ppermute x28, waiting for transfers between devices, swap(): return lax.ppermute(array, 'tensor', [(i, i ^ bit) for i in range(count)])  39.9 us
    pallas_call x1, Pallas kernels, attn_bwd(): pl.pallas_call(functools.partial(bwd_kernel, heads, parts), out_shape=jax...  31.4 us
    pallas_call x1, Pallas kernels, attn_fwd(): pl.pallas_call(functools.partial(fwd_kernel, heads, parts), out_shape=(ja...  30 us
    pallas_call x1, Pallas kernels, start(): pl.pallas_call(functools.partial(start_kernel, count, chunks), out_shape=...  27.8 us
    pallas_call x1, Pallas kernels, wgrad(): pl.pallas_call(functools.partial(wgrad_kernel, parts, n), out_shape=jax.S...  24.5 us
    ppermute x28, starting transfers between devices, swap(): return lax.ppermute(array, 'tensor', [(i, i ^ bit) for i in range(count)])  17.5 us
  transfers between devices with their start and end apart: 30, of which 8 were waited for; matrix products, arithmetic and copies ran while one was open for 15% of the time, Pallas kernels for 34%

commit v1 on v0

--- a/solution.py
+++ b/solution.py
@@ -750,10 +750,9 @@
     return near + got.astype(f32), beside
 
 
-def end_kernel(count, blocks, mine, out, total, own, inbox, near, mid, far, own_sem, in_sem, near_sem, far_sem):
+def end_kernel(count, mine, total, near, mid, far, near_sem, far_sem):
     t = lax.axis_index("tensor")
     g = lax.axis_index("dp")
-    f32 = jnp.float32
     barrier = pltpu.get_barrier_semaphore()
     for c in (1, 2, 3):
         pl.semaphore_signal(barrier, inc=1, device_id={"tensor": flipped(t, c)}, device_id_type=MESH)
@@ -766,17 +765,6 @@
             mine, near.at[c - 1], near_sem.at[0, c - 1], near_sem.at[1, c - 1], {"tensor": flipped(t, c)}, MESH
         )
         for c in (1, 2, 3)
-    ]
-    ins = [
-        pltpu.make_async_remote_copy(
-            blocks.at[flipped(g, e)],
-            inbox.at[e - 1],
-            in_sem.at[0, e - 1],
-            in_sem.at[1, e - 1],
-            {"dp": flipped(g, e)},
-            MESH,
-        )
-        for e in range(1, count)
     ]
     fars = [
         pltpu.make_async_remote_copy(
@@ -784,7 +772,6 @@
         )
         for e in range(1, count)
     ]
-    kept = pltpu.make_async_copy(blocks.at[g], own, own_sem.at[0])
     for copy in nears:
         copy.start()
     for copy in nears:
@@ -792,51 +779,36 @@
     mid[...] = (mine[...] + near[0]) + (near[1] + near[2])
     for copy in fars:
         copy.start()
-    for copy in ins:
-        copy.start()
-    kept.start()
     for copy in fars:
         copy.wait_recv()
     level = [mid[...]] + [far[e] for e in range(count - 1)]
     while len(level) > 1:
         level = [level[k] + level[k + 1] for k in range(0, len(level), 2)]
     total[...] = level[0]
-    kept.wait()
-    out[...] = own[...].astype(f32)
-    for e, copy in enumerate(ins):
-        copy.wait_recv()
-        out[...] += inbox[e].astype(f32)
-    for copy in nears + fars + ins:
+    for copy in nears + fars:
         copy.wait_send()
 
 
-def end(blocks, mine):
-    count, rows, cols = blocks.shape
+def end(mine):
+    count = lax.axis_size("dp")
     dma = pltpu.SemaphoreType.DMA
     vmem = pl.BlockSpec(memory_space=pltpu.VMEM)
     return pl.pallas_call(
         functools.partial(end_kernel, count),
-        out_shape=(
-            jax.ShapeDtypeStruct((rows, cols), jnp.float32),
-            jax.ShapeDtypeStruct(mine.shape, jnp.float32),
-        ),
-        in_specs=[pl.BlockSpec(memory_space=pl.ANY), vmem],
-        out_specs=(vmem, vmem),
+        out_shape=jax.ShapeDtypeStruct(mine.shape, jnp.float32),
+        in_specs=[vmem],
+        out_specs=vmem,
         scratch_shapes=[
-            pltpu.VMEM((rows, cols), blocks.dtype),
-            pltpu.VMEM((count - 1, rows, cols), blocks.dtype),
             pltpu.VMEM((3, *mine.shape), jnp.float32),
             pltpu.VMEM(mine.shape, jnp.float32),
             pltpu.VMEM((count - 1, *mine.shape), jnp.float32),
-            dma((1,)),
-            dma((2, count - 1)),
             dma((2, 3)),
             dma((2, count - 1)),
         ],
         compiler_params=pltpu.CompilerParams(collective_id=1, has_side_effects=True),
-        cost_estimate=pl.CostEstimate(flops=0, bytes_accessed=50_000_000, transcendentals=0),
+        cost_estimate=pl.CostEstimate(flops=0, bytes_accessed=30_000_000, transcendentals=0),
         name="end",
-    )(blocks, mine)
+    )(mine)
 
 
 def local(
@@ -922,8 +894,8 @@
     near = [dot_nt(g, qkv_all).astype(bf16) for g in late[:2]]
     weight_qkv = sum(dot_tn(x, g) for x, g in zip(late[4:8], late[:4]))
     last = jnp.concatenate([weight_qkv, late[8]], axis=1).astype(bf16)
-    last = last.reshape(lax.axis_size("dp"), shard, -1)
     last, weight_ffn, got[0] = lax.optimization_barrier((last, weight_ffn, got[0]))
+    summed_last = lax.psum_scatter(last, "dp", scatter_dimension=0, tiled=True)
     came = swap(near[1], 1)
     got[1], last, came, early, block_output = lax.optimization_barrier((got[1], last, came, early, block_output))
     grad_input, small = input_back(
@@ -932,7 +904,8 @@
     weight_ffn = weight_ffn.astype(f32)
     sum_gate_up = weight_ffn[:, : 2 * units].reshape(shard, 2, units)
     sum_down = weight_ffn[:, 2 * units :]
-    last, small = end(last, small)
+    small = end(small)
+    last = summed_last.astype(f32)
     sum_qkv = last[:, : 3 * feats].reshape(shard, 3, feats)
     sum_out = last[:, 3 * feats :]
     return (

time: 373 us -> 365 us (0.979)
  the two profiles are of different devices: /device:TPU:8 before, /device:TPU:0 now
where the time goes in v1:
time: 365 us; the launch traced here: 360 us
  Pallas kernels  192 us (53%)
  waiting for transfers between devices  56.8 us (16%)
  other arithmetic  31.3 us (9%)
  matrix products  25.9 us (7%)
  local copies, waits for them, and re-layouts  23 us (6%)
  starting transfers between devices  15.9 us (4%)
  between operations  14.7 us (4%)
    ppermute x28, waiting for transfers between devices, swap(): return lax.ppermute(array, 'tensor', [(i, i ^ bit) for i in range(count)])  46.1 us
    pallas_call x4, Pallas kernels, ffn_rows(): pl.pallas_call(functools.partial(ffn_kernel, tile), out_shape=(wide, wide...  42.8 us
    pallas_call x1, Pallas kernels, attn_bwd(): pl.pallas_call(functools.partial(bwd_kernel, heads, parts), out_shape=jax...  30.2 us
    pallas_call x1, Pallas kernels, start(): pl.pallas_call(functools.partial(start_kernel, count, chunks), out_shape=...  29.3 us
    pallas_call x1, Pallas kernels, attn_fwd(): pl.pallas_call(functools.partial(fwd_kernel, heads, parts), out_shape=(ja...  28.5 us
    pallas_call x1, Pallas kernels, wgrad(): pl.pallas_call(functools.partial(wgrad_kernel, parts, n), out_shape=jax.S...  24.5 us
    pallas_call x1, Pallas kernels, end(): pl.pallas_call(functools.partial(end_kernel, count), out_shape=jax.ShapeD...  21.5 us
    ppermute x28, starting transfers between devices, swap(): return lax.ppermute(array, 'tensor', [(i, i ^ bit) for i in range(count)])  15.8 us
  transfers between devices with their start and end apart: 31, of which 10 were waited for; matrix products, arithmetic and copies ran while one was open for 17% of the time, Pallas kernels for 42%

profile of v1, /device:TPU:0, one launch (start us, length us, event | category | flops | bytes accessed | tf_op | source)
XLA Modules:
  0.0 360.2 jit_solution(15830669553593961671)
XLA Ops:
  7.2 1.5 fusion.7
  8.7 2.1 convert_element_type.104
  10.8 2.2 multiply_reduce_fusion.3
  16.9 29.3 %start.1 = (bf16[640,768]{1,0:T(8,128)(2,1)}, bf16[640,768]{1,0:T(8,128)(2,1)}, bf16[640,768]{1,0:T(8,128)(2,1)}, bf16[8,96,576]{2,1,0:T(8,128)(2,1)}, bf16[8,96,192]{2,1,0:T(8,128)(2,1)}) custom-call(bf16[640,768]{1,0:T(8,128)(2,1)} %multiply_convert_fusion.1.x, bf16[96,576]{1,0:T(8,128)(2,1)} %copy.37.qkv, bf16[96,192]{1,0:T(8,128)(2,1)} %convert_element_type.108.wo), custom_call_target="tpu_custom_call" | custom-call | bytes 100000000 | tf_op jit(solution)/shard_map/start/pallas_call | solution.py:703
  46.9 1.3 collective-permute-start.2
  48.5 2.1 convert_element_type.113
  51.3 4.0 %fusion.5 = (bf16[640,768]{1,0:T(8,128)(2,1)}, f32[640,768]{1,0:T(8,128)}) fusion(f32[640,1536]{1,0:T(8,128)S(1)} %convert_element_type.113, f32[]{:T(128)} %bitcast.6, f32[]{:T(128)} %bitcast.5), kind=kLoop, calls=%fused_computation.51 | loop fusion | flops 1966080 | bytes 6881288 | tf_op jit(solution)/shard_map/convert_element_type | solution.py:843
  55.8 1.8 convolution_convert_fusion.6.refs_1_
  57.6 1.8 convolution_convert_fusion.7.refs_0_
  59.5 1.9 convolution_convert_fusion.4.refs_3_
  61.3 1.8 convolution_convert_fusion.5.refs_2_
  63.2 28.5 %attn_fwd.1 = (bf16[4,640,192]{2,1,0:T(8,128)(2,1)}, f32[192,2560]{1,0:T(8,128)}, f32[8,2560]{1,0:T(8,128)}) custom-call(s32[1,5]{1,0:T(1,128)} %len_ref.3, s32[1]{0:T(128)} %bitcast.2.me_ref, bf16[640,576]{1,0:T(8,128)(2,1)} %convolution_convert_fusion.7.refs_0_, bf16[640,576]{1,0:T(8,128)(2,1)} %convolution_convert_fusion.6.refs_1_, ...), custom_call_target="tpu_custom_call" | custom-call | flops 2013265920 | bytes 5898240 | tf_op jit(solution)/shard_map/attn_fwd/pallas_call | solution.py:146
  91.7 2.4 slice_bitcast_fusion.7
  94.1 1.6 collective-permute-start.5
  95.7 1.4 fusion.4
  97.7 6.9 %collective-permute-done.5 = bf16[640,192]{1,0:T(8,128)(2,1)S(1)} collective-permute-done((bf16[640,192]{1,0:T(8,128)(2,1)S(1)}, bf16[640,192]{1,0:T(8,128)(2,1)S(1)}, u32[]{:S(2)}, u32[]{:S(2)}) %collective-permute-start.5) | collective-permute-done | bytes 245792 | tf_op jit(solution)/shard_map/ppermute | solution.py:575
  106.0 4.8 %collective-permute-done.6 = bf16[640,192]{1,0:T(8,128)(2,1)S(1)} collective-permute-done((bf16[640,192]{1,0:T(8,128)(2,1)S(1)}, bf16[640,192]{1,0:T(8,128)(2,1)S(1)}, u32[]{:S(2)}, u32[]{:S(2)}) %collective-permute-start.6) | collective-permute-done | bytes 245792 | tf_op jit(solution)/shard_map/ppermute | solution.py:575
  111.8 1.4 copy-done.4
  113.7 1.6 collective-permute-start.7
  115.3 10.7 %ffn_rows.4 = (bf16[640,768]{1,0:T(8,128)(2,1)}, bf16[640,768]{1,0:T(8,128)(2,1)}, bf16[640,768]{1,0:T(8,128)(2,1)}, f32[640,768]{1,0:T(8,128)}, bf16[640,768]{1,0:T(8,128)(2,1)}) custom-call(bf16[640,768]{1,0:T(8,128)(2,1)} %copy-done.31, bf16[640,768]{1,0:T(8,128)(2,1)} %get-tuple-element.84.g_ref.refs_4_, ...), custom_call_target="tpu_custom_call" | custom-call | flops 4529848320 | bytes 10420224 | tf_op jit(solution)/shard_map/ffn_rows/pallas_call | solution.py:372
  126.0 10.6 %ffn_rows.5 = (bf16[640,768]{1,0:T(8,128)(2,1)}, bf16[640,768]{1,0:T(8,128)(2,1)}, bf16[640,768]{1,0:T(8,128)(2,1)}, f32[640,768]{1,0:T(8,128)}, bf16[640,768]{1,0:T(8,128)(2,1)}) custom-call(bf16[640,768]{1,0:T(8,128)(2,1)} %collective-permute-done.8.x_ref.refs_1_, bf16[640,768]{1,0:T(8,128)(2,1)} %collective-permute-done.9.g_ref.refs_5_, ...), custom_call_target="tpu_custom_call" | custom-call | flops 4529848320 | bytes 10420224 | tf_op jit(solution)/shard_map/ffn_rows/pallas_call | solution.py:372
  137.7 2.8 collective-permute-done.10.x_ref.refs_3_
  141.5 10.9 %ffn_rows.7 = (bf16[640,768]{1,0:T(8,128)(2,1)}, bf16[640,768]{1,0:T(8,128)(2,1)}, bf16[640,768]{1,0:T(8,128)(2,1)}, f32[640,768]{1,0:T(8,128)}, bf16[640,768]{1,0:T(8,128)(2,1)}) custom-call(bf16[640,768]{1,0:T(8,128)(2,1)} %copy-done.47, bf16[640,768]{1,0:T(8,128)(2,1)} %collective-permute-done.11.g_ref.refs_7_, ...), custom_call_target="tpu_custom_call" | custom-call | flops 4529848320 | bytes 10420224 | tf_op jit(solution)/shard_map/ffn_rows/pallas_call | solution.py:372
  153.0 10.6 %ffn_rows.6 = (bf16[640,768]{1,0:T(8,128)(2,1)}, bf16[640,768]{1,0:T(8,128)(2,1)}, bf16[640,768]{1,0:T(8,128)(2,1)}, f32[640,768]{1,0:T(8,128)}, bf16[640,768]{1,0:T(8,128)(2,1)}) custom-call(bf16[640,768]{1,0:T(8,128)(2,1)} %collective-permute-done.7.x_ref.refs_2_, bf16[640,768]{1,0:T(8,128)(2,1)} %collective-permute-done.g_ref.refs_6_, ...), custom_call_target="tpu_custom_call" | custom-call | flops 4529848320 | bytes 10420224 | tf_op jit(solution)/shard_map/ffn_rows/pallas_call | solution.py:372
  163.6 2.7 add_convert_fusion.3
  166.3 1.6 collective-permute-start.15
  167.9 24.5 %wgrad.1 = bf16[768,2304]{1,0:T(8,128)(2,1)} custom-call(bf16[640,768]{1,0:T(8,128)(2,1)} %copy-done.31, bf16[640,768]{1,0:T(8,128)(2,1)} %collective-permute-done.8.x_ref.refs_1_, bf16[640,768]{1,0:T(8,128)(2,1)} %collective-permute-done.7.x_ref.refs_2_, bf16[640,768]{1,0:T(8,128)(2,1)} %copy-done.47, bf16[640,768]{1,0:T(8,128)(2,1)} %get-tuple-element.84.g_ref.refs_4_, ...), custom_call_target="tpu_custom_call" | custom-call | flops 9059696640 | bytes 23199744 | tf_op jit(solution)/shard_map/wgrad/pallas_call | solution.py:445
  193.3 7.8 %middle_back.1 = (f32[640,768]{1,0:T(8,128)}, bf16[640,768]{1,0:T(8,128)(2,1)}, bf16[640,192]{1,0:T(8,128)(2,1)}, bf16[640,192]{1,0:T(8,128)(2,1)}, bf16[640,192...) custom-call(bf16[640,768]{1,0:T(8,128)(2,1)} %get-tuple-element.93.share, bf16[640,768]{1,0:T(8,128)(2,1)} %copy-done.32, ...), custom_call_target="tpu_custom_call" | custom-call | flops 754974720 | bytes 10813440 | tf_op jit(solution)/shard_map/middle_back/pallas_call | solution.py:502
  201.6 1.4 collective-permute-start.19
  203.3 3.4 add_convert_fusion.4
  207.2 4.8 %collective-permute-done.18.refs_6_ = bf16[640,192]{1,0:T(8,128)(2,1)S(1)} collective-permute-done((bf16[640,192]{1,0:T(8,128)(2,1)}, bf16[640,192]{1,0:T(8,128)(2,1)S(1)}, u32[]{:S(2)}, u32[]{:S(2)}) %collective-permute-start.18) | collective-permute-done | bytes 245792 | tf_op jit(solution)/shard_map/ppermute | solution.py:575
  212.0 6.1 %collective-permute-done.19.refs_7_ = bf16[640,192]{1,0:T(8,128)(2,1)S(1)} collective-permute-done((bf16[640,192]{1,0:T(8,128)(2,1)}, bf16[640,192]{1,0:T(8,128)(2,1)S(1)}, u32[]{:S(2)}, u32[]{:S(2)}) %collective-permute-start.19) | collective-permute-done | bytes 245792 | tf_op jit(solution)/shard_map/ppermute | solution.py:575
  224.8 30.2 %attn_bwd.1 = bf16[4,640,576]{2,1,0:T(8,128)(2,1)} custom-call(s32[1,5]{1,0:T(1,128)} %len_ref.3, s32[1]{0:T(128)} %bitcast.2.me_ref, bf16[640,576]{1,0:T(8,128)(2,1)} %convolution_convert_fusion.7.refs_0_, bf16[640,576]{1,0:T(8,128)(2,1)} %convolution_convert_fusion.6.refs_1_, bf16[640,576]{1,0:T(8,128)(2,1)} %convolution_convert_fusion.5.refs_2_, ...), custom_call_target="tpu_custom_call" | custom-call | flops 5033164800 | bytes 9830400 | tf_op jit(solution)/shard_map/attn_bwd/pallas_call | solution.py:290
  255.0 1.7 fusion.3
  256.8 2.3 convolution_convert_fusion.2
  261.0 1.3 collective-permute-done.23
  269.2 8.5 %collective-permute-done.25.got_a = bf16[320,768]{1,0:T(8,128)(2,1)} collective-permute-done((bf16[320,768]{1,0:T(8,128)(2,1)S(1)}, bf16[320,768]{1,0:T(8,128)(2,1)}, u32[]{:S(2)}, u32[]{:S(2)}) %collective-permute-start.25) | collective-permute-done | bytes 491552 | tf_op jit(solution)/shard_map/ppermute | solution.py:575
  277.7 1.6 copy.48
  279.4 4.8 %add_convert_fusion.1 = (bf16[640,768]{1,0:T(8,128)(2,1)S(1)}, f32[640,768]{1,0:T(8,128)S(1)}) fusion(f32[640,768]{1,0:T(8,128)S(1)} %get-tuple-element.189, f32[]{:T(128)} %bitcast.5, f32[640,768]{1,0:T(8,128)} %copy-done.4, bf16[640,768]{1,0:T(8,128)(2,1)} %collective-permute-done.13, f32[640,768]{1,0:T(8,128)} %get-tuple-element.136, ...), kind=kLoop, calls=%fused_computation.2 | loop fusion | flops 3932160 | bytes 11796484 | tf_op jit(solution)/shard_map/convert
  285.3 2.6 multiply_reduce_fusion.1
  288.0 1.4 pad_maximum_fusion
  290.4 2.0 convolution_convert_fusion.share
  293.2 9.9 %collective-permute-done.24.got_b = bf16[320,768]{1,0:T(8,128)(2,1)S(1)} collective-permute-done((bf16[320,768]{1,0:T(8,128)(2,1)S(1)}, bf16[320,768]{1,0:T(8,128)(2,1)S(1)}, u32[]{:S(2)}, u32[]{:S(2)}) %collective-permute-start.24) | collective-permute-done | bytes 491552 | tf_op jit(solution)/shard_map/ppermute | solution.py:575
  304.2 8.0 %input_back.1 = (f32[640,1536]{1,0:T(8,128)}, f32[8,768]{1,0:T(8,128)}) custom-call(bf16[640,768]{1,0:T(8,128)(2,1)} %convolution_convert_fusion.share, bf16[640,768]{1,0:T(8,128)(2,1)} %copy-done.33, bf16[320,768]{1,0:T(8,128)(2,1)} %collective-permute-done.25.got_a, bf16[320,768]{1,0:T(8,128)(2,1)} %copy-done.35, bf16[640,1536]{1,0:T(8,128)(2,1)} %inputs.1, ...), custom_call_target="tpu_custom_call" | custom-call | flops 29491200 | bytes 14745600 | tf_op jit(solution)/shard_map/input_back/pallas_call | solution.py:550
  312.2 21.5 %end.1 = f32[8,768]{1,0:T(8,128)} custom-call(f32[8,768]{1,0:T(8,128)} %get-tuple-element.147.mine), custom_call_target="tpu_custom_call" | custom-call | bytes 30000000 | tf_op jit(solution)/shard_map/end/pallas_call | solution.py:796
  336.4 1.4 slice_reduce_fusion.1
  337.7 1.4 slice_reduce_fusion.2
  339.2 10.6 %reduce-scatter.7.cloned.1.call-done = bf16[96,768]{1,0:T(8,128)(2,1)} async-done(((bf16[768,768]{1,0:T(8,128)(2,1)}), bf16[96,768]{1,0:T(8,128)(2,1)}) %reduce-scatter.7.cloned.1.call-update) | async-done | bytes 147472
  (198 shorter events, 40.2 us)
Async XLA Ops:
  7.2 108.1 %all-gather.2.cloned.1.call-start = ((), (), s32[]{:S(2)}) async-start(), calls=%async_computation.2 | async-start | bytes 3981312 | tf_op jit(solution)/shard_map/all_gather | solution.py:835
  46.3 231.5 %reduce-scatter.5.cloned.1.call-start = ((), (), s32[]{:S(2)}) async-start(), calls=%async_computation.3 | async-start | bytes 3981312 | tf_op jit(solution)/shard_map/reduce_scatter | solution.py:863
  46.3 45.3 %collective-permute-start.1 = (bf16[768,192]{1,0:T(8,128)(2,1)}, bf16[768,192]{1,0:T(8,128)(2,1)S(1)}, u32[]{:S(2)}, u32[]{:S(2)}) collective-permute-start(bf16[768,192]{1,0:T(8,128)(2,1)} %bitcast.70), channel_id=1, source_target_pairs={{0,2},{1,3},{2,0},{3,1},{4,6},{5,7},{6,4},{7,5},{8,10},{9,11},{10,... | collective-permute-start | bytes 884744 | tf_op jit(solution)/shard_map/ppermute | solution.py:575
  46.9 44.8 %collective-permute-start.2 = (bf16[768,192]{1,0:T(8,128)(2,1)}, bf16[768,192]{1,0:T(8,128)(2,1)S(1)}, u32[]{:S(2)}, u32[]{:S(2)}) collective-permute-start(bf16[768,192]{1,0:T(8,128)(2,1)} %bitcast.71), channel_id=1, source_target_pairs={{0,3},{1,2},{2,1},{3,0},{4,7},{5,6},{6,5},{7,4},{8,11},{9,10},{10,... | collective-permute-start | bytes 884744 | tf_op jit(solution)/shard_map/ppermute | solution.py:575
  48.2 57.0 %collective-permute-start.4 = (bf16[768,192]{1,0:T(8,128)(2,1)}, bf16[768,192]{1,0:T(8,128)(2,1)S(1)}, u32[]{:S(2)}, u32[]{:S(2)}) collective-permute-start(bf16[768,192]{1,0:T(8,128)(2,1)} %bitcast.72), channel_id=1, source_target_pairs={{0,1},{1,0},{2,3},{3,2},{4,5},{5,4},{6,7},{7,6},{8,9},{9,8},{10,11... | collective-permute-start | bytes 884744 | tf_op jit(solution)/shard_map/ppermute | solution.py:575
  50.6 4.7 %copy-start.2 = (f32[640,1536]{1,0:T(8,128)}, f32[640,1536]{1,0:T(8,128)S(1)}, u32[]{:S(2)}) copy-start(f32[640,1536]{1,0:T(8,128)S(1)} %convert_element_type.113) | copy-start | bytes 11796484
  55.3 36.4 %collective-permute-start = (bf16[640,768]{1,0:T(8,128)(2,1)}, bf16[640,768]{1,0:T(8,128)(2,1)}, u32[]{:S(2)}, u32[]{:S(2)}) collective-permute-start(bf16[640,768]{1,0:T(8,128)(2,1)} %get-tuple-element.84.g_ref.refs_4_), channel_id=1, source_target_pairs={{0,2},{1,3},{2,0},{3,1},{4,6},{5,7},{6,4},{7,5},{8,10},{9,11},{10,... | collective-permute-start | bytes 2949128 | tf_op jit(solution)/shard_map/ppermute | solution.py:575
  55.7 70.2 %collective-permute-start.9 = (bf16[640,768]{1,0:T(8,128)(2,1)}, bf16[640,768]{1,0:T(8,128)(2,1)}, u32[]{:S(2)}, u32[]{:S(2)}) collective-permute-start(bf16[640,768]{1,0:T(8,128)(2,1)} %get-tuple-element.84.g_ref.refs_4_), channel_id=1, source_target_pairs={{0,1},{1,0},{2,3},{3,2},{4,5},{5,4},{6,7},{7,6},{8,9},{9,8},{10,11... | collective-permute-start | bytes 2949128 | tf_op jit(solution)/shard_map/ppermute | solution.py:575
  91.6 13.0 %copy-start.16 = (bf16[768,192]{1,0:T(8,128)(2,1)}, bf16[768,192]{1,0:T(8,128)(2,1)S(1)}, u32[]{:S(2)}) copy-start(bf16[768,192]{1,0:T(8,128)(2,1)S(1)} %collective-permute-done.1.refs_2_) | copy-start | bytes 884740
  91.7 19.1 %copy-start.14 = (bf16[768,192]{1,0:T(8,128)(2,1)}, bf16[768,192]{1,0:T(8,128)(2,1)S(1)}, u32[]{:S(2)}) copy-start(bf16[768,192]{1,0:T(8,128)(2,1)S(1)} %collective-permute-done.2.refs_3_) | copy-start | bytes 884740
  94.1 10.6 %collective-permute-start.5 = (bf16[640,192]{1,0:T(8,128)(2,1)S(1)}, bf16[640,192]{1,0:T(8,128)(2,1)S(1)}, u32[]{:S(2)}, u32[]{:S(2)}) collective-permute-start(bf16[640,192]{1,0:T(8,128)(2,1)S(1)} %get-tuple-element.197), channel_id=1, source_target_pairs={{0,2},{1,3},{2,0},{3,1},{4,6},{5,7},{6,4},{7,5},{8,10},{9,11},{10,... | collective-permute-start | bytes 737288 | tf_op jit(solution)/shard_map/ppermute | solution.py:575
  97.1 8.0 %collective-permute-start.3 = (bf16[640,192]{1,0:T(8,128)(2,1)S(1)}, bf16[640,192]{1,0:T(8,128)(2,1)S(1)}, u32[]{:S(2)}, u32[]{:S(2)}) collective-permute-start(bf16[640,192]{1,0:T(8,128)(2,1)S(1)} %get-tuple-element.198), channel_id=1, source_target_pairs={{0,1},{1,0},{2,3},{3,2},{4,5},{5,4},{6,7},{7,6},{8,9},{9,8},{10,11... | collective-permute-start | bytes 737288 | tf_op jit(solution)/shard_map/ppermute | solution.py:575
  97.4 13.4 %collective-permute-start.6 = (bf16[640,192]{1,0:T(8,128)(2,1)S(1)}, bf16[640,192]{1,0:T(8,128)(2,1)S(1)}, u32[]{:S(2)}, u32[]{:S(2)}) collective-permute-start(bf16[640,192]{1,0:T(8,128)(2,1)S(1)} %get-tuple-element.196), channel_id=1, source_target_pairs={{0,3},{1,2},{2,1},{3,0},{4,7},{5,6},{6,5},{7,4},{8,11},{9,10},{10,... | collective-permute-start | bytes 737288 | tf_op jit(solution)/shard_map/ppermute | solution.py:575
  105.2 6.6 %copy-start.17 = (bf16[768,192]{1,0:T(8,128)(2,1)}, bf16[768,192]{1,0:T(8,128)(2,1)S(1)}, u32[]{:S(2)}) copy-start(bf16[768,192]{1,0:T(8,128)(2,1)S(1)} %collective-permute-done.4.refs_1_) | copy-start | bytes 884740
  106.0 7.2 %copy-start.40 = (f32[768]{0:T(1024)S(1)}, f32[768]{0:T(1024)}, u32[]{:S(2)}) copy-start(f32[768]{0:T(1024)} %param.18) | copy-start | bytes 9220
  113.4 12.6 %collective-permute-start.8 = (bf16[640,768]{1,0:T(8,128)(2,1)S(1)}, bf16[640,768]{1,0:T(8,128)(2,1)}, u32[]{:S(2)}, u32[]{:S(2)}) collective-permute-start(bf16[640,768]{1,0:T(8,128)(2,1)S(1)} %multiply_convert_fusion.x_ref.refs_0_), channel_id=1, source_target_pairs={{0,1},{1,0},{2,3},{3,2},{4,5},{5,4},{6,7},{7,6},{8,9},{9,8},{10,11... | collective-permute-start | bytes 2949128 | tf_op jit(solution)/shard_map/ppermute | solution.py:575
  113.7 24.0 %collective-permute-start.7 = (bf16[640,768]{1,0:T(8,128)(2,1)S(1)}, bf16[640,768]{1,0:T(8,128)(2,1)}, u32[]{:S(2)}, u32[]{:S(2)}) collective-permute-start(bf16[640,768]{1,0:T(8,128)(2,1)S(1)} %multiply_convert_fusion.x_ref.refs_0_), channel_id=1, source_target_pairs={{0,2},{1,3},{2,0},{3,1},{4,6},{5,7},{6,4},{7,5},{8,10},{9,11},{10,... | collective-permute-start | bytes 2949128 | tf_op jit(solution)/shard_map/ppermute | solution.py:575
  115.3 22.4 %collective-permute-start.11 = (bf16[640,768]{1,0:T(8,128)(2,1)}, bf16[640,768]{1,0:T(8,128)(2,1)}, u32[]{:S(2)}, u32[]{:S(2)}) collective-permute-start(bf16[640,768]{1,0:T(8,128)(2,1)} %collective-permute-done.g_ref.refs_6_), channel_id=1, source_target_pairs={{0,1},{1,0},{2,3},{3,2},{4,5},{5,4},{6,7},{7,6},{8,9},{9,8},{10,11... | collective-permute-start | bytes 2949128 | tf_op jit(solution)/shard_map/ppermute | solution.py:575
  137.7 2.8 collective-permute-start.10
  152.4 11.2 %collective-permute-start.14 = (bf16[640,768]{1,0:T(8,128)(2,1)}, bf16[640,768]{1,0:T(8,128)(2,1)}, u32[]{:S(2)}, u32[]{:S(2)}) collective-permute-start(bf16[640,768]{1,0:T(8,128)(2,1)} %get-tuple-element.95), channel_id=1, source_target_pairs={{0,1},{1,0},{2,3},{3,2},{4,5},{5,4},{6,7},{7,6},{8,9},{9,8},{10,11... | collective-permute-start | bytes 2949128 | tf_op jit(solution)/shard_map/ppermute | solution.py:575
  152.6 39.7 %collective-permute-start.16 = (bf16[640,768]{1,0:T(8,128)(2,1)}, bf16[640,768]{1,0:T(8,128)(2,1)S(1)}, u32[]{:S(2)}, u32[]{:S(2)}) collective-permute-start(bf16[640,768]{1,0:T(8,128)(2,1)} %get-tuple-element.96), channel_id=1, source_target_pairs={{0,1},{1,0},{2,3},{3,2},{4,5},{5,4},{6,7},{7,6},{8,9},{9,8},{10,11... | collective-permute-start | bytes 2949128 | tf_op jit(solution)/shard_map/ppermute | solution.py:575
  166.3 26.1 %collective-permute-start.15 = (bf16[640,768]{1,0:T(8,128)(2,1)}, bf16[640,768]{1,0:T(8,128)(2,1)}, u32[]{:S(2)}, u32[]{:S(2)}) collective-permute-start(bf16[640,768]{1,0:T(8,128)(2,1)} %add_convert_fusion.3), channel_id=1, source_target_pairs={{0,2},{1,3},{2,0},{3,1},{4,6},{5,7},{6,4},{7,5},{8,10},{9,11},{10,... | collective-permute-start | bytes 2949128 | tf_op jit(solution)/shard_map/ppermute | solution.py:575
  167.9 35.4 %collective-permute-start.12 = (f32[640,768]{1,0:T(8,128)}, f32[640,768]{1,0:T(8,128)}, u32[]{:S(2)}, u32[]{:S(2)}) collective-permute-start(f32[640,768]{1,0:T(8,128)} %get-tuple-element.92), channel_id=1, source_target_pairs={{0,1},{1,0},{2,3},{3,2},{4,5},{5,4},{6,7},{7,6},{8,9},{9,8},{10,11... | collective-permute-start | bytes 5898248 | tf_op jit(solution)/shard_map/ppermute | solution.py:575
  192.4 157.4 %reduce-scatter.7.cloned.1.call-start = ((), (), s32[]{:S(2)}) async-start(), calls=%async_computation.4 | async-start | bytes 1327104
  201.1 10.9 %collective-permute-start.18 = (bf16[640,192]{1,0:T(8,128)(2,1)}, bf16[640,192]{1,0:T(8,128)(2,1)S(1)}, u32[]{:S(2)}, u32[]{:S(2)}) collective-permute-start(bf16[640,192]{1,0:T(8,128)(2,1)} %get-tuple-element.112), channel_id=1, source_target_pairs={{0,2},{1,3},{2,0},{3,1},{4,6},{5,7},{6,4},{7,5},{8,10},{9,11},{10,... | collective-permute-start | bytes 737288 | tf_op jit(solution)/shard_map/ppermute | solution.py:575
  201.6 16.4 %collective-permute-start.19 = (bf16[640,192]{1,0:T(8,128)(2,1)}, bf16[640,192]{1,0:T(8,128)(2,1)S(1)}, u32[]{:S(2)}, u32[]{:S(2)}) collective-permute-start(bf16[640,192]{1,0:T(8,128)(2,1)} %get-tuple-element.113), channel_id=1, source_target_pairs={{0,3},{1,2},{2,1},{3,0},{4,7},{5,6},{6,5},{7,4},{8,11},{9,10},{10,... | collective-permute-start | bytes 737288 | tf_op jit(solution)/shard_map/ppermute | solution.py:575
  203.0 21.0 %collective-permute-start.17 = (bf16[640,192]{1,0:T(8,128)(2,1)}, bf16[640,192]{1,0:T(8,128)(2,1)S(1)}, u32[]{:S(2)}, u32[]{:S(2)}) collective-permute-start(bf16[640,192]{1,0:T(8,128)(2,1)} %get-tuple-element.111), channel_id=1, source_target_pairs={{0,1},{1,0},{2,3},{3,2},{4,5},{5,4},{6,7},{7,6},{8,9},{9,8},{10,11... | collective-permute-start | bytes 737288 | tf_op jit(solution)/shard_map/ppermute | solution.py:575
  203.3 14.8 %copy-start.5 = (bf16[640,768]{1,0:T(8,128)(2,1)S(1)}, bf16[640,768]{1,0:T(8,128)(2,1)}, u32[]{:S(2)}) copy-start(bf16[640,768]{1,0:T(8,128)(2,1)} %get-tuple-element.117) | copy-start | bytes 2949124
  203.3 14.8 %copy-start.24 = (bf16[640,192]{1,0:T(8,128)(2,1)S(1)}, bf16[640,192]{1,0:T(8,128)(2,1)}, u32[]{:S(2)}) copy-start(bf16[640,192]{1,0:T(8,128)(2,1)} %copy-done.23) | copy-start | bytes 737284
  203.3 17.1 %copy-start.22 = (bf16[640,192]{1,0:T(8,128)(2,1)S(1)}, bf16[640,192]{1,0:T(8,128)(2,1)}, u32[]{:S(2)}) copy-start(bf16[640,192]{1,0:T(8,128)(2,1)} %copy-done.21) | copy-start | bytes 737284
  206.7 15.3 %copy-start.19 = (bf16[640,192]{1,0:T(8,128)(2,1)S(1)}, bf16[640,192]{1,0:T(8,128)(2,1)}, u32[]{:S(2)}) copy-start(bf16[640,192]{1,0:T(8,128)(2,1)} %copy-done.18) | copy-start | bytes 737284
  206.7 50.0 %collective-permute-start.13 = (bf16[640,768]{1,0:T(8,128)(2,1)}, bf16[640,768]{1,0:T(8,128)(2,1)}, u32[]{:S(2)}, u32[]{:S(2)}) collective-permute-start(bf16[640,768]{1,0:T(8,128)(2,1)} %add_convert_fusion.4), channel_id=1, source_target_pairs={{0,2},{1,3},{2,0},{3,1},{4,6},{5,7},{6,4},{7,5},{8,10},{9,11},{10,... | collective-permute-start | bytes 2949128 | tf_op jit(solution)/shard_map/ppermute | solution.py:575
  211.9 11.2 %copy-start.48 = (bf16[640,192]{1,0:T(8,128)(2,1)}, bf16[640,192]{1,0:T(8,128)(2,1)S(1)}, u32[]{:S(2)}) copy-start(bf16[640,192]{1,0:T(8,128)(2,1)S(1)} %collective-permute-done.18.refs_6_) | copy-start | bytes 737284
  218.1 5.1 %copy-start.49 = (bf16[640,192]{1,0:T(8,128)(2,1)}, bf16[640,192]{1,0:T(8,128)(2,1)S(1)}, u32[]{:S(2)}) copy-start(bf16[640,192]{1,0:T(8,128)(2,1)S(1)} %collective-permute-done.19.refs_7_) | copy-start | bytes 737284
  219.2 35.7 %collective-permute-start.20 = (bf16[768,192]{0,1:T(8,128)(2,1)}, bf16[768,192]{0,1:T(8,128)(2,1)}, u32[]{:S(2)}, u32[]{:S(2)}) collective-permute-start(bf16[768,192]{0,1:T(8,128)(2,1)} %convolution_convert_fusion.10), channel_id=1, source_target_pairs={{0,1},{1,0},{2,3},{3,2},{4,5},{5,4},{6,7},{7,6},{8,9},{9,8},{10,11... | collective-permute-start | bytes 884744 | tf_op jit(solution)/shard_map/ppermute | solution.py:575
  221.5 33.4 %collective-permute-start.21 = (bf16[768,192]{0,1:T(8,128)(2,1)}, bf16[768,192]{0,1:T(8,128)(2,1)}, u32[]{:S(2)}, u32[]{:S(2)}) collective-permute-start(bf16[768,192]{0,1:T(8,128)(2,1)} %convolution_convert_fusion.9), channel_id=1, source_target_pairs={{0,2},{1,3},{2,0},{3,1},{4,6},{5,7},{6,4},{7,5},{8,10},{9,11},{10,... | collective-permute-start | bytes 884744 | tf_op jit(solution)/shard_map/ppermute | solution.py:575
  223.1 31.8 %collective-permute-start.22 = (bf16[768,192]{0,1:T(8,128)(2,1)}, bf16[768,192]{0,1:T(8,128)(2,1)}, u32[]{:S(2)}, u32[]{:S(2)}) collective-permute-start(bf16[768,192]{0,1:T(8,128)(2,1)} %convolution_convert_fusion.8), channel_id=1, source_target_pairs={{0,3},{1,2},{2,1},{3,0},{4,7},{5,6},{6,5},{7,4},{8,11},{9,10},{10,... | collective-permute-start | bytes 884744 | tf_op jit(solution)/shard_map/ppermute | solution.py:575
  224.8 30.2 %copy-start.20 = (bf16[640,192]{1,0:T(8,128)(2,1)S(1)}, bf16[640,192]{1,0:T(8,128)(2,1)}, u32[]{:S(2)}) copy-start(bf16[640,192]{1,0:T(8,128)(2,1)} %get-tuple-element.118) | copy-start | bytes 737284
  259.0 3.2 collective-permute-start.23
  260.7 18.7 %collective-permute-start.27 = (f32[640,768]{1,0:T(8,128)}, f32[640,768]{1,0:T(8,128)}, u32[]{:S(2)}, u32[]{:S(2)}) collective-permute-start(f32[640,768]{1,0:T(8,128)} %get-tuple-element.137), channel_id=1, source_target_pairs={{0,1},{1,0},{2,3},{3,2},{4,5},{5,4},{6,7},{7,6},{8,9},{9,8},{10,11... | collective-permute-start | bytes 5898248 | tf_op jit(solution)/shard_map/ppermute | solution.py:575
  261.0 4.6 %copy-start.8 = (bf16[640,576]{1,0:T(8,128)(2,1)}, bf16[640,576]{1,0:T(8,128)(2,1)S(1)}, u32[]{:S(2)}) copy-start(bf16[640,576]{1,0:T(8,128)(2,1)S(1)} %get-tuple-element.125) | copy-start | bytes 2211844
  264.1 13.6 %collective-permute-start.25 = (bf16[320,768]{1,0:T(8,128)(2,1)S(1)}, bf16[320,768]{1,0:T(8,128)(2,1)}, u32[]{:S(2)}, u32[]{:S(2)}) collective-permute-start(bf16[320,768]{1,0:T(8,128)(2,1)S(1)} %get-tuple-element.199), channel_id=1, source_target_pairs={{0,2},{1,3},{2,0},{3,1},{4,6},{5,7},{6,4},{7,5},{8,10},{9,11},{10,... | collective-permute-start | bytes 1474568 | tf_op jit(solution)/shard_map/ppermute | solution.py:575
  279.4 4.9 %copy-start.11 = (bf16[640,576]{1,0:T(8,128)(2,1)S(1)}, bf16[640,576]{1,0:T(8,128)(2,1)}, u32[]{:S(2)}) copy-start(bf16[640,576]{1,0:T(8,128)(2,1)} %copy-done.10) | copy-start | bytes 2211844
  279.4 4.9 %copy-start.46 = (bf16[8,96,576]{2,1,0:T(8,128)(2,1)S(1)}, bf16[8,96,576]{2,1,0:T(8,128)(2,1)}, u32[]{:S(2)}) copy-start(bf16[8,96,576]{2,1,0:T(8,128)(2,1)} %get-tuple-element.79) | copy-start | bytes 2654212
  279.4 5.9 %copy-start.1 = (f32[640,1536]{1,0:T(8,128)S(1)}, f32[640,1536]{1,0:T(8,128)}, u32[]{:S(2)}) copy-start(f32[640,1536]{1,0:T(8,128)} %copy-done) | copy-start | bytes 11796484
  279.4 5.9 %copy-start.3 = (f32[640,1536]{1,0:T(8,128)S(1)}, f32[640,1536]{1,0:T(8,128)}, u32[]{:S(2)}) copy-start(f32[640,1536]{1,0:T(8,128)} %copy-done.2) | copy-start | bytes 11796484
  285.2 17.8 %collective-permute-start.26 = (bf16[640,768]{1,0:T(8,128)(2,1)S(1)}, bf16[640,768]{1,0:T(8,128)(2,1)S(1)}, u32[]{:S(2)}, u32[]{:S(2)}) collective-permute-start(bf16[640,768]{1,0:T(8,128)(2,1)S(1)} %convolution_convert_fusion.1), channel_id=1, source_target_pairs={{0,1},{1,0},{2,3},{3,2},{4,5},{5,4},{6,7},{7,6},{8,9},{9,8},{10,11... | collective-permute-start | bytes 2949128 | tf_op jit(solution)/shard_map/ppermute | solution.py:575
  289.4 13.6 %collective-permute-start.24 = (bf16[320,768]{1,0:T(8,128)(2,1)S(1)}, bf16[320,768]{1,0:T(8,128)(2,1)S(1)}, u32[]{:S(2)}, u32[]{:S(2)}) collective-permute-start(bf16[320,768]{1,0:T(8,128)(2,1)S(1)} %copy-done.36), channel_id=1, source_target_pairs={{0,2},{1,3},{2,0},{3,1},{4,6},{5,7},{6,4},{7,5},{8,10},{9,11},{10,... | collective-permute-start | bytes 1474568 | tf_op jit(solution)/shard_map/ppermute | solution.py:575
  (34 other events, 73.0 us)
Sparse Core Ops, SparseCore 0:
  46.4 63.8 all-gather.1
  192.5 81.6 reduce-scatter.4
  279.5 70.2 reduce-scatter.6

commit v2 on v1

--- a/solution.py
+++ b/solution.py
@@ -891,11 +891,12 @@
     half = far.shape[0] // 2
     got = [swap(far[:half], 2), swap(far[half:], 2)]
     *late, far = lax.optimization_barrier((*grad_proj, *normed_attn, weight_out, far))
-    near = [dot_nt(g, qkv_all).astype(bf16) for g in late[:2]]
     weight_qkv = sum(dot_tn(x, g) for x, g in zip(late[4:8], late[:4]))
     last = jnp.concatenate([weight_qkv, late[8]], axis=1).astype(bf16)
-    last, weight_ffn, got[0] = lax.optimization_barrier((last, weight_ffn, got[0]))
+    last, weight_ffn = lax.optimization_barrier((last, weight_ffn))
     summed_last = lax.psum_scatter(last, "dp", scatter_dimension=0, tiled=True)
+    got[0], *late = lax.optimization_barrier((got[0], *late[:2]))
+    near = [dot_nt(g, qkv_all).astype(bf16) for g in late]
     came = swap(near[1], 1)
     got[1], last, came, early, block_output = lax.optimization_barrier((got[1], last, came, early, block_output))
     grad_input, small = input_back(

time: 365 us -> 358 us (0.981)
  waiting for transfers between devices: 56.8 us -> 51.9 us
  Pallas kernels: 192 us -> 188 us
    pallas_call x1, Pallas kernels: 21.5 us -> 13 us  [end(): pl.pallas_call(functools.partial(end_kernel, count), out_shape=jax.ShapeD...]
    ppermute x28, waiting for transfers between devices: 46.1 us -> 39.8 us  [swap(): return lax.ppermute(array, 'tensor', [(i, i ^ bit) for i in range(count)])]
  transfers between devices with their start and end apart: 31 -> 31, of which waited for: 10 -> 10; matrix products, arithmetic and copies ran while one was open for 17% -> 18% of each run, Pallas kernels for 42% -> 42%
where the time goes in v2:
time: 358 us; the launch traced here: 351 us
  Pallas kernels  188 us (53%)
  waiting for transfers between devices  51.9 us (14%)
  other arithmetic  31.3 us (9%)
  matrix products  26 us (7%)
  local copies, waits for them, and re-layouts  23 us (6%)
  starting transfers between devices  15.9 us (4%)
  between operations  14.7 us (4%)
    pallas_call x4, Pallas kernels, ffn_rows(): pl.pallas_call(functools.partial(ffn_kernel, tile), out_shape=(wide, wide...  42.8 us
    ppermute x28, waiting for transfers between devices, swap(): return lax.ppermute(array, 'tensor', [(i, i ^ bit) for i in range(count)])  39.8 us
    pallas_call x1, Pallas kernels, attn_bwd(): pl.pallas_call(functools.partial(bwd_kernel, heads, parts), out_shape=jax...  31.9 us
    pallas_call x1, Pallas kernels, attn_fwd(): pl.pallas_call(functools.partial(fwd_kernel, heads, parts), out_shape=(ja...  31 us
    pallas_call x1, Pallas kernels, start(): pl.pallas_call(functools.partial(start_kernel, count, chunks), out_shape=...  29.3 us
    pallas_call x1, Pallas kernels, wgrad(): pl.pallas_call(functools.partial(wgrad_kernel, parts, n), out_shape=jax.S...  24.5 us
    ppermute x28, starting transfers between devices, swap(): return lax.ppermute(array, 'tensor', [(i, i ^ bit) for i in range(count)])  15.7 us
    pallas_call x1, Pallas kernels, end(): pl.pallas_call(functools.partial(end_kernel, count), out_shape=jax.ShapeD...  13 us
  transfers between devices with their start and end apart: 31, of which 10 were waited for; matrix products, arithmetic and copies ran while one was open for 18% of the time, Pallas kernels for 42%

profile of v2, /device:TPU:0, one launch (start us, length us, event | category | flops | bytes accessed | tf_op | source)
XLA Modules:
  0.0 351.2 jit_solution(17913716467500062913)
XLA Ops:
  7.2 1.5 fusion.7
  8.7 2.1 convert_element_type.104
  10.8 2.2 multiply_reduce_fusion.3
  16.9 29.3 %start.1 = (bf16[640,768]{1,0:T(8,128)(2,1)}, bf16[640,768]{1,0:T(8,128)(2,1)}, bf16[640,768]{1,0:T(8,128)(2,1)}, bf16[8,96,576]{2,1,0:T(8,128)(2,1)}, bf16[8,96,192]{2,1,0:T(8,128)(2,1)}) custom-call(bf16[640,768]{1,0:T(8,128)(2,1)} %multiply_convert_fusion.1.x, bf16[96,576]{1,0:T(8,128)(2,1)} %copy.37.qkv, bf16[96,192]{1,0:T(8,128)(2,1)} %convert_element_type.108.wo), custom_call_target="tpu_custom_call" | custom-call | bytes 100000000 | tf_op jit(solution)/shard_map/start/pallas_call | solution.py:703
  46.9 1.3 collective-permute-start.2
  48.5 2.1 convert_element_type.113
  51.3 4.0 %fusion.5 = (bf16[640,768]{1,0:T(8,128)(2,1)}, f32[640,768]{1,0:T(8,128)}) fusion(f32[640,1536]{1,0:T(8,128)S(1)} %convert_element_type.113, f32[]{:T(128)} %bitcast.6, f32[]{:T(128)} %bitcast.5), kind=kLoop, calls=%fused_computation.51 | loop fusion | flops 1966080 | bytes 6881288 | tf_op jit(solution)/shard_map/convert_element_type | solution.py:843
  55.8 1.8 convolution_convert_fusion.6.refs_1_
  57.6 1.8 convolution_convert_fusion.7.refs_0_
  59.5 1.9 convolution_convert_fusion.4.refs_3_
  61.3 1.8 convolution_convert_fusion.5.refs_2_
  63.2 31.0 %attn_fwd.1 = (bf16[4,640,192]{2,1,0:T(8,128)(2,1)}, f32[192,2560]{1,0:T(8,128)}, f32[8,2560]{1,0:T(8,128)}) custom-call(s32[1,5]{1,0:T(1,128)} %len_ref.3, s32[1]{0:T(128)} %bitcast.2.me_ref, bf16[640,576]{1,0:T(8,128)(2,1)} %convolution_convert_fusion.7.refs_0_, bf16[640,576]{1,0:T(8,128)(2,1)} %convolution_convert_fusion.6.refs_1_, ...), custom_call_target="tpu_custom_call" | custom-call | flops 2013265920 | bytes 5898240 | tf_op jit(solution)/shard_map/attn_fwd/pallas_call | solution.py:146
  94.2 2.4 slice_bitcast_fusion.7
  96.6 1.6 collective-permute-start.5
  98.2 1.5 fusion.4
  100.3 6.9 %collective-permute-done.5 = bf16[640,192]{1,0:T(8,128)(2,1)S(1)} collective-permute-done((bf16[640,192]{1,0:T(8,128)(2,1)S(1)}, bf16[640,192]{1,0:T(8,128)(2,1)S(1)}, u32[]{:S(2)}, u32[]{:S(2)}) %collective-permute-start.5) | collective-permute-done | bytes 245792 | tf_op jit(solution)/shard_map/ppermute | solution.py:575
  108.5 4.8 %collective-permute-done.6 = bf16[640,192]{1,0:T(8,128)(2,1)S(1)} collective-permute-done((bf16[640,192]{1,0:T(8,128)(2,1)S(1)}, bf16[640,192]{1,0:T(8,128)(2,1)S(1)}, u32[]{:S(2)}, u32[]{:S(2)}) %collective-permute-start.6) | collective-permute-done | bytes 245792 | tf_op jit(solution)/shard_map/ppermute | solution.py:575
  114.3 1.4 copy-done.4
  116.2 1.6 collective-permute-start.7
  117.8 10.7 %ffn_rows.4 = (bf16[640,768]{1,0:T(8,128)(2,1)}, bf16[640,768]{1,0:T(8,128)(2,1)}, bf16[640,768]{1,0:T(8,128)(2,1)}, f32[640,768]{1,0:T(8,128)}, bf16[640,768]{1,0:T(8,128)(2,1)}) custom-call(bf16[640,768]{1,0:T(8,128)(2,1)} %copy-done.31, bf16[640,768]{1,0:T(8,128)(2,1)} %get-tuple-element.86.g_ref.refs_4_, ...), custom_call_target="tpu_custom_call" | custom-call | flops 4529848320 | bytes 10420224 | tf_op jit(solution)/shard_map/ffn_rows/pallas_call | solution.py:372
  128.5 10.6 %ffn_rows.5 = (bf16[640,768]{1,0:T(8,128)(2,1)}, bf16[640,768]{1,0:T(8,128)(2,1)}, bf16[640,768]{1,0:T(8,128)(2,1)}, f32[640,768]{1,0:T(8,128)}, bf16[640,768]{1,0:T(8,128)(2,1)}) custom-call(bf16[640,768]{1,0:T(8,128)(2,1)} %collective-permute-done.8.x_ref.refs_1_, bf16[640,768]{1,0:T(8,128)(2,1)} %collective-permute-done.9.g_ref.refs_5_, ...), custom_call_target="tpu_custom_call" | custom-call | flops 4529848320 | bytes 10420224 | tf_op jit(solution)/shard_map/ffn_rows/pallas_call | solution.py:372
  140.2 2.8 collective-permute-done.10.x_ref.refs_3_
  144.0 10.9 %ffn_rows.7 = (bf16[640,768]{1,0:T(8,128)(2,1)}, bf16[640,768]{1,0:T(8,128)(2,1)}, bf16[640,768]{1,0:T(8,128)(2,1)}, f32[640,768]{1,0:T(8,128)}, bf16[640,768]{1,0:T(8,128)(2,1)}) custom-call(bf16[640,768]{1,0:T(8,128)(2,1)} %copy-done.47, bf16[640,768]{1,0:T(8,128)(2,1)} %collective-permute-done.11.g_ref.refs_7_, ...), custom_call_target="tpu_custom_call" | custom-call | flops 4529848320 | bytes 10420224 | tf_op jit(solution)/shard_map/ffn_rows/pallas_call | solution.py:372
  155.5 10.6 %ffn_rows.6 = (bf16[640,768]{1,0:T(8,128)(2,1)}, bf16[640,768]{1,0:T(8,128)(2,1)}, bf16[640,768]{1,0:T(8,128)(2,1)}, f32[640,768]{1,0:T(8,128)}, bf16[640,768]{1,0:T(8,128)(2,1)}) custom-call(bf16[640,768]{1,0:T(8,128)(2,1)} %collective-permute-done.7.x_ref.refs_2_, bf16[640,768]{1,0:T(8,128)(2,1)} %collective-permute-done.g_ref.refs_6_, ...), custom_call_target="tpu_custom_call" | custom-call | flops 4529848320 | bytes 10420224 | tf_op jit(solution)/shard_map/ffn_rows/pallas_call | solution.py:372
  166.1 2.7 add_convert_fusion.3
  168.8 1.6 collective-permute-start.15
  170.4 24.5 %wgrad.1 = bf16[768,2304]{1,0:T(8,128)(2,1)} custom-call(bf16[640,768]{1,0:T(8,128)(2,1)} %copy-done.31, bf16[640,768]{1,0:T(8,128)(2,1)} %collective-permute-done.8.x_ref.refs_1_, bf16[640,768]{1,0:T(8,128)(2,1)} %collective-permute-done.7.x_ref.refs_2_, bf16[640,768]{1,0:T(8,128)(2,1)} %copy-done.47, bf16[640,768]{1,0:T(8,128)(2,1)} %get-tuple-element.86.g_ref.refs_4_, ...), custom_call_target="tpu_custom_call" | custom-call | flops 9059696640 | bytes 23199744 | tf_op jit(solution)/shard_map/wgrad/pallas_call | solution.py:445
  195.8 7.8 %middle_back.1 = (f32[640,768]{1,0:T(8,128)}, bf16[640,768]{1,0:T(8,128)(2,1)}, bf16[640,192]{1,0:T(8,128)(2,1)}, bf16[640,192]{1,0:T(8,128)(2,1)}, bf16[640,192...) custom-call(bf16[640,768]{1,0:T(8,128)(2,1)} %get-tuple-element.95.share, bf16[640,768]{1,0:T(8,128)(2,1)} %copy-done.32, ...), custom_call_target="tpu_custom_call" | custom-call | flops 754974720 | bytes 10813440 | tf_op jit(solution)/shard_map/middle_back/pallas_call | solution.py:502
  204.1 1.5 collective-permute-start.19
  205.9 3.4 add_convert_fusion.4
  209.7 4.8 %collective-permute-done.18.refs_6_ = bf16[640,192]{1,0:T(8,128)(2,1)S(1)} collective-permute-done((bf16[640,192]{1,0:T(8,128)(2,1)}, bf16[640,192]{1,0:T(8,128)(2,1)S(1)}, u32[]{:S(2)}, u32[]{:S(2)}) %collective-permute-start.18) | collective-permute-done | bytes 245792 | tf_op jit(solution)/shard_map/ppermute | solution.py:575
  214.5 6.1 %collective-permute-done.19.refs_7_ = bf16[640,192]{1,0:T(8,128)(2,1)S(1)} collective-permute-done((bf16[640,192]{1,0:T(8,128)(2,1)}, bf16[640,192]{1,0:T(8,128)(2,1)S(1)}, u32[]{:S(2)}, u32[]{:S(2)}) %collective-permute-start.19) | collective-permute-done | bytes 245792 | tf_op jit(solution)/shard_map/ppermute | solution.py:575
  227.4 31.9 %attn_bwd.1 = bf16[4,640,576]{2,1,0:T(8,128)(2,1)} custom-call(s32[1,5]{1,0:T(1,128)} %len_ref.3, s32[1]{0:T(128)} %bitcast.2.me_ref, bf16[640,576]{1,0:T(8,128)(2,1)} %convolution_convert_fusion.7.refs_0_, bf16[640,576]{1,0:T(8,128)(2,1)} %convolution_convert_fusion.6.refs_1_, bf16[640,576]{1,0:T(8,128)(2,1)} %convolution_convert_fusion.5.refs_2_, ...), custom_call_target="tpu_custom_call" | custom-call | flops 5033164800 | bytes 9830400 | tf_op jit(solution)/shard_map/attn_bwd/pallas_call | solution.py:290
  259.3 1.7 fusion.3
  261.1 2.3 convolution_convert_fusion.2
  265.2 1.3 collective-permute-done.23
  273.6 1.6 copy.48
  275.3 4.8 %add_convert_fusion.1 = (bf16[640,768]{1,0:T(8,128)(2,1)S(1)}, f32[640,768]{1,0:T(8,128)S(1)}) fusion(f32[640,768]{1,0:T(8,128)S(1)} %get-tuple-element.193, f32[]{:T(128)} %bitcast.5, f32[640,768]{1,0:T(8,128)} %copy-done.4, bf16[640,768]{1,0:T(8,128)(2,1)} %collective-permute-done.13, f32[640,768]{1,0:T(8,128)} %get-tuple-element.139, ...), kind=kLoop, calls=%fused_computation.2 | loop fusion | flops 3932160 | bytes 11796484 | tf_op jit(solution)/shard_map/convert
  280.1 2.2 collective-permute-done.25.got_a
  283.4 2.6 multiply_reduce_fusion.1
  286.1 1.4 pad_maximum_fusion
  288.6 2.0 convolution_convert_fusion.share
  291.3 9.8 %collective-permute-done.24.got_b = bf16[320,768]{1,0:T(8,128)(2,1)S(1)} collective-permute-done((bf16[320,768]{1,0:T(8,128)(2,1)S(1)}, bf16[320,768]{1,0:T(8,128)(2,1)S(1)}, u32[]{:S(2)}, u32[]{:S(2)}) %collective-permute-start.24) | collective-permute-done | bytes 491552 | tf_op jit(solution)/shard_map/ppermute | solution.py:575
  302.2 8.0 %input_back.1 = (f32[640,1536]{1,0:T(8,128)}, f32[8,768]{1,0:T(8,128)}) custom-call(bf16[640,768]{1,0:T(8,128)(2,1)} %convolution_convert_fusion.share, bf16[640,768]{1,0:T(8,128)(2,1)} %copy-done.33, bf16[320,768]{1,0:T(8,128)(2,1)} %collective-permute-done.25.got_a, bf16[320,768]{1,0:T(8,128)(2,1)} %copy-done.35, bf16[640,1536]{1,0:T(8,128)(2,1)} %inputs.1, ...), custom_call_target="tpu_custom_call" | custom-call | flops 29491200 | bytes 14745600 | tf_op jit(solution)/shard_map/input_back/pallas_call | solution.py:550
  310.2 13.0 %end.1 = f32[8,768]{1,0:T(8,128)} custom-call(f32[8,768]{1,0:T(8,128)} %get-tuple-element.151.mine), custom_call_target="tpu_custom_call" | custom-call | bytes 30000000 | tf_op jit(solution)/shard_map/end/pallas_call | solution.py:796
  325.9 1.4 slice_reduce_fusion.1
  327.3 1.4 slice_reduce_fusion.2
  328.7 12.0 %reduce-scatter.7.cloned.1.call-done = bf16[96,768]{1,0:T(8,128)(2,1)} async-done(((bf16[768,768]{1,0:T(8,128)(2,1)}), bf16[96,768]{1,0:T(8,128)(2,1)}) %reduce-scatter.7.cloned.1.call-update) | async-done | bytes 147472
  (198 shorter events, 40.2 us)
Async XLA Ops:
  7.2 110.7 %all-gather.2.cloned.1.call-start = ((), (), s32[]{:S(2)}) async-start(), calls=%async_computation.2 | async-start | bytes 3981312 | tf_op jit(solution)/shard_map/all_gather | solution.py:835
  46.3 227.4 %reduce-scatter.5.cloned.1.call-start = ((), (), s32[]{:S(2)}) async-start(), calls=%async_computation.3 | async-start | bytes 3981312 | tf_op jit(solution)/shard_map/reduce_scatter | solution.py:863
  46.3 47.8 %collective-permute-start.1 = (bf16[768,192]{1,0:T(8,128)(2,1)}, bf16[768,192]{1,0:T(8,128)(2,1)S(1)}, u32[]{:S(2)}, u32[]{:S(2)}) collective-permute-start(bf16[768,192]{1,0:T(8,128)(2,1)} %bitcast.70), channel_id=1, source_target_pairs={{0,2},{1,3},{2,0},{3,1},{4,6},{5,7},{6,4},{7,5},{8,10},{9,11},{10,... | collective-permute-start | bytes 884744 | tf_op jit(solution)/shard_map/ppermute | solution.py:575
  46.9 47.3 %collective-permute-start.2 = (bf16[768,192]{1,0:T(8,128)(2,1)}, bf16[768,192]{1,0:T(8,128)(2,1)S(1)}, u32[]{:S(2)}, u32[]{:S(2)}) collective-permute-start(bf16[768,192]{1,0:T(8,128)(2,1)} %bitcast.71), channel_id=1, source_target_pairs={{0,3},{1,2},{2,1},{3,0},{4,7},{5,6},{6,5},{7,4},{8,11},{9,10},{10,... | collective-permute-start | bytes 884744 | tf_op jit(solution)/shard_map/ppermute | solution.py:575
  48.2 59.5 %collective-permute-start.4 = (bf16[768,192]{1,0:T(8,128)(2,1)}, bf16[768,192]{1,0:T(8,128)(2,1)S(1)}, u32[]{:S(2)}, u32[]{:S(2)}) collective-permute-start(bf16[768,192]{1,0:T(8,128)(2,1)} %bitcast.72), channel_id=1, source_target_pairs={{0,1},{1,0},{2,3},{3,2},{4,5},{5,4},{6,7},{7,6},{8,9},{9,8},{10,11... | collective-permute-start | bytes 884744 | tf_op jit(solution)/shard_map/ppermute | solution.py:575
  50.6 4.7 %copy-start.2 = (f32[640,1536]{1,0:T(8,128)}, f32[640,1536]{1,0:T(8,128)S(1)}, u32[]{:S(2)}) copy-start(f32[640,1536]{1,0:T(8,128)S(1)} %convert_element_type.113) | copy-start | bytes 11796484
  55.3 38.9 %collective-permute-start = (bf16[640,768]{1,0:T(8,128)(2,1)}, bf16[640,768]{1,0:T(8,128)(2,1)}, u32[]{:S(2)}, u32[]{:S(2)}) collective-permute-start(bf16[640,768]{1,0:T(8,128)(2,1)} %get-tuple-element.86.g_ref.refs_4_), channel_id=1, source_target_pairs={{0,2},{1,3},{2,0},{3,1},{4,6},{5,7},{6,4},{7,5},{8,10},{9,11},{10,... | collective-permute-start | bytes 2949128 | tf_op jit(solution)/shard_map/ppermute | solution.py:575
  55.7 72.8 %collective-permute-start.9 = (bf16[640,768]{1,0:T(8,128)(2,1)}, bf16[640,768]{1,0:T(8,128)(2,1)}, u32[]{:S(2)}, u32[]{:S(2)}) collective-permute-start(bf16[640,768]{1,0:T(8,128)(2,1)} %get-tuple-element.86.g_ref.refs_4_), channel_id=1, source_target_pairs={{0,1},{1,0},{2,3},{3,2},{4,5},{5,4},{6,7},{7,6},{8,9},{9,8},{10,11... | collective-permute-start | bytes 2949128 | tf_op jit(solution)/shard_map/ppermute | solution.py:575
  94.2 13.0 %copy-start.16 = (bf16[768,192]{1,0:T(8,128)(2,1)}, bf16[768,192]{1,0:T(8,128)(2,1)S(1)}, u32[]{:S(2)}) copy-start(bf16[768,192]{1,0:T(8,128)(2,1)S(1)} %collective-permute-done.1.refs_2_) | copy-start | bytes 884740
  94.2 19.1 %copy-start.14 = (bf16[768,192]{1,0:T(8,128)(2,1)}, bf16[768,192]{1,0:T(8,128)(2,1)S(1)}, u32[]{:S(2)}) copy-start(bf16[768,192]{1,0:T(8,128)(2,1)S(1)} %collective-permute-done.2.refs_3_) | copy-start | bytes 884740
  96.6 10.6 %collective-permute-start.5 = (bf16[640,192]{1,0:T(8,128)(2,1)S(1)}, bf16[640,192]{1,0:T(8,128)(2,1)S(1)}, u32[]{:S(2)}, u32[]{:S(2)}) collective-permute-start(bf16[640,192]{1,0:T(8,128)(2,1)S(1)} %get-tuple-element.201), channel_id=1, source_target_pairs={{0,2},{1,3},{2,0},{3,1},{4,6},{5,7},{6,4},{7,5},{8,10},{9,11},{10,... | collective-permute-start | bytes 737288 | tf_op jit(solution)/shard_map/ppermute | solution.py:575
  99.7 8.0 %collective-permute-start.3 = (bf16[640,192]{1,0:T(8,128)(2,1)S(1)}, bf16[640,192]{1,0:T(8,128)(2,1)S(1)}, u32[]{:S(2)}, u32[]{:S(2)}) collective-permute-start(bf16[640,192]{1,0:T(8,128)(2,1)S(1)} %get-tuple-element.202), channel_id=1, source_target_pairs={{0,1},{1,0},{2,3},{3,2},{4,5},{5,4},{6,7},{7,6},{8,9},{9,8},{10,11... | collective-permute-start | bytes 737288 | tf_op jit(solution)/shard_map/ppermute | solution.py:575
  99.9 13.4 %collective-permute-start.6 = (bf16[640,192]{1,0:T(8,128)(2,1)S(1)}, bf16[640,192]{1,0:T(8,128)(2,1)S(1)}, u32[]{:S(2)}, u32[]{:S(2)}) collective-permute-start(bf16[640,192]{1,0:T(8,128)(2,1)S(1)} %get-tuple-element.200), channel_id=1, source_target_pairs={{0,3},{1,2},{2,1},{3,0},{4,7},{5,6},{6,5},{7,4},{8,11},{9,10},{10,... | collective-permute-start | bytes 737288 | tf_op jit(solution)/shard_map/ppermute | solution.py:575
  107.7 6.6 %copy-start.17 = (bf16[768,192]{1,0:T(8,128)(2,1)}, bf16[768,192]{1,0:T(8,128)(2,1)S(1)}, u32[]{:S(2)}) copy-start(bf16[768,192]{1,0:T(8,128)(2,1)S(1)} %collective-permute-done.4.refs_1_) | copy-start | bytes 884740
  108.5 7.2 %copy-start.40 = (f32[768]{0:T(1024)S(1)}, f32[768]{0:T(1024)}, u32[]{:S(2)}) copy-start(f32[768]{0:T(1024)} %param.18) | copy-start | bytes 9220
  115.9 12.6 %collective-permute-start.8 = (bf16[640,768]{1,0:T(8,128)(2,1)S(1)}, bf16[640,768]{1,0:T(8,128)(2,1)}, u32[]{:S(2)}, u32[]{:S(2)}) collective-permute-start(bf16[640,768]{1,0:T(8,128)(2,1)S(1)} %multiply_convert_fusion.x_ref.refs_0_), channel_id=1, source_target_pairs={{0,1},{1,0},{2,3},{3,2},{4,5},{5,4},{6,7},{7,6},{8,9},{9,8},{10,11... | collective-permute-start | bytes 2949128 | tf_op jit(solution)/shard_map/ppermute | solution.py:575
  116.2 24.0 %collective-permute-start.7 = (bf16[640,768]{1,0:T(8,128)(2,1)S(1)}, bf16[640,768]{1,0:T(8,128)(2,1)}, u32[]{:S(2)}, u32[]{:S(2)}) collective-permute-start(bf16[640,768]{1,0:T(8,128)(2,1)S(1)} %multiply_convert_fusion.x_ref.refs_0_), channel_id=1, source_target_pairs={{0,2},{1,3},{2,0},{3,1},{4,6},{5,7},{6,4},{7,5},{8,10},{9,11},{10,... | collective-permute-start | bytes 2949128 | tf_op jit(solution)/shard_map/ppermute | solution.py:575
  117.8 22.4 %collective-permute-start.11 = (bf16[640,768]{1,0:T(8,128)(2,1)}, bf16[640,768]{1,0:T(8,128)(2,1)}, u32[]{:S(2)}, u32[]{:S(2)}) collective-permute-start(bf16[640,768]{1,0:T(8,128)(2,1)} %collective-permute-done.g_ref.refs_6_), channel_id=1, source_target_pairs={{0,1},{1,0},{2,3},{3,2},{4,5},{5,4},{6,7},{7,6},{8,9},{9,8},{10,11... | collective-permute-start | bytes 2949128 | tf_op jit(solution)/shard_map/ppermute | solution.py:575
  140.2 2.8 collective-permute-start.10
  154.9 11.2 %collective-permute-start.14 = (bf16[640,768]{1,0:T(8,128)(2,1)}, bf16[640,768]{1,0:T(8,128)(2,1)}, u32[]{:S(2)}, u32[]{:S(2)}) collective-permute-start(bf16[640,768]{1,0:T(8,128)(2,1)} %get-tuple-element.97), channel_id=1, source_target_pairs={{0,1},{1,0},{2,3},{3,2},{4,5},{5,4},{6,7},{7,6},{8,9},{9,8},{10,11... | collective-permute-start | bytes 2949128 | tf_op jit(solution)/shard_map/ppermute | solution.py:575
  155.1 39.7 %collective-permute-start.16 = (bf16[640,768]{1,0:T(8,128)(2,1)}, bf16[640,768]{1,0:T(8,128)(2,1)S(1)}, u32[]{:S(2)}, u32[]{:S(2)}) collective-permute-start(bf16[640,768]{1,0:T(8,128)(2,1)} %get-tuple-element.98), channel_id=1, source_target_pairs={{0,1},{1,0},{2,3},{3,2},{4,5},{5,4},{6,7},{7,6},{8,9},{9,8},{10,11... | collective-permute-start | bytes 2949128 | tf_op jit(solution)/shard_map/ppermute | solution.py:575
  168.8 26.1 %collective-permute-start.15 = (bf16[640,768]{1,0:T(8,128)(2,1)}, bf16[640,768]{1,0:T(8,128)(2,1)}, u32[]{:S(2)}, u32[]{:S(2)}) collective-permute-start(bf16[640,768]{1,0:T(8,128)(2,1)} %add_convert_fusion.3), channel_id=1, source_target_pairs={{0,2},{1,3},{2,0},{3,1},{4,6},{5,7},{6,4},{7,5},{8,10},{9,11},{10,... | collective-permute-start | bytes 2949128 | tf_op jit(solution)/shard_map/ppermute | solution.py:575
  170.4 35.5 %collective-permute-start.12 = (f32[640,768]{1,0:T(8,128)}, f32[640,768]{1,0:T(8,128)}, u32[]{:S(2)}, u32[]{:S(2)}) collective-permute-start(f32[640,768]{1,0:T(8,128)} %get-tuple-element.94), channel_id=1, source_target_pairs={{0,1},{1,0},{2,3},{3,2},{4,5},{5,4},{6,7},{7,6},{8,9},{9,8},{10,11... | collective-permute-start | bytes 5898248 | tf_op jit(solution)/shard_map/ppermute | solution.py:575
  194.9 145.9 %reduce-scatter.7.cloned.1.call-start = ((), (), s32[]{:S(2)}) async-start(), calls=%async_computation.4 | async-start | bytes 1327104
  203.7 10.9 %collective-permute-start.18 = (bf16[640,192]{1,0:T(8,128)(2,1)}, bf16[640,192]{1,0:T(8,128)(2,1)S(1)}, u32[]{:S(2)}, u32[]{:S(2)}) collective-permute-start(bf16[640,192]{1,0:T(8,128)(2,1)} %get-tuple-element.114), channel_id=1, source_target_pairs={{0,2},{1,3},{2,0},{3,1},{4,6},{5,7},{6,4},{7,5},{8,10},{9,11},{10,... | collective-permute-start | bytes 737288 | tf_op jit(solution)/shard_map/ppermute | solution.py:575
  204.1 16.5 %collective-permute-start.19 = (bf16[640,192]{1,0:T(8,128)(2,1)}, bf16[640,192]{1,0:T(8,128)(2,1)S(1)}, u32[]{:S(2)}, u32[]{:S(2)}) collective-permute-start(bf16[640,192]{1,0:T(8,128)(2,1)} %get-tuple-element.115), channel_id=1, source_target_pairs={{0,3},{1,2},{2,1},{3,0},{4,7},{5,6},{6,5},{7,4},{8,11},{9,10},{10,... | collective-permute-start | bytes 737288 | tf_op jit(solution)/shard_map/ppermute | solution.py:575
  205.6 21.0 %collective-permute-start.17 = (bf16[640,192]{1,0:T(8,128)(2,1)}, bf16[640,192]{1,0:T(8,128)(2,1)S(1)}, u32[]{:S(2)}, u32[]{:S(2)}) collective-permute-start(bf16[640,192]{1,0:T(8,128)(2,1)} %get-tuple-element.113), channel_id=1, source_target_pairs={{0,1},{1,0},{2,3},{3,2},{4,5},{5,4},{6,7},{7,6},{8,9},{9,8},{10,11... | collective-permute-start | bytes 737288 | tf_op jit(solution)/shard_map/ppermute | solution.py:575
  205.9 14.8 %copy-start.5 = (bf16[640,768]{1,0:T(8,128)(2,1)S(1)}, bf16[640,768]{1,0:T(8,128)(2,1)}, u32[]{:S(2)}) copy-start(bf16[640,768]{1,0:T(8,128)(2,1)} %get-tuple-element.119) | copy-start | bytes 2949124
  205.9 14.8 %copy-start.24 = (bf16[640,192]{1,0:T(8,128)(2,1)S(1)}, bf16[640,192]{1,0:T(8,128)(2,1)}, u32[]{:S(2)}) copy-start(bf16[640,192]{1,0:T(8,128)(2,1)} %copy-done.23) | copy-start | bytes 737284
  205.9 17.1 %copy-start.22 = (bf16[640,192]{1,0:T(8,128)(2,1)S(1)}, bf16[640,192]{1,0:T(8,128)(2,1)}, u32[]{:S(2)}) copy-start(bf16[640,192]{1,0:T(8,128)(2,1)} %copy-done.21) | copy-start | bytes 737284
  209.3 15.2 %copy-start.19 = (bf16[640,192]{1,0:T(8,128)(2,1)S(1)}, bf16[640,192]{1,0:T(8,128)(2,1)}, u32[]{:S(2)}) copy-start(bf16[640,192]{1,0:T(8,128)(2,1)} %copy-done.18) | copy-start | bytes 737284
  209.3 51.8 %collective-permute-start.13 = (bf16[640,768]{1,0:T(8,128)(2,1)}, bf16[640,768]{1,0:T(8,128)(2,1)}, u32[]{:S(2)}, u32[]{:S(2)}) collective-permute-start(bf16[640,768]{1,0:T(8,128)(2,1)} %add_convert_fusion.4), channel_id=1, source_target_pairs={{0,2},{1,3},{2,0},{3,1},{4,6},{5,7},{6,4},{7,5},{8,10},{9,11},{10,... | collective-permute-start | bytes 2949128 | tf_op jit(solution)/shard_map/ppermute | solution.py:575
  214.5 11.1 %copy-start.48 = (bf16[640,192]{1,0:T(8,128)(2,1)}, bf16[640,192]{1,0:T(8,128)(2,1)S(1)}, u32[]{:S(2)}) copy-start(bf16[640,192]{1,0:T(8,128)(2,1)S(1)} %collective-permute-done.18.refs_6_) | copy-start | bytes 737284
  220.7 5.0 %copy-start.49 = (bf16[640,192]{1,0:T(8,128)(2,1)}, bf16[640,192]{1,0:T(8,128)(2,1)S(1)}, u32[]{:S(2)}) copy-start(bf16[640,192]{1,0:T(8,128)(2,1)S(1)} %collective-permute-done.19.refs_7_) | copy-start | bytes 737284
  221.8 37.5 %collective-permute-start.20 = (bf16[768,192]{0,1:T(8,128)(2,1)}, bf16[768,192]{0,1:T(8,128)(2,1)}, u32[]{:S(2)}, u32[]{:S(2)}) collective-permute-start(bf16[768,192]{0,1:T(8,128)(2,1)} %convolution_convert_fusion.10), channel_id=1, source_target_pairs={{0,1},{1,0},{2,3},{3,2},{4,5},{5,4},{6,7},{7,6},{8,9},{9,8},{10,11... | collective-permute-start | bytes 884744 | tf_op jit(solution)/shard_map/ppermute | solution.py:575
  224.1 35.2 %collective-permute-start.21 = (bf16[768,192]{0,1:T(8,128)(2,1)}, bf16[768,192]{0,1:T(8,128)(2,1)}, u32[]{:S(2)}, u32[]{:S(2)}) collective-permute-start(bf16[768,192]{0,1:T(8,128)(2,1)} %convolution_convert_fusion.9), channel_id=1, source_target_pairs={{0,2},{1,3},{2,0},{3,1},{4,6},{5,7},{6,4},{7,5},{8,10},{9,11},{10,... | collective-permute-start | bytes 884744 | tf_op jit(solution)/shard_map/ppermute | solution.py:575
  225.7 33.7 %collective-permute-start.22 = (bf16[768,192]{0,1:T(8,128)(2,1)}, bf16[768,192]{0,1:T(8,128)(2,1)}, u32[]{:S(2)}, u32[]{:S(2)}) collective-permute-start(bf16[768,192]{0,1:T(8,128)(2,1)} %convolution_convert_fusion.8), channel_id=1, source_target_pairs={{0,3},{1,2},{2,1},{3,0},{4,7},{5,6},{6,5},{7,4},{8,11},{9,10},{10,... | collective-permute-start | bytes 884744 | tf_op jit(solution)/shard_map/ppermute | solution.py:575
  227.4 32.0 %copy-start.20 = (bf16[640,192]{1,0:T(8,128)(2,1)S(1)}, bf16[640,192]{1,0:T(8,128)(2,1)}, u32[]{:S(2)}) copy-start(bf16[640,192]{1,0:T(8,128)(2,1)} %get-tuple-element.120) | copy-start | bytes 737284
  263.4 3.1 collective-permute-start.23
  264.9 10.4 %collective-permute-start.27 = (f32[640,768]{1,0:T(8,128)}, f32[640,768]{1,0:T(8,128)}, u32[]{:S(2)}, u32[]{:S(2)}) collective-permute-start(f32[640,768]{1,0:T(8,128)} %get-tuple-element.140), channel_id=1, source_target_pairs={{0,1},{1,0},{2,3},{3,2},{4,5},{5,4},{6,7},{7,6},{8,9},{9,8},{10,11... | collective-permute-start | bytes 5898248 | tf_op jit(solution)/shard_map/ppermute | solution.py:575
  265.2 4.8 %copy-start.8 = (bf16[640,576]{1,0:T(8,128)(2,1)}, bf16[640,576]{1,0:T(8,128)(2,1)S(1)}, u32[]{:S(2)}) copy-start(bf16[640,576]{1,0:T(8,128)(2,1)S(1)} %get-tuple-element.143) | copy-start | bytes 2211844
  268.5 13.8 %collective-permute-start.25 = (bf16[320,768]{1,0:T(8,128)(2,1)}, bf16[320,768]{1,0:T(8,128)(2,1)}, u32[]{:S(2)}, u32[]{:S(2)}) collective-permute-start(bf16[320,768]{1,0:T(8,128)(2,1)} %get-tuple-element.203), channel_id=1, source_target_pairs={{0,2},{1,3},{2,0},{3,1},{4,6},{5,7},{6,4},{7,5},{8,10},{9,11},{10,... | collective-permute-start | bytes 1474568 | tf_op jit(solution)/shard_map/ppermute | solution.py:575
  275.3 7.1 %copy-start.11 = (bf16[640,576]{1,0:T(8,128)(2,1)S(1)}, bf16[640,576]{1,0:T(8,128)(2,1)}, u32[]{:S(2)}) copy-start(bf16[640,576]{1,0:T(8,128)(2,1)} %copy-done.10) | copy-start | bytes 2211844
  275.3 7.0 %copy-start.46 = (bf16[8,96,576]{2,1,0:T(8,128)(2,1)S(1)}, bf16[8,96,576]{2,1,0:T(8,128)(2,1)}, u32[]{:S(2)}) copy-start(bf16[8,96,576]{2,1,0:T(8,128)(2,1)} %get-tuple-element.81) | copy-start | bytes 2654212
  275.3 8.1 %copy-start.1 = (f32[640,1536]{1,0:T(8,128)S(1)}, f32[640,1536]{1,0:T(8,128)}, u32[]{:S(2)}) copy-start(f32[640,1536]{1,0:T(8,128)} %copy-done) | copy-start | bytes 11796484
  275.3 8.1 %copy-start.3 = (f32[640,1536]{1,0:T(8,128)S(1)}, f32[640,1536]{1,0:T(8,128)}, u32[]{:S(2)}) copy-start(f32[640,1536]{1,0:T(8,128)} %copy-done.2) | copy-start | bytes 11796484
  283.3 17.8 %collective-permute-start.26 = (bf16[640,768]{1,0:T(8,128)(2,1)S(1)}, bf16[640,768]{1,0:T(8,128)(2,1)S(1)}, u32[]{:S(2)}, u32[]{:S(2)}) collective-permute-start(bf16[640,768]{1,0:T(8,128)(2,1)S(1)} %convolution_convert_fusion.1), channel_id=1, source_target_pairs={{0,1},{1,0},{2,3},{3,2},{4,5},{5,4},{6,7},{7,6},{8,9},{9,8},{10,11... | collective-permute-start | bytes 2949128 | tf_op jit(solution)/shard_map/ppermute | solution.py:575
  287.5 13.6 %collective-permute-start.24 = (bf16[320,768]{1,0:T(8,128)(2,1)S(1)}, bf16[320,768]{1,0:T(8,128)(2,1)S(1)}, u32[]{:S(2)}, u32[]{:S(2)}) collective-permute-start(bf16[320,768]{1,0:T(8,128)(2,1)S(1)} %copy-done.36), channel_id=1, source_target_pairs={{0,2},{1,3},{2,0},{3,1},{4,6},{5,7},{6,4},{7,5},{8,10},{9,11},{10,... | collective-permute-start | bytes 1474568 | tf_op jit(solution)/shard_map/ppermute | solution.py:575
  (34 other events, 73.7 us)
Sparse Core Ops, SparseCore 0:
  46.4 63.8 all-gather.1
  195.0 77.9 reduce-scatter.4
  276.4 64.2 reduce-scatter.6

commit v3 on v2

--- a/solution.py
+++ b/solution.py
@@ -893,20 +893,20 @@
     *late, far = lax.optimization_barrier((*grad_proj, *normed_attn, weight_out, far))
     weight_qkv = sum(dot_tn(x, g) for x, g in zip(late[4:8], late[:4]))
     last = jnp.concatenate([weight_qkv, late[8]], axis=1).astype(bf16)
-    last, weight_ffn = lax.optimization_barrier((last, weight_ffn))
-    summed_last = lax.psum_scatter(last, "dp", scatter_dimension=0, tiled=True)
-    got[0], *late = lax.optimization_barrier((got[0], *late[:2]))
+    last, got[0] = lax.optimization_barrier((last.reshape(lax.axis_size("dp"), shard, -1), got[0]))
+    last = lax.all_to_all(last, "dp", split_axis=0, concat_axis=0, tiled=True)
+    got[0], weight_ffn, *late = lax.optimization_barrier((got[0], weight_ffn, *late[:2]))
     near = [dot_nt(g, qkv_all).astype(bf16) for g in late]
     came = swap(near[1], 1)
-    got[1], last, came, early, block_output = lax.optimization_barrier((got[1], last, came, early, block_output))
+    got[1], came, early, block_output = lax.optimization_barrier((got[1], came, early, block_output))
     grad_input, small = input_back(
         near[0], came, got, block_input, cotangent, grad_middle, early, gain_attn, mix_matrix, correct_gain
     )
     weight_ffn = weight_ffn.astype(f32)
     sum_gate_up = weight_ffn[:, : 2 * units].reshape(shard, 2, units)
     sum_down = weight_ffn[:, 2 * units :]
-    small = end(small)
-    last = summed_last.astype(f32)
+    small, last = lax.optimization_barrier((end(small), last))
+    last = last.astype(f32).sum(axis=0)
     sum_qkv = last[:, : 3 * feats].reshape(shard, 3, feats)
     sum_out = last[:, 3 * feats :]
     return (

time: 358 us -> 361 us (level)
  waiting for transfers between devices: 51.9 us -> 39.3 us
  starting transfers between devices: 15.9 us -> 25.4 us
  matrix products: 26 us -> 31.3 us
  other arithmetic: 31.3 us -> 35.5 us
    unnamed x4 -> x2, waiting for transfers between devices: 12.1 us -> 0.03 us
    all_to_all x0 -> x1, starting transfers between devices: none -> 8.65 us  [local(): last = lax.all_to_all(last, 'dp', split_axis=0, concat_axis=0, tiled=True)]
    unnamed x108 -> x96, local copies, waits for them, and re-layouts: 9.1 us -> 5.4 us
    dot_general x8, matrix products: 9.51 us -> 13.2 us  [dot_nt(): lax.dot_general(a, b, (((1,), (1,)), ((), ())), preferred_element_type=jn...]
  transfers between devices with their start and end apart: 31 -> 31, of which waited for: 10 -> 9; matrix products, arithmetic and copies ran while one was open for 18% -> 19% of each run, Pallas kernels for 42% -> 42%
where the time goes in v3:
time: 361 us; the launch traced here: 356 us
  Pallas kernels  190 us (53%)
  waiting for transfers between devices  39.3 us (11%)
  other arithmetic  35.5 us (10%)
  matrix products  31.3 us (9%)
  starting transfers between devices  25.4 us (7%)
  local copies, waits for them, and re-layouts  20.2 us (6%)
  between operations  14.9 us (4%)
    pallas_call x4, Pallas kernels, ffn_rows(): pl.pallas_call(functools.partial(ffn_kernel, tile), out_shape=(wide, wide...  42.7 us
    ppermute x28, waiting for transfers between devices, swap(): return lax.ppermute(array, 'tensor', [(i, i ^ bit) for i in range(count)])  39.2 us
    pallas_call x1, Pallas kernels, attn_bwd(): pl.pallas_call(functools.partial(bwd_kernel, heads, parts), out_shape=jax...  32 us
    pallas_call x1, Pallas kernels, attn_fwd(): pl.pallas_call(functools.partial(fwd_kernel, heads, parts), out_shape=(ja...  31 us
    pallas_call x1, Pallas kernels, start(): pl.pallas_call(functools.partial(start_kernel, count, chunks), out_shape=...  29.3 us
    pallas_call x1, Pallas kernels, wgrad(): pl.pallas_call(functools.partial(wgrad_kernel, parts, n), out_shape=jax.S...  24.5 us
    ppermute x28, starting transfers between devices, swap(): return lax.ppermute(array, 'tensor', [(i, i ^ bit) for i in range(count)])  16.7 us
    pallas_call x1, Pallas kernels, end(): pl.pallas_call(functools.partial(end_kernel, count), out_shape=jax.ShapeD...  14.5 us
  transfers between devices with their start and end apart: 31, of which 9 were waited for; matrix products, arithmetic and copies ran while one was open for 19% of the time, Pallas kernels for 42%

profile of v3, /device:TPU:0, one launch (start us, length us, event | category | flops | bytes accessed | tf_op | source)
XLA Modules:
  0.0 356.3 jit_solution(8584190161921978065)
XLA Ops:
  7.2 1.4 fusion.7
  8.6 2.1 convert_element_type.105
  10.8 2.2 multiply_reduce_fusion.3
  16.9 29.3 %start.1 = (bf16[640,768]{1,0:T(8,128)(2,1)}, bf16[640,768]{1,0:T(8,128)(2,1)}, bf16[640,768]{1,0:T(8,128)(2,1)}, bf16[8,96,576]{2,1,0:T(8,128)(2,1)}, bf16[8,96,192]{2,1,0:T(8,128)(2,1)}) custom-call(bf16[640,768]{1,0:T(8,128)(2,1)} %multiply_convert_fusion.1.x, bf16[96,576]{1,0:T(8,128)(2,1)} %copy.37.qkv, bf16[96,192]{1,0:T(8,128)(2,1)} %convert_element_type.109.wo), custom_call_target="tpu_custom_call" | custom-call | bytes 100000000 | tf_op jit(solution)/shard_map/start/pallas_call | solution.py:703
  48.5 2.1 convert_element_type.114
  51.2 4.0 %fusion.5 = (bf16[640,768]{1,0:T(8,128)(2,1)}, f32[640,768]{1,0:T(8,128)}) fusion(f32[640,1536]{1,0:T(8,128)S(1)} %convert_element_type.114, f32[]{:T(128)} %bitcast.6, f32[]{:T(128)} %bitcast.5), kind=kLoop, calls=%fused_computation.52 | loop fusion | flops 1966080 | bytes 6881288 | tf_op jit(solution)/shard_map/convert_element_type | solution.py:843
  55.7 1.9 convolution_convert_fusion.6.refs_1_
  57.5 1.9 convolution_convert_fusion.7.refs_0_
  59.4 1.9 convolution_convert_fusion.4.refs_3_
  61.3 1.8 convolution_convert_fusion.5.refs_2_
  63.1 31.0 %attn_fwd.1 = (bf16[4,640,192]{2,1,0:T(8,128)(2,1)}, f32[192,2560]{1,0:T(8,128)}, f32[8,2560]{1,0:T(8,128)}) custom-call(s32[1,5]{1,0:T(1,128)} %len_ref.3, s32[1]{0:T(128)} %bitcast.2.me_ref, bf16[640,576]{1,0:T(8,128)(2,1)} %convolution_convert_fusion.7.refs_0_, bf16[640,576]{1,0:T(8,128)(2,1)} %convolution_convert_fusion.6.refs_1_, ...), custom_call_target="tpu_custom_call" | custom-call | flops 2013265920 | bytes 5898240 | tf_op jit(solution)/shard_map/attn_fwd/pallas_call | solution.py:146
  94.2 2.4 slice_bitcast_fusion.7
  96.6 1.6 collective-permute-start.5
  98.2 1.5 fusion.4
  100.2 6.9 %collective-permute-done.5 = bf16[640,192]{1,0:T(8,128)(2,1)S(1)} collective-permute-done((bf16[640,192]{1,0:T(8,128)(2,1)S(1)}, bf16[640,192]{1,0:T(8,128)(2,1)S(1)}, u32[]{:S(2)}, u32[]{:S(2)}) %collective-permute-start.5) | collective-permute-done | bytes 245792 | tf_op jit(solution)/shard_map/ppermute | solution.py:575
  108.5 4.8 %collective-permute-done.6 = bf16[640,192]{1,0:T(8,128)(2,1)S(1)} collective-permute-done((bf16[640,192]{1,0:T(8,128)(2,1)S(1)}, bf16[640,192]{1,0:T(8,128)(2,1)S(1)}, u32[]{:S(2)}, u32[]{:S(2)}) %collective-permute-start.6) | collective-permute-done | bytes 245792 | tf_op jit(solution)/shard_map/ppermute | solution.py:575
  114.2 1.4 copy-done.2
  116.2 1.6 collective-permute-start.7
  117.8 10.6 %ffn_rows.4 = (bf16[640,768]{1,0:T(8,128)(2,1)}, bf16[640,768]{1,0:T(8,128)(2,1)}, bf16[640,768]{1,0:T(8,128)(2,1)}, f32[640,768]{1,0:T(8,128)}, bf16[640,768]{1,0:T(8,128)(2,1)}) custom-call(bf16[640,768]{1,0:T(8,128)(2,1)} %copy-done.30, bf16[640,768]{1,0:T(8,128)(2,1)} %get-tuple-element.89.g_ref.refs_4_, ...), custom_call_target="tpu_custom_call" | custom-call | flops 4529848320 | bytes 10420224 | tf_op jit(solution)/shard_map/ffn_rows/pallas_call | solution.py:372
  128.4 10.6 %ffn_rows.5 = (bf16[640,768]{1,0:T(8,128)(2,1)}, bf16[640,768]{1,0:T(8,128)(2,1)}, bf16[640,768]{1,0:T(8,128)(2,1)}, f32[640,768]{1,0:T(8,128)}, bf16[640,768]{1,0:T(8,128)(2,1)}) custom-call(bf16[640,768]{1,0:T(8,128)(2,1)} %collective-permute-done.8.x_ref.refs_1_, bf16[640,768]{1,0:T(8,128)(2,1)} %collective-permute-done.9.g_ref.refs_5_, ...), custom_call_target="tpu_custom_call" | custom-call | flops 4529848320 | bytes 10420224 | tf_op jit(solution)/shard_map/ffn_rows/pallas_call | solution.py:372
  140.1 2.8 collective-permute-done.10.x_ref.refs_3_
  143.9 10.9 %ffn_rows.7 = (bf16[640,768]{1,0:T(8,128)(2,1)}, bf16[640,768]{1,0:T(8,128)(2,1)}, bf16[640,768]{1,0:T(8,128)(2,1)}, f32[640,768]{1,0:T(8,128)}, bf16[640,768]{1,0:T(8,128)(2,1)}) custom-call(bf16[640,768]{1,0:T(8,128)(2,1)} %copy-done.43, bf16[640,768]{1,0:T(8,128)(2,1)} %collective-permute-done.11.g_ref.refs_7_, ...), custom_call_target="tpu_custom_call" | custom-call | flops 4529848320 | bytes 10420224 | tf_op jit(solution)/shard_map/ffn_rows/pallas_call | solution.py:372
  155.4 10.7 %ffn_rows.6 = (bf16[640,768]{1,0:T(8,128)(2,1)}, bf16[640,768]{1,0:T(8,128)(2,1)}, bf16[640,768]{1,0:T(8,128)(2,1)}, f32[640,768]{1,0:T(8,128)}, bf16[640,768]{1,0:T(8,128)(2,1)}) custom-call(bf16[640,768]{1,0:T(8,128)(2,1)} %collective-permute-done.7.x_ref.refs_2_, bf16[640,768]{1,0:T(8,128)(2,1)} %collective-permute-done.g_ref.refs_6_, ...), custom_call_target="tpu_custom_call" | custom-call | flops 4529848320 | bytes 10420224 | tf_op jit(solution)/shard_map/ffn_rows/pallas_call | solution.py:372
  166.1 2.7 add_convert_fusion.3
  168.8 1.6 collective-permute-start.15
  170.3 24.5 %wgrad.1 = bf16[768,2304]{1,0:T(8,128)(2,1)} custom-call(bf16[640,768]{1,0:T(8,128)(2,1)} %copy-done.30, bf16[640,768]{1,0:T(8,128)(2,1)} %collective-permute-done.8.x_ref.refs_1_, bf16[640,768]{1,0:T(8,128)(2,1)} %collective-permute-done.7.x_ref.refs_2_, bf16[640,768]{1,0:T(8,128)(2,1)} %copy-done.43, bf16[640,768]{1,0:T(8,128)(2,1)} %get-tuple-element.89.g_ref.refs_4_, ...), custom_call_target="tpu_custom_call" | custom-call | flops 9059696640 | bytes 23199744 | tf_op jit(solution)/shard_map/wgrad/pallas_call | solution.py:445
  195.8 7.8 %middle_back.1 = (f32[640,768]{1,0:T(8,128)}, bf16[640,768]{1,0:T(8,128)(2,1)}, bf16[640,192]{1,0:T(8,128)(2,1)}, bf16[640,192]{1,0:T(8,128)(2,1)}, bf16[640,192...) custom-call(bf16[640,768]{1,0:T(8,128)(2,1)} %get-tuple-element.98.share, bf16[640,768]{1,0:T(8,128)(2,1)} %copy-done.31, ...), custom_call_target="tpu_custom_call" | custom-call | flops 754974720 | bytes 10813440 | tf_op jit(solution)/shard_map/middle_back/pallas_call | solution.py:502
  204.1 1.4 collective-permute-start.19
  205.8 3.4 add_convert_fusion.4
  209.7 4.8 %collective-permute-done.18.refs_6_ = bf16[640,192]{1,0:T(8,128)(2,1)S(1)} collective-permute-done((bf16[640,192]{1,0:T(8,128)(2,1)}, bf16[640,192]{1,0:T(8,128)(2,1)S(1)}, u32[]{:S(2)}, u32[]{:S(2)}) %collective-permute-start.18) | collective-permute-done | bytes 245792 | tf_op jit(solution)/shard_map/ppermute | solution.py:575
  214.4 6.1 %collective-permute-done.19.refs_7_ = bf16[640,192]{1,0:T(8,128)(2,1)S(1)} collective-permute-done((bf16[640,192]{1,0:T(8,128)(2,1)}, bf16[640,192]{1,0:T(8,128)(2,1)S(1)}, u32[]{:S(2)}, u32[]{:S(2)}) %collective-permute-start.19) | collective-permute-done | bytes 245792 | tf_op jit(solution)/shard_map/ppermute | solution.py:575
  227.3 32.0 %attn_bwd.1 = bf16[4,640,576]{2,1,0:T(8,128)(2,1)} custom-call(s32[1,5]{1,0:T(1,128)} %len_ref.3, s32[1]{0:T(128)} %bitcast.2.me_ref, bf16[640,576]{1,0:T(8,128)(2,1)} %convolution_convert_fusion.7.refs_0_, bf16[640,576]{1,0:T(8,128)(2,1)} %convolution_convert_fusion.6.refs_1_, bf16[640,576]{1,0:T(8,128)(2,1)} %convolution_convert_fusion.5.refs_2_, ...), custom_call_target="tpu_custom_call" | custom-call | flops 5033164800 | bytes 9830400 | tf_op jit(solution)/shard_map/attn_bwd/pallas_call | solution.py:290
  259.3 2.4 fusion.3
  261.7 2.3 convolution_convert_fusion.2
  265.3 1.8 collective-permute-done.23
  273.0 2.0 add_convert_fusion.5
  275.0 1.5 copy.42
  277.6 1.3 pad_maximum_fusion.1
  279.0 3.9 %collective-permute-done.25.got_a = bf16[320,768]{1,0:T(8,128)(2,1)} collective-permute-done((bf16[320,768]{1,0:T(8,128)(2,1)}, bf16[320,768]{1,0:T(8,128)(2,1)}, u32[]{:S(2)}, u32[]{:S(2)}) %collective-permute-start.25) | collective-permute-done | bytes 491552 | tf_op jit(solution)/shard_map/ppermute | solution.py:575
  282.9 8.6 %all-to-all-start = ((bf16[8,96,768]{2,1,0:T(8,128)(2,1)}), bf16[8,96,768]{2,1,0:T(8,128)(2,1)S(1)}, u32[]{:S(2)}, u32[]{:S(2)}) async-start(bf16[8,96,768]{2,1,0:T(8,128)(2,1)} %pad_maximum_fusion.1), calls=%async_computation.1 | async-start | bytes 2359296 | tf_op jit(solution)/shard_map/all_to_all | solution.py:897
  292.1 5.9 %add_convert_fusion.1 = (bf16[640,768]{1,0:T(8,128)(2,1)}, f32[640,768]{1,0:T(8,128)}) fusion(f32[640,768]{1,0:T(8,128)S(1)} %get-tuple-element.189, f32[]{:T(128)} %bitcast.5, f32[640,768]{1,0:T(8,128)} %copy-done.2, bf16[640,768]{1,0:T(8,128)(2,1)} %collective-permute-done.13, f32[640,768]{1,0:T(8,128)} %get-tuple-element.142, ...), kind=kLoop, calls=%fused_computation.3 | loop fusion | flops 3932160 | bytes 11796484 | tf_op jit(solution)/shard_map/convert
  298.0 3.5 convolution_convert_fusion.1
  301.5 5.9 %multiply_reduce_fusion.1 = (f32[768]{0:T(1024)S(1)}, f32[768]{0:T(1024)S(1)}, bf16[640,768]{1,0:T(8,128)(2,1)S(1)}) fusion(f32[640,768]{1,0:T(8,128)S(1)} %copy-done.6, f32[640,1536]{1,0:T(8,128)} %copy-done.1, f32[]{:T(128)} %bitcast.6, f32[640,1536]{1,0:T(8,128)} %copy-done, f32[]{:T(128)} %bitcast.19, f32[]{:T(128)} %bitcast.18), kind=kLoop, calls=%fused_computation.5 | loop fusion | flops 4913664 | bytes 10819596 | tf_op jit(solution)/shard_map/reduce_sum | solution.py:883
  307.5 1.4 pad_maximum_fusion
  312.8 3.1 convolution_convert_fusion.share
  315.9 6.9 %collective-permute-done.24.got_b = bf16[320,768]{1,0:T(8,128)(2,1)} collective-permute-done((bf16[320,768]{1,0:T(8,128)(2,1)}, bf16[320,768]{1,0:T(8,128)(2,1)}, u32[]{:S(2)}, u32[]{:S(2)}) %collective-permute-start.24) | collective-permute-done | bytes 491552 | tf_op jit(solution)/shard_map/ppermute | solution.py:575
  322.9 7.9 %input_back.1 = (f32[640,1536]{1,0:T(8,128)}, f32[8,768]{1,0:T(8,128)}) custom-call(bf16[640,768]{1,0:T(8,128)(2,1)} %convolution_convert_fusion.share, bf16[640,768]{1,0:T(8,128)(2,1)} %collective-permute-done.26.came, bf16[320,768]{1,0:T(8,128)(2,1)} %collective-permute-done.25.got_a, bf16[320,768]{1,0:T(8,128)(2,1)} %collective-permute-done.24.got_b, ...), custom_call_target="tpu_custom_call" | custom-call | flops 29491200 | bytes 14745600 | tf_op jit(solution)/shard_map/input_back/pallas_call | solution.py:550
  330.8 14.5 %end.1 = f32[8,768]{1,0:T(8,128)} custom-call(f32[8,768]{1,0:T(8,128)} %get-tuple-element.153.mine), custom_call_target="tpu_custom_call" | custom-call | bytes 30000000 | tf_op jit(solution)/shard_map/end/pallas_call | solution.py:796
  (189 shorter events, 39.2 us)
Async XLA Ops:
  7.2 110.6 %all-gather.2.cloned.1.call-start = ((), (), s32[]{:S(2)}) async-start(), calls=%async_computation.2 | async-start | bytes 3981312 | tf_op jit(solution)/shard_map/all_gather | solution.py:835
  46.2 251.8 %reduce-scatter.2.cloned.1.call-start = ((), (), s32[]{:S(2)}) async-start(), calls=%async_computation.3 | async-start | bytes 3981312 | tf_op jit(solution)/shard_map/reduce_scatter | solution.py:863
  46.3 47.9 %collective-permute-start.1 = (bf16[768,192]{1,0:T(8,128)(2,1)}, bf16[768,192]{1,0:T(8,128)(2,1)S(1)}, u32[]{:S(2)}, u32[]{:S(2)}) collective-permute-start(bf16[768,192]{1,0:T(8,128)(2,1)} %bitcast.72), channel_id=1, source_target_pairs={{0,2},{1,3},{2,0},{3,1},{4,6},{5,7},{6,4},{7,5},{8,10},{9,11},{10,... | collective-permute-start | bytes 884744 | tf_op jit(solution)/shard_map/ppermute | solution.py:575
  46.8 47.3 %collective-permute-start.2 = (bf16[768,192]{1,0:T(8,128)(2,1)}, bf16[768,192]{1,0:T(8,128)(2,1)S(1)}, u32[]{:S(2)}, u32[]{:S(2)}) collective-permute-start(bf16[768,192]{1,0:T(8,128)(2,1)} %bitcast.73), channel_id=1, source_target_pairs={{0,3},{1,2},{2,1},{3,0},{4,7},{5,6},{6,5},{7,4},{8,11},{9,10},{10,... | collective-permute-start | bytes 884744 | tf_op jit(solution)/shard_map/ppermute | solution.py:575
  48.1 59.5 %collective-permute-start.4 = (bf16[768,192]{1,0:T(8,128)(2,1)}, bf16[768,192]{1,0:T(8,128)(2,1)S(1)}, u32[]{:S(2)}, u32[]{:S(2)}) collective-permute-start(bf16[768,192]{1,0:T(8,128)(2,1)} %bitcast.74), channel_id=1, source_target_pairs={{0,1},{1,0},{2,3},{3,2},{4,5},{5,4},{6,7},{7,6},{8,9},{9,8},{10,11... | collective-permute-start | bytes 884744 | tf_op jit(solution)/shard_map/ppermute | solution.py:575
  50.5 4.7 %copy-start.1 = (f32[640,1536]{1,0:T(8,128)}, f32[640,1536]{1,0:T(8,128)S(1)}, u32[]{:S(2)}) copy-start(f32[640,1536]{1,0:T(8,128)S(1)} %convert_element_type.114) | copy-start | bytes 11796484
  51.2 4.4 %copy-start.28 = (bf16[640,768]{1,0:T(8,128)(2,1)S(1)}, bf16[640,768]{1,0:T(8,128)(2,1)}, u32[]{:S(2)}) copy-start(bf16[640,768]{1,0:T(8,128)(2,1)} %get-tuple-element.131) | copy-start | bytes 2949124
  51.2 4.4 %copy-start.41 = (bf16[8,96,576]{2,1,0:T(8,128)(2,1)S(1)}, bf16[8,96,576]{2,1,0:T(8,128)(2,1)}, u32[]{:S(2)}) copy-start(bf16[8,96,576]{2,1,0:T(8,128)(2,1)} %get-tuple-element.84) | copy-start | bytes 2654212
  55.2 38.9 %collective-permute-start = (bf16[640,768]{1,0:T(8,128)(2,1)}, bf16[640,768]{1,0:T(8,128)(2,1)}, u32[]{:S(2)}, u32[]{:S(2)}) collective-permute-start(bf16[640,768]{1,0:T(8,128)(2,1)} %get-tuple-element.89.g_ref.refs_4_), channel_id=1, source_target_pairs={{0,2},{1,3},{2,0},{3,1},{4,6},{5,7},{6,4},{7,5},{8,10},{9,11},{10,... | collective-permute-start | bytes 2949128 | tf_op jit(solution)/shard_map/ppermute | solution.py:575
  55.7 72.7 %collective-permute-start.9 = (bf16[640,768]{1,0:T(8,128)(2,1)}, bf16[640,768]{1,0:T(8,128)(2,1)}, u32[]{:S(2)}, u32[]{:S(2)}) collective-permute-start(bf16[640,768]{1,0:T(8,128)(2,1)} %get-tuple-element.89.g_ref.refs_4_), channel_id=1, source_target_pairs={{0,1},{1,0},{2,3},{3,2},{4,5},{5,4},{6,7},{7,6},{8,9},{9,8},{10,11... | collective-permute-start | bytes 2949128 | tf_op jit(solution)/shard_map/ppermute | solution.py:575
  94.1 13.0 %copy-start.15 = (bf16[768,192]{1,0:T(8,128)(2,1)}, bf16[768,192]{1,0:T(8,128)(2,1)S(1)}, u32[]{:S(2)}) copy-start(bf16[768,192]{1,0:T(8,128)(2,1)S(1)} %collective-permute-done.1.refs_2_) | copy-start | bytes 884740
  94.1 19.1 %copy-start.13 = (bf16[768,192]{1,0:T(8,128)(2,1)}, bf16[768,192]{1,0:T(8,128)(2,1)S(1)}, u32[]{:S(2)}) copy-start(bf16[768,192]{1,0:T(8,128)(2,1)S(1)} %collective-permute-done.2.refs_3_) | copy-start | bytes 884740
  96.6 10.6 %collective-permute-start.5 = (bf16[640,192]{1,0:T(8,128)(2,1)S(1)}, bf16[640,192]{1,0:T(8,128)(2,1)S(1)}, u32[]{:S(2)}, u32[]{:S(2)}) collective-permute-start(bf16[640,192]{1,0:T(8,128)(2,1)S(1)} %get-tuple-element.197), channel_id=1, source_target_pairs={{0,2},{1,3},{2,0},{3,1},{4,6},{5,7},{6,4},{7,5},{8,10},{9,11},{10,... | collective-permute-start | bytes 737288 | tf_op jit(solution)/shard_map/ppermute | solution.py:575
  99.6 8.0 %collective-permute-start.3 = (bf16[640,192]{1,0:T(8,128)(2,1)S(1)}, bf16[640,192]{1,0:T(8,128)(2,1)S(1)}, u32[]{:S(2)}, u32[]{:S(2)}) collective-permute-start(bf16[640,192]{1,0:T(8,128)(2,1)S(1)} %get-tuple-element.198), channel_id=1, source_target_pairs={{0,1},{1,0},{2,3},{3,2},{4,5},{5,4},{6,7},{7,6},{8,9},{9,8},{10,11... | collective-permute-start | bytes 737288 | tf_op jit(solution)/shard_map/ppermute | solution.py:575
  99.9 13.3 %collective-permute-start.6 = (bf16[640,192]{1,0:T(8,128)(2,1)S(1)}, bf16[640,192]{1,0:T(8,128)(2,1)S(1)}, u32[]{:S(2)}, u32[]{:S(2)}) collective-permute-start(bf16[640,192]{1,0:T(8,128)(2,1)S(1)} %get-tuple-element.196), channel_id=1, source_target_pairs={{0,3},{1,2},{2,1},{3,0},{4,7},{5,6},{6,5},{7,4},{8,11},{9,10},{10,... | collective-permute-start | bytes 737288 | tf_op jit(solution)/shard_map/ppermute | solution.py:575
  107.6 6.5 %copy-start.16 = (bf16[768,192]{1,0:T(8,128)(2,1)}, bf16[768,192]{1,0:T(8,128)(2,1)S(1)}, u32[]{:S(2)}) copy-start(bf16[768,192]{1,0:T(8,128)(2,1)S(1)} %collective-permute-done.4.refs_1_) | copy-start | bytes 884740
  108.5 7.1 %copy-start.37 = (f32[768]{0:T(1024)S(1)}, f32[768]{0:T(1024)}, u32[]{:S(2)}) copy-start(f32[768]{0:T(1024)} %param.18) | copy-start | bytes 9220
  115.8 12.6 %collective-permute-start.8 = (bf16[640,768]{1,0:T(8,128)(2,1)S(1)}, bf16[640,768]{1,0:T(8,128)(2,1)}, u32[]{:S(2)}, u32[]{:S(2)}) collective-permute-start(bf16[640,768]{1,0:T(8,128)(2,1)S(1)} %multiply_convert_fusion.x_ref.refs_0_), channel_id=1, source_target_pairs={{0,1},{1,0},{2,3},{3,2},{4,5},{5,4},{6,7},{7,6},{8,9},{9,8},{10,11... | collective-permute-start | bytes 2949128 | tf_op jit(solution)/shard_map/ppermute | solution.py:575
  116.2 24.0 %collective-permute-start.7 = (bf16[640,768]{1,0:T(8,128)(2,1)S(1)}, bf16[640,768]{1,0:T(8,128)(2,1)}, u32[]{:S(2)}, u32[]{:S(2)}) collective-permute-start(bf16[640,768]{1,0:T(8,128)(2,1)S(1)} %multiply_convert_fusion.x_ref.refs_0_), channel_id=1, source_target_pairs={{0,2},{1,3},{2,0},{3,1},{4,6},{5,7},{6,4},{7,5},{8,10},{9,11},{10,... | collective-permute-start | bytes 2949128 | tf_op jit(solution)/shard_map/ppermute | solution.py:575
  117.7 22.4 %collective-permute-start.11 = (bf16[640,768]{1,0:T(8,128)(2,1)}, bf16[640,768]{1,0:T(8,128)(2,1)}, u32[]{:S(2)}, u32[]{:S(2)}) collective-permute-start(bf16[640,768]{1,0:T(8,128)(2,1)} %collective-permute-done.g_ref.refs_6_), channel_id=1, source_target_pairs={{0,1},{1,0},{2,3},{3,2},{4,5},{5,4},{6,7},{7,6},{8,9},{9,8},{10,11... | collective-permute-start | bytes 2949128 | tf_op jit(solution)/shard_map/ppermute | solution.py:575
  140.1 2.8 collective-permute-start.10
  154.8 11.3 %collective-permute-start.14 = (bf16[640,768]{1,0:T(8,128)(2,1)}, bf16[640,768]{1,0:T(8,128)(2,1)}, u32[]{:S(2)}, u32[]{:S(2)}) collective-permute-start(bf16[640,768]{1,0:T(8,128)(2,1)} %get-tuple-element.100), channel_id=1, source_target_pairs={{0,1},{1,0},{2,3},{3,2},{4,5},{5,4},{6,7},{7,6},{8,9},{9,8},{10,11... | collective-permute-start | bytes 2949128 | tf_op jit(solution)/shard_map/ppermute | solution.py:575
  155.0 39.8 %collective-permute-start.16 = (bf16[640,768]{1,0:T(8,128)(2,1)}, bf16[640,768]{1,0:T(8,128)(2,1)S(1)}, u32[]{:S(2)}, u32[]{:S(2)}) collective-permute-start(bf16[640,768]{1,0:T(8,128)(2,1)} %get-tuple-element.101), channel_id=1, source_target_pairs={{0,1},{1,0},{2,3},{3,2},{4,5},{5,4},{6,7},{7,6},{8,9},{9,8},{10,11... | collective-permute-start | bytes 2949128 | tf_op jit(solution)/shard_map/ppermute | solution.py:575
  168.8 26.1 %collective-permute-start.15 = (bf16[640,768]{1,0:T(8,128)(2,1)}, bf16[640,768]{1,0:T(8,128)(2,1)}, u32[]{:S(2)}, u32[]{:S(2)}) collective-permute-start(bf16[640,768]{1,0:T(8,128)(2,1)} %add_convert_fusion.3), channel_id=1, source_target_pairs={{0,2},{1,3},{2,0},{3,1},{4,6},{5,7},{6,4},{7,5},{8,10},{9,11},{10,... | collective-permute-start | bytes 2949128 | tf_op jit(solution)/shard_map/ppermute | solution.py:575
  170.3 35.5 %collective-permute-start.12 = (f32[640,768]{1,0:T(8,128)}, f32[640,768]{1,0:T(8,128)}, u32[]{:S(2)}, u32[]{:S(2)}) collective-permute-start(f32[640,768]{1,0:T(8,128)} %get-tuple-element.97), channel_id=1, source_target_pairs={{0,1},{1,0},{2,3},{3,2},{4,5},{5,4},{6,7},{7,6},{8,9},{9,8},{10,11... | collective-permute-start | bytes 5898248 | tf_op jit(solution)/shard_map/ppermute | solution.py:575
  203.6 10.9 %collective-permute-start.18 = (bf16[640,192]{1,0:T(8,128)(2,1)}, bf16[640,192]{1,0:T(8,128)(2,1)S(1)}, u32[]{:S(2)}, u32[]{:S(2)}) collective-permute-start(bf16[640,192]{1,0:T(8,128)(2,1)} %get-tuple-element.117), channel_id=1, source_target_pairs={{0,2},{1,3},{2,0},{3,1},{4,6},{5,7},{6,4},{7,5},{8,10},{9,11},{10,... | collective-permute-start | bytes 737288 | tf_op jit(solution)/shard_map/ppermute | solution.py:575
  204.1 16.4 %collective-permute-start.19 = (bf16[640,192]{1,0:T(8,128)(2,1)}, bf16[640,192]{1,0:T(8,128)(2,1)S(1)}, u32[]{:S(2)}, u32[]{:S(2)}) collective-permute-start(bf16[640,192]{1,0:T(8,128)(2,1)} %get-tuple-element.118), channel_id=1, source_target_pairs={{0,3},{1,2},{2,1},{3,0},{4,7},{5,6},{6,5},{7,4},{8,11},{9,10},{10,... | collective-permute-start | bytes 737288 | tf_op jit(solution)/shard_map/ppermute | solution.py:575
  205.5 21.0 %collective-permute-start.17 = (bf16[640,192]{1,0:T(8,128)(2,1)}, bf16[640,192]{1,0:T(8,128)(2,1)S(1)}, u32[]{:S(2)}, u32[]{:S(2)}) collective-permute-start(bf16[640,192]{1,0:T(8,128)(2,1)} %get-tuple-element.116), channel_id=1, source_target_pairs={{0,1},{1,0},{2,3},{3,2},{4,5},{5,4},{6,7},{7,6},{8,9},{9,8},{10,11... | collective-permute-start | bytes 737288 | tf_op jit(solution)/shard_map/ppermute | solution.py:575
  205.8 14.7 %copy-start.3 = (bf16[640,768]{1,0:T(8,128)(2,1)S(1)}, bf16[640,768]{1,0:T(8,128)(2,1)}, u32[]{:S(2)}) copy-start(bf16[640,768]{1,0:T(8,128)(2,1)} %get-tuple-element.122) | copy-start | bytes 2949124
  205.8 14.7 %copy-start.23 = (bf16[640,192]{1,0:T(8,128)(2,1)S(1)}, bf16[640,192]{1,0:T(8,128)(2,1)}, u32[]{:S(2)}) copy-start(bf16[640,192]{1,0:T(8,128)(2,1)} %copy-done.22) | copy-start | bytes 737284
  205.8 17.1 %copy-start.21 = (bf16[640,192]{1,0:T(8,128)(2,1)S(1)}, bf16[640,192]{1,0:T(8,128)(2,1)}, u32[]{:S(2)}) copy-start(bf16[640,192]{1,0:T(8,128)(2,1)} %copy-done.20) | copy-start | bytes 737284
  209.2 15.3 %copy-start.18 = (bf16[640,192]{1,0:T(8,128)(2,1)S(1)}, bf16[640,192]{1,0:T(8,128)(2,1)}, u32[]{:S(2)}) copy-start(bf16[640,192]{1,0:T(8,128)(2,1)} %copy-done.17) | copy-start | bytes 737284
  209.2 52.5 %collective-permute-start.13 = (bf16[640,768]{1,0:T(8,128)(2,1)}, bf16[640,768]{1,0:T(8,128)(2,1)}, u32[]{:S(2)}, u32[]{:S(2)}) collective-permute-start(bf16[640,768]{1,0:T(8,128)(2,1)} %add_convert_fusion.4), channel_id=1, source_target_pairs={{0,2},{1,3},{2,0},{3,1},{4,6},{5,7},{6,4},{7,5},{8,10},{9,11},{10,... | collective-permute-start | bytes 2949128 | tf_op jit(solution)/shard_map/ppermute | solution.py:575
  214.4 11.2 %copy-start.44 = (bf16[640,192]{1,0:T(8,128)(2,1)}, bf16[640,192]{1,0:T(8,128)(2,1)S(1)}, u32[]{:S(2)}) copy-start(bf16[640,192]{1,0:T(8,128)(2,1)S(1)} %collective-permute-done.18.refs_6_) | copy-start | bytes 737284
  220.5 5.1 %copy-start.45 = (bf16[640,192]{1,0:T(8,128)(2,1)}, bf16[640,192]{1,0:T(8,128)(2,1)S(1)}, u32[]{:S(2)}) copy-start(bf16[640,192]{1,0:T(8,128)(2,1)S(1)} %collective-permute-done.19.refs_7_) | copy-start | bytes 737284
  221.7 37.6 %collective-permute-start.20 = (bf16[768,192]{0,1:T(8,128)(2,1)}, bf16[768,192]{0,1:T(8,128)(2,1)}, u32[]{:S(2)}, u32[]{:S(2)}) collective-permute-start(bf16[768,192]{0,1:T(8,128)(2,1)} %convolution_convert_fusion.10), channel_id=1, source_target_pairs={{0,1},{1,0},{2,3},{3,2},{4,5},{5,4},{6,7},{7,6},{8,9},{9,8},{10,11... | collective-permute-start | bytes 884744 | tf_op jit(solution)/shard_map/ppermute | solution.py:575
  224.0 35.3 %collective-permute-start.21 = (bf16[768,192]{0,1:T(8,128)(2,1)}, bf16[768,192]{0,1:T(8,128)(2,1)}, u32[]{:S(2)}, u32[]{:S(2)}) collective-permute-start(bf16[768,192]{0,1:T(8,128)(2,1)} %convolution_convert_fusion.9), channel_id=1, source_target_pairs={{0,2},{1,3},{2,0},{3,1},{4,6},{5,7},{6,4},{7,5},{8,10},{9,11},{10,... | collective-permute-start | bytes 884744 | tf_op jit(solution)/shard_map/ppermute | solution.py:575
  225.6 33.6 %collective-permute-start.22 = (bf16[768,192]{0,1:T(8,128)(2,1)}, bf16[768,192]{0,1:T(8,128)(2,1)}, u32[]{:S(2)}, u32[]{:S(2)}) collective-permute-start(bf16[768,192]{0,1:T(8,128)(2,1)} %convolution_convert_fusion.8), channel_id=1, source_target_pairs={{0,3},{1,2},{2,1},{3,0},{4,7},{5,6},{6,5},{7,4},{8,11},{9,10},{10,... | collective-permute-start | bytes 884744 | tf_op jit(solution)/shard_map/ppermute | solution.py:575
  227.3 32.0 %copy-start.19 = (bf16[640,192]{1,0:T(8,128)(2,1)S(1)}, bf16[640,192]{1,0:T(8,128)(2,1)}, u32[]{:S(2)}) copy-start(bf16[640,192]{1,0:T(8,128)(2,1)} %get-tuple-element.123) | copy-start | bytes 737284
  264.0 3.0 collective-permute-start.23
  264.9 27.3 %collective-permute-start.27 = (f32[640,768]{1,0:T(8,128)}, f32[640,768]{1,0:T(8,128)}, u32[]{:S(2)}, u32[]{:S(2)}) collective-permute-start(f32[640,768]{1,0:T(8,128)} %get-tuple-element.143), channel_id=1, source_target_pairs={{0,1},{1,0},{2,3},{3,2},{4,5},{5,4},{6,7},{7,6},{8,9},{9,8},{10,11... | collective-permute-start | bytes 5898248 | tf_op jit(solution)/shard_map/ppermute | solution.py:575
  265.2 4.3 %copy-start.10 = (bf16[640,576]{1,0:T(8,128)(2,1)}, bf16[640,576]{1,0:T(8,128)(2,1)S(1)}, u32[]{:S(2)}) copy-start(bf16[640,576]{1,0:T(8,128)(2,1)S(1)} %get-tuple-element.140) | copy-start | bytes 2211844
  265.2 5.3 %copy-start.8 = (bf16[640,576]{1,0:T(8,128)(2,1)}, bf16[640,576]{1,0:T(8,128)(2,1)S(1)}, u32[]{:S(2)}) copy-start(bf16[640,576]{1,0:T(8,128)(2,1)S(1)} %get-tuple-element.146) | copy-start | bytes 2211844
  269.1 13.8 %collective-permute-start.25 = (bf16[320,768]{1,0:T(8,128)(2,1)}, bf16[320,768]{1,0:T(8,128)(2,1)}, u32[]{:S(2)}, u32[]{:S(2)}) collective-permute-start(bf16[320,768]{1,0:T(8,128)(2,1)} %get-tuple-element.199), channel_id=1, source_target_pairs={{0,2},{1,3},{2,0},{3,1},{4,6},{5,7},{6,4},{7,5},{8,10},{9,11},{10,... | collective-permute-start | bytes 1474568 | tf_op jit(solution)/shard_map/ppermute | solution.py:575
  282.9 62.4 %all-to-all-start = ((bf16[8,96,768]{2,1,0:T(8,128)(2,1)}), bf16[8,96,768]{2,1,0:T(8,128)(2,1)S(1)}, u32[]{:S(2)}, u32[]{:S(2)}) async-start(bf16[8,96,768]{2,1,0:T(8,128)(2,1)} %pad_maximum_fusion.1), calls=%async_computation.1 | async-start | bytes 2359296 | tf_op jit(solution)/shard_map/all_to_all | solution.py:897
  301.5 21.3 %collective-permute-start.26 = (bf16[640,768]{1,0:T(8,128)(2,1)}, bf16[640,768]{1,0:T(8,128)(2,1)}, u32[]{:S(2)}, u32[]{:S(2)}) collective-permute-start(bf16[640,768]{1,0:T(8,128)(2,1)} %convolution_convert_fusion.1), channel_id=1, source_target_pairs={{0,1},{1,0},{2,3},{3,2},{4,5},{5,4},{6,7},{7,6},{8,9},{9,8},{10,11... | collective-permute-start | bytes 2949128 | tf_op jit(solution)/shard_map/ppermute | solution.py:575
  301.5 5.9 %copy-start.7 = (bf16[640,768]{1,0:T(8,128)(2,1)S(1)}, bf16[640,768]{1,0:T(8,128)(2,1)}, u32[]{:S(2)}) copy-start(bf16[640,768]{1,0:T(8,128)(2,1)} %get-tuple-element.182) | copy-start | bytes 2949124
  308.9 13.9 %collective-permute-start.24 = (bf16[320,768]{1,0:T(8,128)(2,1)}, bf16[320,768]{1,0:T(8,128)(2,1)}, u32[]{:S(2)}, u32[]{:S(2)}) collective-permute-start(bf16[320,768]{1,0:T(8,128)(2,1)} %get-tuple-element.200), channel_id=1, source_target_pairs={{0,2},{1,3},{2,0},{3,1},{4,6},{5,7},{6,4},{7,5},{8,10},{9,11},{10,... | collective-permute-start | bytes 1474568 | tf_op jit(solution)/shard_map/ppermute | solution.py:575
  (30 other events, 64.9 us)
Sparse Core Ops, SparseCore 0:
  46.3 63.8 all-gather.1
  195.0 81.4 reduce-scatter.1
